TPU v7x, 32 devices: a whole 2x2x4 slice. The times are simulated.
32 devices in a mesh: rows: 4 (over y, core), heads: 8 (over z, x).
Axes of the slice: x: 2, y: 2, z: 4, core: 2. Of those that a mesh axis runs over, the one named last changes fastest.
Arguments:
- stream: float32 [4, 512, 2048], P('rows'), may hold values from -6 to 6
- doc_starts: int32 [4, 512], P('rows'), may hold values from 0 to 1, as said below
- valid_mask: int32 [4, 512], P('rows'), may hold values from 0 to 1, as said below
- first_gain: float32 [2048], P('heads'), may hold values from 0.5 to 1.5
- w_query: float32 [2048, 2048], P(None, 'heads'), may hold values from -0.125 to 0.125
- w_key: float32 [2048, 2048], P(None, 'heads'), may hold values from -0.125 to 0.125
- w_value: float32 [2048, 2048], P(None, 'heads'), may hold values from -0.125 to 0.125
- w_rate: float32 [2048, 32], P(None, 'heads'), may hold values from -0.125 to 0.125
- b_rate: float32 [32], P('heads'), may hold values from -3 to 3
- inner_weight: float32 [32, 64, 64], P('heads'), may hold values from -0.75 to 0.75
- inner_bias: float32 [32, 64], P('heads'), may hold values from -4 to 4
- inner_gain: float32 [32, 64], P('heads'), may hold values from 0.5 to 1.5
- inner_shift: float32 [32, 64], P('heads'), may hold values from -3 to 3
- post_gain: float32 [2048], P('heads'), may hold values from 0.5 to 1.5
- post_shift: float32 [2048], P('heads'), may hold values from -3 to 3
- w_gate_attn: float32 [2048, 2048], P(None, 'heads'), may hold values from -0.125 to 0.125
- w_out: float32 [2048, 2048], P(None, 'heads'), may hold values from -0.125 to 0.125
- second_gain: float32 [2048], P('heads'), may hold values from 0.5 to 1.5
- w_gate: float32 [2048, 5504], P(None, 'heads'), may hold values from -0.125 to 0.125
- w_up: float32 [2048, 5504], P(None, 'heads'), may hold values from -0.125 to 0.125
- w_down: float32 [5504, 2048], P('heads'), may hold values from -0.078125 to 0.078125
- cotangent: float32 [4, 512, 2048], P('rows', None, 'heads'), may hold values from -6 to 6
Outputs:
- output: float32 [4, 512, 2048], P('rows', None, 'heads')
- grad_stream: float32 [4, 512, 2048], P('rows', None, 'heads')
- grad_first_gain: float32 [2048], P('heads')
- grad_query: float32 [2048, 2048], P(None, 'heads')
- grad_key: float32 [2048, 2048], P(None, 'heads')
- grad_value: float32 [2048, 2048], P(None, 'heads')
- grad_rate: float32 [2048, 32], P(None, 'heads')
- grad_rate_bias: float32 [32], P('heads')
- grad_inner_weight: float32 [32, 64, 64], P('heads')
- grad_inner_bias: float32 [32, 64], P('heads')
- grad_inner_gain: float32 [32, 64], P('heads')
- grad_inner_shift: float32 [32, 64], P('heads')
- grad_post_gain: float32 [2048], P('heads')
- grad_post_shift: float32 [2048], P('heads')
- grad_gate_attn: float32 [2048, 2048], P(None, 'heads')
- grad_out: float32 [2048, 2048], P(None, 'heads')
- grad_second_gain: float32 [2048], P('heads')
- grad_gate: float32 [2048, 5504], P(None, 'heads')
- grad_up: float32 [2048, 5504], P(None, 'heads')
- grad_down: float32 [5504, 2048], P('heads')
- rms_values: float32 [5], replicated
Inputs may be any that keep to these rules, and one draw needn't show every extreme that they name: `doc_starts`: every row's first token is 1, and 1 stands only at positions that are multiples of 16. `valid_mask`: in each row the valid tokens are a leading run of 256 tokens or more.
All inputs are finite; a program needn't handle non-finite values.
Results may differ from a plain program's by a relative error of at most 0.0003.
Values sent between devices are 32-bit elements; how exact they have to be, the bound alone decides.
No kernel may reach another device: no remote copies, remote signals or barrier semaphores. Data moves between devices by JAX's collectives and lax.ppermute only.
A program may use at most 192 MiB of HBM per device.

v0:
```python
import math

import jax
import jax.numpy as jnp
from jax import lax
from jax.sharding import PartitionSpec as P

MB = 16


precise = lax.Precision.HIGHEST
epsilon = 1e-06


def product(left, right):
    return jnp.dot(left, right, precision=precise, preferred_element_type=jnp.float32)


def left_product(left, right):
    return lax.dot_general(
        left, right, (((0,), (0,)), ((), ())), precision=precise, preferred_element_type=jnp.float32
    )


def right_product(left, right):
    return lax.dot_general(
        left, right, (((1,), (1,)), ((), ())), precision=precise, preferred_element_type=jnp.float32
    )


def rms_norm(array, gain):
    return array * lax.rsqrt(jnp.mean(array * array, -1, keepdims=True) + epsilon) * gain


def layer_norm(array, gain, shift):
    center = array - jnp.mean(array, -1, keepdims=True)
    return center * lax.rsqrt(jnp.mean(center * center, -1, keepdims=True) + epsilon) * gain + shift


def activate(array):
    return jax.nn.gelu(array, approximate=True)


def inner_step(
    state,
    query_rows,
    key_rows,
    value_rows,
    rate_rows,
    reset_flags,
    w_init,
    b_init,
    norm_gain,
    norm_shift,
):
    weight, offset = state
    keep = (reset_flags == 0).astype(jnp.float32)
    weight = keep[:, None, None, None] * weight + (1.0 - keep[:, None, None, None]) * w_init
    offset = keep[:, None, None] * offset + (1.0 - keep[:, None, None]) * b_init
    block_len = query_rows.shape[1]
    recon = jnp.einsum("rihd,rhde->rihe", key_rows, weight, precision=precise) + offset[:, None]
    center = recon - jnp.mean(recon, -1, keepdims=True)
    inv_std = lax.rsqrt(jnp.mean(center * center, -1, keepdims=True) + epsilon)
    unit_rows = center * inv_std
    error = (unit_rows * norm_gain + norm_shift - (value_rows - key_rows)) * norm_gain
    inner_grad = inv_std * (
        error
        - jnp.mean(error, -1, keepdims=True)
        - unit_rows * jnp.mean(error * unit_rows, -1, keepdims=True)
    )
    position = jnp.arange(1, block_len + 1, dtype=jnp.float32)
    causal = (jnp.arange(block_len)[:, None] >= jnp.arange(block_len)[None, :]).astype(jnp.float32)
    step_size = causal * jnp.moveaxis(rate_rows, 1, 2)[:, :, None, :] / position[:, None]
    scores = jnp.einsum("rihd,rjhd->rhij", query_rows, key_rows, precision=precise)
    shifted = offset[:, None] - jnp.einsum(
        "rhij,rjhd->rihd", step_size, inner_grad, precision=precise
    )
    inner_out = (
        jnp.einsum("rihd,rhde->rihe", query_rows, weight, precision=precise)
        - jnp.einsum("rhij,rjhd->rihd", step_size * scores, inner_grad, precision=precise)
        + shifted
    )
    last_rate = rate_rows / block_len
    weight = weight - jnp.einsum(
        "rjh,rjhd,rjhe->rhde", last_rate, key_rows, inner_grad, precision=precise
    )
    offset = offset - jnp.einsum("rjh,rjhe->rhe", last_rate, inner_grad, precision=precise)
    return ((weight, offset), query_rows + layer_norm(inner_out, norm_gain, norm_shift))


def ttt_layer(queries, keys, values, rate, starts, w_init, b_init, norm_gain, norm_shift):
    rows, length, heads, dim = queries.shape
    count = length // MB
    per = math.gcd(count, 8)
    turns = count // per

    def split(array):
        array = array.reshape((rows, turns, per, MB) + array.shape[2:])
        return jnp.moveaxis(array, 0, 2)

    resets = jnp.moveaxis(starts[:, ::MB].reshape(rows, turns, per), 0, 2)

    def turn(state, block):
        block_q, block_k, block_v, block_rate, block_reset = block
        results = []
        for index in range(per):
            state, result = inner_step(
                state,
                block_q[index],
                block_k[index],
                block_v[index],
                block_rate[index],
                block_reset[index],
                w_init,
                b_init,
                norm_gain,
                norm_shift,
            )
            results.append(result)
        return (state, jnp.stack(results))

    initial = (
        jnp.zeros((rows, heads, dim, dim), jnp.float32),
        jnp.zeros((rows, heads, dim), jnp.float32),
    )
    final, results = lax.scan(
        jax.checkpoint(turn),
        initial,
        (split(queries), split(keys), split(values), split(rate), resets),
    )
    return jnp.moveaxis(results, 2, 0).reshape(rows, length, heads, dim)


def on_device(
    stream,
    doc_starts,
    valid_mask,
    first_gain,
    w_query,
    w_key,
    w_value,
    w_rate,
    b_rate,
    inner_weight,
    inner_bias,
    inner_gain,
    inner_shift,
    post_gain,
    post_shift,
    w_gate_attn,
    w_out,
    second_gain,
    w_gate,
    w_up,
    w_down,
    cotangent,
):
    rows, length, width = stream.shape
    tokens = stream.reshape(rows * length, width)
    slab = second_gain.shape[0]
    column = lax.axis_index("heads") * slab
    heads_here, head_dim = inner_bias.shape
    span = heads_here * head_dim
    total_span = span * lax.axis_size("heads")
    gain_one, gain_two = (
        lax.all_gather(first_gain, "heads", axis=0, tiled=True),
        lax.all_gather(second_gain, "heads", axis=0, tiled=True),
    )

    def mixer(
        tokens_in,
        gain_in,
        query_w,
        key_w,
        value_w,
        gate_w,
        rate_w,
        rate_b,
        init_w,
        init_b,
        norm_gain,
        norm_shift,
    ):
        normed = rms_norm(tokens_in, gain_in)
        joined = product(normed, jnp.concatenate([query_w, key_w, value_w, gate_w], axis=1))
        head_shape = (rows, length, heads_here, head_dim)
        queries = joined[:, :span].reshape(head_shape)
        keys = joined[:, span : 2 * span].reshape(head_shape)
        values = joined[:, 2 * span : 3 * span].reshape(head_shape)
        rate = (jax.nn.sigmoid(product(normed, rate_w) + rate_b) / head_dim).reshape(
            rows, length, heads_here
        )
        mixed_heads = ttt_layer(
            queries, keys, values, rate, doc_starts, init_w, init_b, norm_gain, norm_shift
        )
        return (mixed_heads.reshape(rows * length, span), joined[:, 3 * span :])

    (mixed, gate_pre), mixer_back = jax.vjp(
        mixer,
        tokens,
        gain_one,
        w_query,
        w_key,
        w_value,
        w_gate_attn,
        w_rate,
        b_rate,
        inner_weight,
        inner_bias,
        inner_gain,
        inner_shift,
    )
    row_sums = lax.psum((jnp.sum(mixed, 1), jnp.sum(mixed * mixed, 1)), "heads")
    row_mean = row_sums[0] / total_span
    inv_std = lax.rsqrt(row_sums[1] / total_span - row_mean * row_mean + epsilon)[:, None]
    centered = (mixed - row_mean[:, None]) * inv_std
    shaped = centered * post_gain + post_shift
    gate_act, gate_back = jax.vjp(activate, gate_pre)
    gated = gate_act * shaped
    gathered = lax.all_gather(gated, "heads", axis=1, tiled=True)
    attn = product(gathered, w_out)
    hidden_in = lax.dynamic_slice_in_dim(tokens, column, slab, 1) + attn
    whole = lax.all_gather(hidden_in, "heads", axis=1, tiled=True)

    def feed(whole_in, gain_in, gate_w, up_w, down_w):
        hnorm = rms_norm(whole_in, gain_in)
        return product(jax.nn.silu(product(hnorm, gate_w)) * product(hnorm, up_w), down_w)

    partial_out, feed_back = jax.vjp(feed, whole, gain_two, w_gate, w_up, w_down)
    ffn = lax.psum_scatter(partial_out, "heads", scatter_dimension=1, tiled=True)
    output = hidden_in + ffn
    grad_output = cotangent.reshape(rows * length, slab)
    grad_whole_out = lax.all_gather(grad_output, "heads", axis=1, tiled=True)
    d_whole, d_gain_two, d_gate, d_up, d_down = feed_back(grad_whole_out)
    d_hidden_part, d_gain_two_sum = (
        lax.psum_scatter(d_whole, "heads", scatter_dimension=1, tiled=True),
        lax.psum_scatter(d_gain_two[None, :], "heads", scatter_dimension=1, tiled=True),
    )
    d_hidden = grad_output + d_hidden_part
    d_w_out = left_product(gathered, d_hidden)
    d_gated = lax.psum_scatter(
        right_product(d_hidden, w_out), "heads", scatter_dimension=1, tiled=True
    )
    d_shaped = d_gated * gate_act
    (d_gate_pre,) = gate_back(d_gated * shaped)
    d_post_gain = jnp.sum(d_shaped * centered, 0)
    d_post_shift = jnp.sum(d_shaped, 0)
    d_center = d_shaped * post_gain
    weights = valid_mask.reshape(-1).astype(jnp.float32)[:, None]
    stream_cols = lax.dynamic_slice_in_dim(tokens, column, slab, 1)
    local_stats = jnp.stack(
        [
            jnp.sum(weights * member * member)
            for member in (stream_cols, attn, hidden_in, ffn, output)
        ]
    )
    back_sums = lax.psum(
        (jnp.sum(d_center, 1), jnp.sum(d_center * centered, 1), local_stats), "heads"
    )
    d_mixed = inv_std * (
        d_center
        - back_sums[0][:, None] / total_span
        - centered * back_sums[1][:, None] / total_span
    )
    (
        d_tokens,
        d_gain_one,
        d_query,
        d_key,
        d_value,
        d_gate_attn,
        d_rate,
        d_rate_bias,
        d_inner_weight,
        d_inner_bias,
        d_inner_gain,
        d_inner_shift,
    ) = mixer_back((d_mixed, d_gate_pre))
    d_input, d_gain_one_sum = (
        lax.psum_scatter(d_tokens, "heads", scatter_dimension=1, tiled=True),
        lax.psum_scatter(d_gain_one[None, :], "heads", scatter_dimension=1, tiled=True),
    )
    d_stream = d_hidden + d_input
    valid_count = jnp.sum(valid_mask).astype(jnp.float32)
    (
        g_first_gain,
        g_query,
        g_key,
        g_value,
        g_rate,
        g_rate_bias,
        g_inner_weight,
        g_inner_bias,
        g_inner_gain,
        g_inner_shift,
        g_post_gain,
        g_post_shift,
        g_gate_attn,
        g_out,
        g_second_gain,
        g_gate,
        g_up,
        g_down,
        stat_total,
        count_total,
    ) = lax.psum(
        (
            d_gain_one_sum[0],
            d_query,
            d_key,
            d_value,
            d_rate,
            d_rate_bias,
            d_inner_weight,
            d_inner_bias,
            d_inner_gain,
            d_inner_shift,
            d_post_gain,
            d_post_shift,
            d_gate_attn,
            d_w_out,
            d_gain_two_sum[0],
            d_gate,
            d_up,
            d_down,
            back_sums[2],
            valid_count,
        ),
        "rows",
    )
    rms_values = jnp.sqrt(stat_total / (count_total * width))
    return (
        output.reshape(rows, length, slab),
        d_stream.reshape(rows, length, slab),
        g_first_gain,
        g_query,
        g_key,
        g_value,
        g_rate,
        g_rate_bias,
        g_inner_weight,
        g_inner_bias,
        g_inner_gain,
        g_inner_shift,
        g_post_gain,
        g_post_shift,
        g_gate_attn,
        g_out,
        g_second_gain,
        g_gate,
        g_up,
        g_down,
        rms_values,
    )


def solution(mesh):
    in_specs = (
        P("rows", None, None),
        P("rows", None),
        P("rows", None),
        P("heads"),
        P(None, "heads"),
        P(None, "heads"),
        P(None, "heads"),
        P(None, "heads"),
        P("heads"),
        P("heads", None, None),
        P("heads", None),
        P("heads", None),
        P("heads", None),
        P("heads"),
        P("heads"),
        P(None, "heads"),
        P(None, "heads"),
        P("heads"),
        P(None, "heads"),
        P(None, "heads"),
        P("heads", None),
        P("rows", None, "heads"),
    )
    out_specs = (
        P("rows", None, "heads"),
        P("rows", None, "heads"),
        P("heads"),
        P(None, "heads"),
        P(None, "heads"),
        P(None, "heads"),
        P(None, "heads"),
        P("heads"),
        P("heads", None, None),
        P("heads", None),
        P("heads", None),
        P("heads", None),
        P("heads"),
        P("heads"),
        P(None, "heads"),
        P(None, "heads"),
        P("heads"),
        P(None, "heads"),
        P(None, "heads"),
        P("heads", None),
        P(),
    )
    return jax.shard_map(
        on_device, mesh=mesh, in_specs=in_specs, out_specs=out_specs, check_vma=False
    )
```

profile of v0, /device:TPU:0, one launch (start us, length us, event | category | flops | bytes accessed | tf_op | source)
XLA Modules:
  0.0 1816.3 jit_solution(16348612572357215892)
XLA Ops:
  13.4 22.3 %all-gather.1 = f32[8,1,256]{2,1,0:T(1,128)S(1)} all-gather(f32[1,1,256]{2,1,0:T(1,128)S(1)} %bitcast.4507), channel_id=1, replica_groups=mesh['rows'=4,'heads'=8] {'heads'}, dimensions={0}, use_global_device_ids=true | all-gather | bytes 9216 | tf_op jit(solution)/shard_map/all_gather | solution.py:166
  46.1 13.9 fusion.1275
  66.7 129.6 %while.55 = (s32[]{:T(128)}, f32[1,4,64,64]{3,2,1,0:T(8,128)S(1)}, f32[1,4,64]{2,1,0:T(4,128)S(1)}, f32[4,8,1,16,4,64]{5,3,4,1,2,0:T(8,128)}, f32[4,1,4,64,64]{4...) while((s32[]{:T(128)}, f32[1,4,64,64]{3,2,1,0:T(8,128)S(1)}, ...), condition=%wide.region_50.51_spmd.clone.clone, body=%wide.region_1.50_spmd.clone.clone.sunk | while | flops 96622112 | bytes 8260089 | solution.py:126
  203.2 17.1 all-reduce.37
  234.3 62.5 %all-gather.7.cloned.1.call-done = f32[512,2048]{1,0:T(8,128)} async-done(((f32[512,256]{1,0:T(8,128)}), f32[512,2048]{1,0:T(8,128)}) %all-gather.7.cloned.1.call-update) | async-done | bytes 4194320 | tf_op jit(solution)/shard_map/all_gather | solution.py:220
  303.5 18.3 %all-gather.2 = f32[8,1,256]{2,1,0:T(1,128)S(1)} all-gather(f32[1,1,256]{2,1,0:T(1,128)S(1)} %bitcast.4508), channel_id=1, replica_groups=mesh['rows'=4,'heads'=8] {'heads'}, dimensions={0}, use_global_device_ids=true | all-gather | bytes 9216 | tf_op jit(solution)/shard_map/all_gather | solution.py:167
  321.8 49.8 %all-gather.11.cloned.1.call-done = f32[1,512,2048]{2,1,0:T(8,128)} async-done(((f32[1,512,256]{2,1,0:T(8,128)}), f32[1,512,2048]{2,1,0:T(8,128)}) %all-gather.11.cloned.1.call-update) | async-done | bytes 4194320 | tf_op jit(solution)/shard_map/all_gather | solution.py:233
  371.7 12.7 fusion.1260
  384.4 62.7 %all-gather.9.cloned.1.call-done = f32[512,2048]{1,0:T(8,128)} async-done(((f32[512,256]{1,0:T(8,128)}), f32[512,2048]{1,0:T(8,128)}) %all-gather.9.cloned.1.call-update) | async-done | bytes 4194320 | tf_op jit(solution)/shard_map/all_gather | solution.py:223
  450.6 12.9 fusion.1268
  484.3 15.4 multiply_reduce_fusion.120
  502.6 14.4 fusion.1316
  517.1 72.4 %reduce-scatter.13.cloned.1.call-done = f32[512,256]{1,0:T(8,128)} async-done(((f32[512,2048]{1,0:T(8,128)}), f32[512,256]{1,0:T(8,128)}) %reduce-scatter.13.cloned.1.call-update) | async-done | bytes 524304 | tf_op jit(solution)/shard_map/reduce_scatter | solution.py:236
  599.6 82.3 %reduce-scatter.11.cloned.1.call-done = f32[512,256]{1,0:T(8,128)} async-done(((f32[512,2048]{1,0:T(8,128)}), f32[512,256]{1,0:T(8,128)}) %reduce-scatter.11.cloned.1.call-update) | async-done | bytes 524304 | tf_op jit(solution)/shard_map/reduce_scatter | solution.py:230
  688.2 86.2 %reduce-scatter.15.cloned.1.call-done = f32[512,256]{1,0:T(8,128)} async-done(((f32[512,2048]{1,0:T(8,128)}), f32[512,256]{1,0:T(8,128)}) %reduce-scatter.15.cloned.1.call-update) | async-done | bytes 524304 | tf_op jit(solution)/shard_map/reduce_scatter | solution.py:241
  777.5 20.8 %all-reduce.36 = (f32[512]{0:T(512)S(1)}, f32[512]{0:T(512)S(1)}, f32[5]{0:T(128)}) all-reduce(f32[512]{0:T(512)S(1)} %get-tuple-element.1288, f32[512]{0:T(512)S(1)} %get-tuple-element.1294, f32[5]{0:T(128)S(1)} %stack.59), channel_id=1, replica_groups=mesh['rows'=4,'heads'=8] {'heads'}, use_global_device_ids=true, to_apply=%region_63.64 | all-reduce | flops 1029 | bytes 8232 | tf_op jit(solution)/shard_map/psum | solution.py:257
  804.4 335.8 %while.54 = (s32[]{:T(128)}, f32[4,64,64]{2,1,0:T(8,128)S(1)}, f32[4,64]{1,0:T(4,128)}, f32[4,64]{1,0:T(4,128)}, f32[4,64]{1,0:T(4,128)}, /*index=5*/f32[1,4,64,...) while((s32[]{:T(128)}, f32[4,64,64]{2,1,0:T(8,128)S(1)}, ...), condition=%wide.region_233.234_spmd.clone, body=%wide.region_64.233_spmd.clone.sunk | while | flops 280920800 | bytes 29616696 | solution.py:126
  1145.8 16.3 fusion.1296
  1177.7 13.4 fusion.1258
  1202.8 12.3 fusion.1266
  1223.3 15.3 fusion.1271
  1249.8 11.9 all-reduce.38
  1262.9 59.7 %reduce-scatter.17.cloned.1.call-done = f32[512,256]{1,0:T(8,128)} async-done(((f32[512,2048]{1,0:T(8,128)}), f32[512,256]{1,0:T(8,128)}) %reduce-scatter.17.cloned.1.call-update) | async-done | bytes 524304 | tf_op jit(solution)/shard_map/reduce_scatter | solution.py:280
  1324.7 463.8 %all-reduce.42.cloned.1.call-done = (f32[2048,256]{1,0:T(8,128)}, f32[2048,256]{1,0:T(8,128)}, f32[2048,256]{1,0:T(8,128)}, f32[4,64,64]{2,1,0:T(8,128)}, f32[20...) async-done(((f32[2048,256]{1,0:T(8,128)}, f32[2048,256]{1,0:T(8,128)}, f32[2048,256]{1,0:T(8,128)}, ...) | async-done | bytes 27459600 | tf_op jit(solution)/shard_map/psum | solution.py:306
  (2496 shorter events, 563.2 us)
Async XLA Ops:
  7.2 289.5 %copy-start = (f32[2048,256]{1,0:T(8,128)S(1)}, f32[2048,256]{1,0:T(8,128)}, u32[]{:S(2)}) copy-start(f32[2048,256]{1,0:T(8,128)} %param.42) | copy-start | bytes 6291460
  7.2 28.4 %copy-start.47 = (f32[2048,4]{0,1:T(4,128)S(1)}, f32[2048,4]{0,1:T(4,128)}, u32[]{:S(2)}) copy-start(f32[2048,4]{0,1:T(4,128)} %param.33) | copy-start | bytes 98308
  7.2 28.4 %copy-start.76 = (f32[4]{0:T(128)S(1)}, f32[4]{0:T(128)}, u32[]{:S(2)}) copy-start(f32[4]{0:T(128)} %param.34) | copy-start | bytes 52
  7.2 289.5 %all-gather.7.cloned.1.call-start = ((), (), s32[]{:S(2)}) async-start(), calls=%async_computation.6 | async-start | bytes 4718592 | tf_op jit(solution)/shard_map/all_gather | solution.py:220
  10.1 25.6 %copy-start.6 = (f32[1,512,2048]{2,1,0:T(8,128)S(1)}, f32[1,512,2048]{2,1,0:T(8,128)}, u32[]{:S(2)}) copy-start(f32[1,512,2048]{2,1,0:T(8,128)} %param.26) | copy-start | bytes 12582916
  13.4 31.8 %copy-start.60 = (f32[512]{0:T(512)}, f32[512]{0:T(512)S(1)}, u32[]{:S(2)}) copy-start(f32[512]{0:T(512)S(1)} %fusion.1332) | copy-start | bytes 6148
  223.2 148.5 %all-gather.11.cloned.1.call-start = ((), (), s32[]{:S(2)}) async-start(), calls=%async_computation.12 | async-start | bytes 4718592 | tf_op jit(solution)/shard_map/all_gather | solution.py:233
  224.0 223.2 %all-gather.9.cloned.1.call-start = ((), (), s32[]{:S(2)}) async-start(), calls=%async_computation.7 | async-start | bytes 4718592 | tf_op jit(solution)/shard_map/all_gather | solution.py:223
  234.3 69.3 %copy-start.75 = (f32[256]{0:T(256)S(1)}, f32[256]{0:T(256)}, u32[]{:S(2)}) copy-start(f32[256]{0:T(256)} %param.43) | copy-start | bytes 3076
  303.5 286.1 %reduce-scatter.13.cloned.1.call-start = ((), (), s32[]{:S(2)}) async-start(), calls=%async_computation.9 | async-start | bytes 4718592 | tf_op jit(solution)/shard_map/reduce_scatter | solution.py:236
  321.8 177.9 %copy-start.34 = (f32[8,1,256]{2,1,0:T(1,128)}, f32[8,1,256]{2,1,0:T(1,128)S(1)}, u32[]{:S(2)}) copy-start(f32[8,1,256]{2,1,0:T(1,128)S(1)} %all-gather.2) | copy-start | bytes 24580
  502.6 179.4 %reduce-scatter.11.cloned.1.call-start = ((), (), s32[]{:S(2)}) async-start(), calls=%async_computation.8 | async-start | bytes 4718592 | tf_op jit(solution)/shard_map/reduce_scatter | solution.py:230
  517.1 257.3 %reduce-scatter.15.cloned.1.call-start = ((), (), s32[]{:S(2)}) async-start(), calls=%async_computation.10 | async-start | bytes 4718592 | tf_op jit(solution)/shard_map/reduce_scatter | solution.py:241
  595.8 86.1 %copy-start.22 = (f32[512,256]{1,0:T(8,128)S(1)}, f32[512,256]{1,0:T(8,128)}, u32[]{:S(2)}) copy-start(f32[512,256]{1,0:T(8,128)} %get-tuple-element.1711) | copy-start | bytes 1572868
  595.8 86.1 %copy-start.26 = (f32[512,256]{1,0:T(8,128)S(1)}, f32[512,256]{1,0:T(8,128)}, u32[]{:S(2)}) copy-start(f32[512,256]{1,0:T(8,128)} %get-tuple-element.1712) | copy-start | bytes 1572868
  595.8 178.6 %copy-start.20 = (f32[512,256]{1,0:T(8,128)S(1)}, f32[512,256]{1,0:T(8,128)}, u32[]{:S(2)}) copy-start(f32[512,256]{1,0:T(8,128)} %transpose.2140) | copy-start | bytes 1572868
  595.8 178.6 %copy-start.63 = (f32[512]{0:T(512)S(1)}, f32[512]{0:T(512)}, u32[]{:S(2)}) copy-start(f32[512]{0:T(512)} %copy-done.62) | copy-start | bytes 6148
  595.8 178.6 %copy-start.65 = (f32[512]{0:T(512)S(1)}, f32[512]{0:T(512)}, u32[]{:S(2)}) copy-start(f32[512]{0:T(512)} %copy-done.64) | copy-start | bytes 6148
  595.8 178.6 %copy-start.69 = (f32[256]{0:T(256)S(1)}, f32[256]{0:T(256)}, u32[]{:S(2)}) copy-start(f32[256]{0:T(256)} %param.39) | copy-start | bytes 3076
  595.8 178.5 %copy-start.71 = (f32[256]{0:T(256)S(1)}, f32[256]{0:T(256)}, u32[]{:S(2)}) copy-start(f32[256]{0:T(256)} %param.40) | copy-start | bytes 3076
  595.9 647.0 %reduce-scatter.21.cloned.1.call-start = ((), (), s32[]{:S(2)}) async-start(), calls=%async_computation.14 | async-start | bytes 1179648
  599.6 649.2 %reduce-scatter.19.cloned.1.call-start = ((), (), s32[]{:S(2)}) async-start(), calls=%async_computation.13 | async-start | bytes 1179648
  1169.7 153.0 %reduce-scatter.17.cloned.1.call-start = ((), (), s32[]{:S(2)}) async-start(), calls=%async_computation.11 | async-start | bytes 4718592 | tf_op jit(solution)/shard_map/reduce_scatter | solution.py:280
  1176.4 612.1 %all-reduce.42.cloned.1.call-start = ((), (), s32[]{:S(2)}) async-start(), calls=%async_computation.15 | async-start | bytes 55050240 | tf_op jit(solution)/shard_map/psum | solution.py:306
  (90 other events, 780.7 us)
Sparse Core Ops, SparseCore 0:
  223.3 73.3 all-gather.6
  298.8 72.8 all-gather.10
  374.3 72.8 all-gather.8
  502.7 86.8 reduce-scatter.12
  593.6 88.2 reduce-scatter.10
  686.0 88.3 reduce-scatter.14
  777.8 64.0 reduce-scatter.20
  1169.8 61.5 reduce-scatter.18
  1235.0 87.5 reduce-scatter.16
  1327.7 460.6 all-reduce.41
where the time goes:
time: 1830 us; the launch traced here: 1820 us
  waiting for transfers between devices  940 us (51%)
  matrix products  446 us (24%)
  local copies, waits for them, and re-layouts  118 us (6%)
  other arithmetic  114 us (6%)
  blocking collectives  90.4 us (5%)
  loops' own time  79.8 us (4%)
    psum x1, waiting for transfers between devices, on_device(): lax.psum((d_gain_one_sum[0], d_query, d_key, d_value, d_rate, d_rate_bias...  464 us
    dot_general x16, matrix products, product(): jnp.dot(left, right, precision=precise, preferred_element_type=jnp.float32)  181 us
    reduce_scatter x1, waiting for transfers between devices, on_device(): lax.psum_scatter(right_product(d_hidden, w_out), 'heads', scatter_dimensi...  86.2 us
    reduce_scatter x1, waiting for transfers between devices, on_device(): lax.psum_scatter(partial_out, 'heads', scatter_dimension=1, tiled=True)  82.3 us
    another operation x2, loops' own time, ttt_layer(): lax.scan(jax.checkpoint(turn), initial, (split(queries), split(keys), spl...  79.8 us
    reduce_scatter x1, waiting for transfers between devices, on_device(): lax.psum_scatter(d_whole, 'heads', scatter_dimension=1, tiled=True)  72.4 us
    all_gather x1, waiting for transfers between devices, on_device(): whole = lax.all_gather(hidden_in, 'heads', axis=1, tiled=True)  62.7 us
    all_gather x1, waiting for transfers between devices, on_device(): gathered = lax.all_gather(gated, 'heads', axis=1, tiled=True)  62.5 us
  transfers between devices with their start and end apart: 10, of which 8 were waited for; matrix products, arithmetic and copies ran while one was open for 25% of the time, Pallas kernels for 0%

commit v1 on v0

v1 whole, which is shorter than its diff:
```python
import functools
import jax, jax.numpy as jnp
from jax import lax
from jax.experimental import pallas as pl
from jax.experimental.pallas import tpu as pltpu

from jax.sharding import PartitionSpec as P

MB = 16
CH = 128
epsilon = 1e-06
f32 = jnp.float32
bf16 = jnp.bfloat16
NN = ((1,), (0,))


def split(x):
    hi = x.astype(bf16)
    return hi, (x - hi.astype(f32)).astype(bf16)


def mm(a, b, dims=NN):
    def one(p, q):
        return lax.dot_general(p, q, (dims, ((), ())), preferred_element_type=f32)

    return one(a[0], b[0]) + (one(a[0], b[1]) + one(a[1], b[0]))


def wide(x):
    hi, lo = split(x)
    return jnp.concatenate([hi, lo], axis=1)


def tall_dot(x, pair):
    rows = x.shape[0]
    cols = pair.shape[1] // 2
    hi, lo = split(x)
    out = lax.dot_general(
        jnp.concatenate([hi, lo], axis=0), pair, (NN, ((), ())), preferred_element_type=f32
    )
    top, low = out[:rows], out[rows:]
    return top[:, :cols] + (top[:, cols:] + low[:, :cols])


def iota(shape, dim):
    return lax.broadcasted_iota(jnp.int32, shape, dim)


def head_sum(x, hd):
    rows, cols = x.shape
    parts = [
        jnp.broadcast_to(jnp.sum(x[i : i + hd], axis=0, keepdims=True), (hd, cols))
        for i in range(0, rows, hd)
    ]
    return parts[0] if len(parts) == 1 else jnp.concatenate(parts, axis=0)


def lane_sum(x):
    return jnp.sum(x, axis=1, keepdims=True)


def coefficients(transposed):
    source = iota((CH, CH), 1 if transposed else 0)
    target = iota((CH, CH), 0 if transposed else 1)
    before = (source // MB < target // MB).astype(f32) * (1.0 / MB)
    inside = ((source // MB == target // MB) & (source <= target)).astype(f32)
    return before, before + inside / ((target % MB) + 1).astype(f32)


def forward_body(
    joined, rate, rate_t, seg, seg_t, w0, b0, gain, shift, mixed, z_out, zb_out, w_out, b_out,
    w_s, b_s, z_s, tau_s, a_s, m_s, *, hd, heads,
):
    pairs = heads * hd // CH
    per = CH // hd
    span = heads * hd
    chunks = joined.shape[0] // CH
    n_inv = 1.0 / hd
    row_head = iota((CH, CH), 0) // hd
    lane_head = iota((CH, CH), 1) // hd
    lane_block = iota((hd, CH), 1) // MB
    block_diag = row_head == lane_head
    w_s[...] = jnp.zeros_like(w_s)
    b_s[...] = jnp.zeros_like(b_s)

    def chunk(c, carry):
        ts = pl.multiple_of(c * CH, CH)
        here = pl.ds(ts, CH)
        seg_row = seg_t[:, here]
        seg_col = seg[here, :]
        last_seg = seg_row[:, CH - 1 : CH]
        prev = jnp.max(jnp.where(iota(seg_t.shape, 1) < ts, seg_t[...], 0.0), keepdims=True)
        carried = seg_row == prev
        in_last = (seg_row == last_seg).astype(f32)
        whole = last_seg == prev
        same = seg_col == seg_row
        before, within = coefficients(False)
        before = jnp.where(same, before, 0.0)
        within = jnp.where(same, within, 0.0)
        for p in range(pairs):
            rows = slice(p * CH, (p + 1) * CH)
            kn = joined[here, span + p * CH : span + (p + 1) * CH]
            qn = joined[here, p * CH : (p + 1) * CH]
            vn = joined[here, 2 * span + p * CH : 2 * span + (p + 1) * CH]
            k_t, q_t, v_t = kn.T, qn.T, vn.T
            ks, kts, qts = split(kn), split(k_t), split(q_t)
            ws, w0s = split(w_s[rows]), split(w0[rows])
            bias = jnp.where(carried, b_s[rows], b0[rows])
            z_s[rows] = jnp.where(carried, mm(ws, kts), mm(w0s, kts)) + bias
            zb_out[rows, here] = jnp.where(carried, mm(ws, qts), mm(w0s, qts)) + bias
            w_out[c, rows] = w_s[rows]
            b_out[c, rows] = b_s[rows]
            tau_s[rows] = gain[rows] * (shift[rows] - v_t + k_t)
            for hh in range(per):
                h = p * per + hh
                own = (row_head == hh).astype(bf16)
                r_col = rate[here, h : h + 1]
                score = mm(ks, (kts[0] * own, kts[1] * own))
                a_s[h] = wide((score + 1.0) * (before * r_col))
                score = mm(ks, (qts[0] * own, qts[1] * own))
                m_s[h] = wide((score + 1.0) * (within * r_col))

        gsq = [jnp.broadcast_to(gain[h * hd : (h + 1) * hd] ** 2, (hd, CH)) for h in range(heads)]
        tsum = [
            jnp.sum(tau_s[h * hd : (h + 1) * hd], axis=0, keepdims=True) * n_inv
            for h in range(heads)
        ]

        def inner(h, z):
            tau = tau_s[h * hd : (h + 1) * hd]
            zg = z * gsq[h]
            m2 = jnp.sum(z * z, axis=0, keepdims=True) * n_inv
            a1 = jnp.sum(zg, axis=0, keepdims=True) * n_inv
            a2 = jnp.sum(z * zg, axis=0, keepdims=True) * n_inv
            a3 = jnp.sum(z * tau, axis=0, keepdims=True) * n_inv
            s = lax.rsqrt(m2 + epsilon)
            c_eu = s * (s * a2 + a3)
            e_mean = s * a1 + tsum[h]
            return (s * s) * (zg - c_eu * z) + s * (tau - e_mean)

        def step(t, zs):
            now = lane_block == t
            new = []
            for h in range(heads):
                g = jnp.where(now, inner(h, zs[h]), 0.0)
                new.append(zs[h] - tall_dot(g, a_s[h]))
            return tuple(new)

        zs = tuple(z_s[h * hd : (h + 1) * hd] for h in range(heads))
        zs = lax.fori_loop(0, CH // MB - 1, step, zs)
        for p in range(pairs):
            rows = slice(p * CH, (p + 1) * CH)
            gs = []
            outs = []
            for hh in range(per):
                h = p * per + hh
                hr = slice(h * hd, (h + 1) * hd)
                z_out[hr, here] = zs[h]
                g = inner(h, zs[h])
                zb = zb_out[hr, here] - tall_dot(g, m_s[h])
                zb_out[hr, here] = zb
                sb = lax.rsqrt(jnp.sum(zb * zb, axis=0, keepdims=True) * n_inv + epsilon)
                outs.append(zb * sb * gain[hr] + shift[hr])
                gs.append(g * (rate_t[h : h + 1, here] * in_last * (1.0 / MB)))
            gw = jnp.concatenate(gs, axis=0)
            lanes = slice(p * CH, (p + 1) * CH)
            mixed[here, lanes] = joined[here, lanes] + jnp.concatenate(outs, axis=0).T
            kn = joined[here, span + p * CH : span + (p + 1) * CH]
            upd = mm(split(gw), split(kn))
            w_s[rows] = jnp.where(whole, w_s[rows], w0[rows]) - jnp.where(block_diag, upd, 0.0)
            b_s[rows] = jnp.where(whole, b_s[rows], b0[rows]) - lane_sum(gw)
        return carry

    lax.fori_loop(0, chunks, chunk, 0)


def ttt_forward(joined, rate, rate_t, seg, seg_t, w0, b0, gain, shift, hd, heads):
    length = joined.shape[0]
    span = heads * hd
    chunks = length // CH
    shape = jax.ShapeDtypeStruct
    return pl.pallas_call(
        functools.partial(forward_body, hd=hd, heads=heads),
        out_shape=(
            shape((length, span), f32),
            shape((span, length), f32),
            shape((span, length), f32),
            shape((chunks, span, CH), f32),
            shape((chunks, span, 1), f32),
        ),
        scratch_shapes=[
            pltpu.VMEM((span, CH), f32),
            pltpu.VMEM((span, 1), f32),
            pltpu.VMEM((span, CH), f32),
            pltpu.VMEM((span, CH), f32),
            pltpu.VMEM((heads, CH, 2 * CH), bf16),
            pltpu.VMEM((heads, CH, 2 * CH), bf16),
        ],
        compiler_params=pltpu.CompilerParams(vmem_limit_bytes=48 << 20),
        name="inner_forward",
    )(joined, rate, rate_t, seg, seg_t, w0, b0, gain, shift)


def backward_body(
    joined, rate_t, seg, seg_t, w0, b0, gain, shift, z_in, zb_in, w_in, b_in, dy,
    dq_out, dk_out, dv_out, dr_out, dw_out, db_out, dg_out, dsh_out,
    dw_s, db_s, p_s, u_s, f_s, bb_s, e2_s, u2_s, gt_s, dzb_s, at_s, sc_s,
    *, hd, heads,
):
    pairs = heads * hd // CH
    per = CH // hd
    span = heads * hd
    chunks = joined.shape[0] // CH
    n_inv = 1.0 / hd
    row_head = iota((CH, CH), 0) // hd
    lane_head = iota((CH, CH), 1) // hd
    lane_block = iota((hd, CH), 1) // MB
    block_diag = row_head == lane_head
    for ref in (dw_s, db_s, dw_out, db_out, dg_out, dsh_out):
        ref[...] = jnp.zeros_like(ref)

    def mean(x):
        return head_sum(x, hd) * n_inv

    def chunk(index, carry):
        c = chunks - 1 - index
        ts = pl.multiple_of(c * CH, CH)
        here = pl.ds(ts, CH)
        seg_row = seg_t[:, here]
        seg_col = seg[here, :]
        last_seg = seg_row[:, CH - 1 : CH]
        prev = jnp.max(jnp.where(iota(seg_t.shape, 1) < ts, seg_t[...], 0.0), keepdims=True)
        carried = seg_row == prev
        carried_col = seg_col == prev
        in_last = (seg_row == last_seg).astype(f32)
        whole = last_seg == prev
        same = seg_col == seg_row
        before, within = coefficients(True)
        before = jnp.where(same, before, 0.0)
        within = jnp.where(same, within, 0.0)
        consts = {}
        for p in range(pairs):
            rows = slice(p * CH, (p + 1) * CH)
            lanes = slice(p * CH, (p + 1) * CH)
            qn = joined[here, p * CH : (p + 1) * CH]
            kn = joined[here, span + p * CH : span + (p + 1) * CH]
            vn = joined[here, 2 * span + p * CH : 2 * span + (p + 1) * CH]
            k_t, v_t, dy_t = kn.T, vn.T, dy[here, lanes].T
            qs, ks, kts = split(qn), split(kn), split(k_t)
            g_col = gain[rows]
            gsq = g_col * g_col
            zb = zb_in[rows, here]
            sb = lax.rsqrt(mean(zb * zb) + epsilon)
            ub = zb * sb
            dg_out[rows] += lane_sum(dy_t * ub)
            dsh_out[rows] += lane_sum(dy_t)
            pb = dy_t * g_col
            dzb = sb * (pb - mean(pb) - ub * mean(pb * ub))
            dzb_s[rows] = dzb
            z = z_in[rows, here]
            s = lax.rsqrt(mean(z * z) + epsilon)
            u = z * s
            gu = gsq * u
            e = gu + g_col * (shift[rows] - v_t + k_t)
            c_eu = mean(e * u)
            g_t = s * (e - mean(e) - u * c_eu)
            gt_s[rows] = g_t
            u_s[rows] = u
            f_s[rows] = g_t + s * gu
            bb_s[rows] = (s * s) * (gsq - c_eu)
            e2_s[rows] = (s * s) * (e + gu)
            u2_s[rows] = s * u
            h1 = s * mean(gu)
            h2 = 2.0 * s * c_eu + s * mean(gu * u)
            dzbs = split(dzb)
            gts = split(g_t)
            dzbn = split(dzb.T)
            from_state = mm(split(dw_s[rows]), kts) + db_s[rows]
            pieces = []
            dq = dy[here, lanes]
            dk = jnp.zeros((CH, CH), f32)
            for hh in range(per):
                h = p * per + hh
                hr = slice(hh * hd, (hh + 1) * hd)
                r_row = rate_t[h : h + 1, here]
                consts[h] = (h1[hh * hd : hh * hd + 1], h2[hh * hd : hh * hd + 1])
                own = (row_head == hh).astype(bf16)
                own_lane = (lane_head == hh).astype(bf16)
                kt_h = (kts[0] * own, kts[1] * own)
                sc = (mm(ks, kt_h) + 1.0) * before
                sc_s[h] = sc
                at_s[h] = wide(sc * r_row)
                scq = (mm(qs, kt_h) + 1.0) * within
                pt = mm(dzbn, (gts[0] * own, gts[1] * own))
                dr_out[h : h + 1, here] = -jnp.sum(pt * scq, axis=0, keepdims=True) - (
                    (1.0 / MB) * in_last
                ) * jnp.sum(g_t[hr] * from_state[hr], axis=0, keepdims=True)
                pm = pt * (within * r_row)
                pms = split(pm)
                pmts = split(pm.T)
                kn_h = (ks[0] * own_lane, ks[1] * own_lane)
                qn_h = (qs[0] * own_lane, qs[1] * own_lane)
                dq = dq - mm(pms, kn_h)
                dk = dk - mm(pmts, qn_h)
                pieces.append(
                    -mm((dzbs[0][hr], dzbs[1][hr]), split(scq * r_row))
                    - from_state[hr] * (r_row * in_last * (1.0 / MB))
                )
            p_s[rows] = jnp.concatenate(pieces, axis=0)
            w0s = split(w0[rows])
            wd = split(w_in[c, rows] - w0[rows])
            zero = jnp.zeros((), bf16)
            dzbn_c = (jnp.where(carried_col, dzbn[0], zero), jnp.where(carried_col, dzbn[1], zero))
            dq_out[here, lanes] = dq + mm(dzbn, w0s) + mm(dzbn_c, wd)
            dk_out[here, lanes] = dk

        def upstream(h, pv):
            hr = slice(h * hd, (h + 1) * hd)
            h1, h2 = consts[h]
            pm = jnp.sum(pv, axis=0, keepdims=True) * n_inv
            q = jnp.sum(pv * u_s[hr], axis=0, keepdims=True) * n_inv
            kf = jnp.sum(pv * f_s[hr], axis=0, keepdims=True) * n_inv
            kappa = kf - h1 * pm - h2 * q
            dz = (pv - pm) * bb_s[hr] - q * e2_s[hr] - kappa * u2_s[hr]
            return dz, pm, q

        def step(index, ps):
            now = lane_block == (CH // MB - 1 - index)
            new = []
            for h in range(heads):
                dz = jnp.where(now, upstream(h, ps[h])[0], 0.0)
                new.append(ps[h] - tall_dot(dz, at_s[h]))
            return tuple(new)

        ps = tuple(p_s[h * hd : (h + 1) * hd] for h in range(heads))
        ps = lax.fori_loop(0, CH // MB - 1, step, ps)

        for p in range(pairs):
            rows = slice(p * CH, (p + 1) * CH)
            lanes = slice(p * CH, (p + 1) * CH)
            qn = joined[here, p * CH : (p + 1) * CH]
            kn = joined[here, span + p * CH : span + (p + 1) * CH]
            vn = joined[here, 2 * span + p * CH : 2 * span + (p + 1) * CH]
            qs, ks = split(qn), split(kn)
            g_t = gt_s[rows]
            gts = split(g_t)
            dzs, des = [], []
            for hh in range(per):
                h = p * per + hh
                hr = slice(h * hd, (h + 1) * hd)
                dz, pm, q = upstream(h, ps[h])
                dzs.append(dz - jnp.sum(dz, axis=0, keepdims=True) * n_inv)
                z = z_in[hr, here]
                s = lax.rsqrt(jnp.sum(z * z, axis=0, keepdims=True) * n_inv + epsilon)
                des.append(s * (ps[h] - pm - u_s[hr] * q))
            dz = jnp.concatenate(dzs, axis=0)
            de = jnp.concatenate(des, axis=0)
            g_col = gain[rows]
            gde = g_col * de
            t_t = shift[rows] + (kn - vn).T
            dg_out[rows] += lane_sum((2.0 * g_col * u_s[rows] + t_t) * de)
            dsh_out[rows] += lane_sum(gde)
            gden = gde.T
            dv_out[here, lanes] = -gden
            dzn = split(dz.T)
            dk = dk_out[here, lanes] + gden
            r_rows = []
            for hh in range(per):
                h = p * per + hh
                r_row = rate_t[h : h + 1, here]
                own = (row_head == hh).astype(bf16)
                own_lane = (lane_head == hh).astype(bf16)
                rt = mm(dzn, (gts[0] * own, gts[1] * own))
                dr_out[h : h + 1, here] -= jnp.sum(rt * sc_s[h], axis=0, keepdims=True)
                ra = rt * (before * r_row)
                dk = dk - mm(split(ra + ra.T), (ks[0] * own_lane, ks[1] * own_lane))
                r_rows.append(jnp.broadcast_to(r_row * in_last * (1.0 / MB), (hd, CH)))
            gw = g_t * jnp.concatenate(r_rows, axis=0)
            w0s = split(w0[rows])
            wd = split(w_in[c, rows] - w0[rows])
            zero = jnp.zeros((), bf16)
            dzn_c = (jnp.where(carried_col, dzn[0], zero), jnp.where(carried_col, dzn[1], zero))
            dk = dk + mm(dzn, w0s) + mm(dzn_c, wd) - mm(split(gw.T), split(dw_s[rows]))
            dk_out[here, lanes] = dk
            dzb = dzb_s[rows]
            dzc = jnp.where(carried, dz, 0.0)
            dzbc = jnp.where(carried, dzb, 0.0)
            diag = jnp.where(block_diag, mm(split(dzc), ks) + mm(split(dzbc), qs), 0.0)
            rest = jnp.where(
                block_diag, mm(split(dz - dzc), ks) + mm(split(dzb - dzbc), qs), 0.0
            )
            dw = dw_s[rows]
            db = db_s[rows]
            dw_out[rows] += jnp.where(whole, 0.0, dw) + rest
            db_out[rows] += jnp.where(whole, 0.0, db) + lane_sum(dz - dzc + dzb - dzbc)
            dw_s[rows] = jnp.where(whole, dw, 0.0) + diag
            db_s[rows] = jnp.where(whole, db, 0.0) + lane_sum(dzc + dzbc)
        return carry

    lax.fori_loop(0, chunks, chunk, 0)


def ttt_backward(joined, rate_t, seg, seg_t, w0, b0, gain, shift, saved, dy, hd, heads):
    length = joined.shape[0]
    span = heads * hd
    shape = jax.ShapeDtypeStruct
    return pl.pallas_call(
        functools.partial(backward_body, hd=hd, heads=heads),
        out_shape=(
            shape((length, span), f32),
            shape((length, span), f32),
            shape((length, span), f32),
            shape((heads, length), f32),
            shape((span, CH), f32),
            shape((span, 1), f32),
            shape((span, 1), f32),
            shape((span, 1), f32),
        ),
        scratch_shapes=[
            pltpu.VMEM((span, CH), f32),
            pltpu.VMEM((span, 1), f32),
        ]
        + [pltpu.VMEM((span, CH), f32)] * 8
        + [
            pltpu.VMEM((heads, CH, 2 * CH), bf16),
            pltpu.VMEM((heads, CH, CH), f32),
        ],
        compiler_params=pltpu.CompilerParams(vmem_limit_bytes=48 << 20),
        name="inner_backward",
    )(joined, rate_t, seg, seg_t, w0, b0, gain, shift, *saved, dy)


def state_in(inner_weight, inner_bias):
    heads, hd, _ = inner_weight.shape
    per = CH // hd
    w_t = jnp.swapaxes(inner_weight, 1, 2)
    w_t = w_t - jnp.mean(w_t, axis=1, keepdims=True)
    placed = [
        jnp.pad(w_t[h], ((0, 0), ((h % per) * hd, CH - hd - (h % per) * hd)))
        for h in range(heads)
    ]
    b = inner_bias - jnp.mean(inner_bias, axis=1, keepdims=True)
    return jnp.concatenate(placed, axis=0), b.reshape(heads * hd, 1)


def state_back(dw, db, heads, hd):
    per = CH // hd
    parts = [
        dw[h * hd : (h + 1) * hd, (h % per) * hd : (h % per + 1) * hd] for h in range(heads)
    ]
    d = jnp.stack(parts)
    d = jnp.swapaxes(d - jnp.mean(d, axis=1, keepdims=True), 1, 2)
    b = db.reshape(heads, hd)
    return d, b - jnp.mean(b, axis=1, keepdims=True)


def product(left, right):
    return jnp.dot(left, right, precision=lax.Precision.HIGH, preferred_element_type=f32)


def left_product(left, right):
    return lax.dot_general(
        left, right, (((0,), (0,)), ((), ())), precision=lax.Precision.HIGH,
        preferred_element_type=f32,
    )


def right_product(left, right):
    return lax.dot_general(
        left, right, (((1,), (1,)), ((), ())), precision=lax.Precision.HIGH,
        preferred_element_type=f32,
    )


def heads_grid():
    size = lax.axis_size("heads")
    deep = 4 if size % 4 == 0 else 1
    return deep, size // deep


def heads_place():
    _, across = heads_grid()
    index = lax.axis_index("heads")
    return index // across, index % across


def shift(value, dz, dx):
    deep, across = heads_grid()
    pairs = [
        (h, (h // across + dz) % deep * across + (h % across + dx) % across)
        for h in range(deep * across)
    ]
    return lax.ppermute(value, "heads", pairs)


def swap(value, axis, bit):
    return lax.ppermute(value, axis, [(i, i ^ bit) for i in range(lax.axis_size(axis))])


def row_shift(value, step):
    size = lax.axis_size("rows")
    return lax.ppermute(value, "rows", [(r, (r + 2 * step) % size) for r in range(size)])


def butterfly(value, axis):
    bit = 1
    while bit < lax.axis_size(axis):
        value = value + swap(value, axis, bit)
        bit *= 2
    return value


def small_gather(value):
    size = lax.axis_size("heads")
    place = jnp.arange(size) == lax.axis_index("heads")
    place = place.reshape((size,) + (1,) * value.ndim)
    return butterfly(jnp.where(place, value[None], 0.0), "heads")


def gather_columns(value, parts=2):
    deep, across = heads_grid()
    z, x = heads_place()
    rows, cols = value.shape
    size = rows // parts
    out = jnp.zeros((rows, cols * deep * across), value.dtype)
    moving = [value[i * size : (i + 1) * size] for i in range(parts)]
    for dz in range(deep):
        if dz:
            moving = [shift(item, 1, 0) for item in moving]
        side = moving
        for dx in range(across):
            if dx:
                side = [shift(item, 0, 1) for item in side]
            column = ((z - dz) % deep * across + (x - dx) % across) * cols
            for i in range(parts):
                out = lax.dynamic_update_slice(out, side[i], (i * size, column))
    return out


def scatter_columns(value, extra=None, parts=2):
    deep, across = heads_grid()
    z, x = heads_place()
    rows, width = value.shape
    cols = width // (deep * across)
    size = rows // parts

    def piece(i, dz, dx):
        column = ((z - dz) % deep * across + (x - dx) % across) * cols
        block = lax.dynamic_slice(value, (i * size, column), (size, cols))
        if extra is not None and i == parts - 1:
            tail = lax.dynamic_slice(extra, (0, column), (extra.shape[0], cols))
            block = jnp.concatenate([block, tail], 0)
        return block

    total = [None] * parts
    for dz in list(range(1, deep)) + [0]:
        for i in range(parts):
            here = None
            for dx in list(range(1, across)) + [0]:
                block = piece(i, dz, dx)
                here = block if here is None else shift(here, 0, 1) + block
            total[i] = here if total[i] is None else shift(total[i], 1, 0) + here
    return jnp.concatenate(total, 0)


def half_of(value, index, axis):
    size = value.shape[axis] // 2
    return lax.dynamic_slice_in_dim(value, index * size, size, axis)


def both_cores(value):
    return jnp.concatenate([value, swap(value, "rows", 1)], 0)


def tokens_half(value, core):
    return jnp.concatenate(
        [half_of(value, core, 1), swap(half_of(value, 1 - core, 1), "rows", 1)], 0
    )


def finish(part, core, axis):
    total = part
    for step in range(1, lax.axis_size("rows") // 2):
        total = total + row_shift(part, step)
    other = swap(total, "rows", 1)
    first = core == 0
    return jnp.concatenate(
        [jnp.where(first, total, other), jnp.where(first, other, total)], axis
    )


def silu_parts(a):
    sig = jax.nn.sigmoid(a)
    return a * sig, sig * (1.0 + a * (1.0 - sig))


def gelu_parts(v):
    k = 0.7978845608028654
    inner = k * (v + 0.044715 * v * v * v)
    th = jnp.tanh(inner)
    slope = 0.5 * (1.0 + th) + 0.5 * v * (1.0 - th * th) * k * (1.0 + 3 * 0.044715 * v * v)
    return 0.5 * v * (1.0 + th), slope


def on_device(
    stream,
    doc_starts,
    valid_mask,
    first_gain,
    w_query,
    w_key,
    w_value,
    w_rate,
    b_rate,
    inner_weight,
    inner_bias,
    inner_gain,
    inner_shift,
    post_gain,
    post_shift,
    w_gate_attn,
    w_out,
    second_gain,
    w_gate,
    w_up,
    w_down,
    cotangent,
):
    _, length, width = stream.shape
    tokens = stream.reshape(length, width)
    slab = second_gain.shape[0]
    column = lax.axis_index("heads") * slab
    core = lax.axis_index("rows") % 2
    heads, hd = inner_bias.shape
    span = heads * hd
    total_span = span * lax.axis_size("heads")
    gains = small_gather(jnp.stack([first_gain, second_gain]))
    gain_one = gains[:, 0].reshape(width)
    gain_two = gains[:, 1].reshape(width)
    grad_output = cotangent.reshape(length, slab)
    dy_full = gather_columns(grad_output)

    w_joined = jnp.concatenate([w_query, w_key, w_value, w_gate_attn, w_rate], axis=1)
    r1 = lax.rsqrt(jnp.mean(tokens * tokens, -1, keepdims=True) + epsilon)
    normed = tokens * r1 * gain_one
    joined = product(normed, w_joined)
    gate_pre = joined[:, 3 * span : 4 * span]
    sig = jax.nn.sigmoid(joined[:, 4 * span :] + b_rate)
    rate = sig / hd
    rate_t = rate.T
    seg = jnp.cumsum(doc_starts.reshape(length)).astype(f32)
    seg, seg_t = seg[:, None], seg[None]
    w0, b0 = state_in(inner_weight, inner_bias)
    gain_col, shift_col = inner_gain.reshape(span, 1), inner_shift.reshape(span, 1)
    mixed, *saved = ttt_forward(
        joined, rate, rate_t, seg, seg_t, w0, b0, gain_col, shift_col, hd, heads
    )
    row_sums = butterfly(jnp.stack([jnp.sum(mixed, 1), jnp.sum(mixed * mixed, 1)]), "heads")
    row_mean = row_sums[0] / total_span
    inv_std = lax.rsqrt(row_sums[1] / total_span - row_mean * row_mean + epsilon)[:, None]
    centered = (mixed - row_mean[:, None]) * inv_std
    shaped = centered * post_gain + post_shift
    gate_act, gate_slope = gelu_parts(gate_pre)
    gathered = gather_columns(gate_act * shaped)
    attn = product(gathered, w_out)
    stream_cols = lax.dynamic_slice_in_dim(tokens, column, slab, 1)
    hidden = stream_cols + attn
    whole = gather_columns(hidden)

    r2 = lax.rsqrt(jnp.mean(whole * whole, -1, keepdims=True) + epsilon)
    hnorm = whole * r2 * gain_two
    a = product(hnorm, w_gate)
    c = product(hnorm, w_up)
    act, slope = silu_parts(a)
    m = act * c
    ffn = scatter_columns(product(m, w_down))
    output = hidden + ffn
    dm = right_product(dy_full, w_down)
    da = dm * c * slope
    dc = dm * act
    dhnorm = right_product(da, w_gate) + right_product(dc, w_up)
    d_gain_two = jnp.sum(dhnorm * whole * r2, 0, keepdims=True)
    weighted = dhnorm * gain_two
    d_whole = r2 * weighted - whole * (r2 * r2 * r2) * jnp.mean(
        whole * weighted, -1, keepdims=True
    )
    pad = jnp.zeros((7, width), f32)
    d_part = scatter_columns(d_whole, jnp.concatenate([d_gain_two, pad], 0))
    d_hidden = grad_output + d_part[:length]
    d_gain_two = d_part[length]

    hnorm_pair = tokens_half(hnorm, core)
    g_gate = finish(left_product(hnorm_pair, both_cores(da)), core, 0)
    g_up = finish(left_product(hnorm_pair, both_cores(dc)), core, 0)
    g_down = finish(left_product(both_cores(m), tokens_half(dy_full, core)), core, 1)

    d_gated = scatter_columns(right_product(d_hidden, w_out))
    g_out = finish(left_product(tokens_half(gathered, core), both_cores(d_hidden)), core, 0)
    d_shaped = d_gated * gate_act
    d_gate_pre = d_gated * shaped * gate_slope
    d_post_gain = jnp.sum(d_shaped * centered, 0)
    d_post_shift = jnp.sum(d_shaped, 0)
    d_center = d_shaped * post_gain
    back_sums = butterfly(
        jnp.stack([jnp.sum(d_center, 1), jnp.sum(d_center * centered, 1)]), "heads"
    )
    d_mixed = inv_std * (
        d_center - back_sums[0][:, None] / total_span
        - centered * back_sums[1][:, None] / total_span
    )
    dq, dk, dv, d_rate, dw, db, dg, dsh = ttt_backward(
        joined, rate_t, seg, seg_t, w0, b0, gain_col, shift_col, saved, d_mixed, hd, heads
    )
    d_inner_weight, d_inner_bias = state_back(dw, db, heads, hd)
    d_rate_pre = d_rate.T * rate * (1.0 - sig)
    d_joined = jnp.concatenate([dq, dk, dv, d_gate_pre, d_rate_pre], 1)
    d_normed = right_product(d_joined, w_joined)
    d_gain_one = jnp.sum(d_normed * tokens * r1, 0, keepdims=True)
    weighted = d_normed * gain_one
    d_tokens = r1 * weighted - tokens * (r1 * r1 * r1) * jnp.mean(
        tokens * weighted, -1, keepdims=True
    )
    d_part = scatter_columns(d_tokens, jnp.concatenate([d_gain_one, pad], 0))
    d_stream = d_hidden + d_part[:length]
    d_gain_one = d_part[length]
    g_joined = finish(left_product(tokens_half(normed, core), both_cores(d_joined)), core, 0)

    weights = valid_mask.reshape(-1).astype(f32)[:, None]
    stats = jnp.stack(
        [
            jnp.sum(weights * member * member)
            for member in (stream_cols, attn, hidden, ffn, output)
        ]
        + [jnp.sum(weights) / lax.axis_size("heads")]
    )
    stats = butterfly(butterfly(stats, "rows"), "heads")
    rms_values = jnp.sqrt(stats[:5] / (stats[5] * width))
    small = [
        d_gain_one, jnp.sum(d_rate_pre, 0), d_inner_weight, d_inner_bias, dg, dsh,
        d_post_gain, d_post_shift, d_gain_two,
    ]
    packed = butterfly(jnp.concatenate([item.reshape(-1) for item in small]), "rows")
    parts = []
    at = 0
    for item in small:
        parts.append(packed[at : at + item.size])
        at += item.size
    return (
        output.reshape(1, length, slab),
        d_stream.reshape(1, length, slab),
        parts[0],
        g_joined[:, :span],
        g_joined[:, span : 2 * span],
        g_joined[:, 2 * span : 3 * span],
        g_joined[:, 4 * span :],
        parts[1],
        parts[2].reshape(heads, hd, hd),
        parts[3].reshape(heads, hd),
        parts[4].reshape(heads, hd),
        parts[5].reshape(heads, hd),
        parts[6],
        parts[7],
        g_joined[:, 3 * span : 4 * span],
        g_out,
        parts[8],
        g_gate,
        g_up,
        g_down,
        rms_values,
    )


def solution(mesh):
    in_specs = (
        P("rows", None, None),
        P("rows", None),
        P("rows", None),
        P("heads"),
        P(None, "heads"),
        P(None, "heads"),
        P(None, "heads"),
        P(None, "heads"),
        P("heads"),
        P("heads", None, None),
        P("heads", None),
        P("heads", None),
        P("heads", None),
        P("heads"),
        P("heads"),
        P(None, "heads"),
        P(None, "heads"),
        P("heads"),
        P(None, "heads"),
        P(None, "heads"),
        P("heads", None),
        P("rows", None, "heads"),
    )
    out_specs = (
        P("rows", None, "heads"),
        P("rows", None, "heads"),
        P("heads"),
        P(None, "heads"),
        P(None, "heads"),
        P(None, "heads"),
        P(None, "heads"),
        P("heads"),
        P("heads", None, None),
        P("heads", None),
        P("heads", None),
        P("heads", None),
        P("heads"),
        P("heads"),
        P(None, "heads"),
        P(None, "heads"),
        P("heads"),
        P(None, "heads"),
        P(None, "heads"),
        P("heads", None),
        P(),
    )
    return jax.shard_map(
        on_device, mesh=mesh, in_specs=in_specs, out_specs=out_specs, check_vma=False
    )
```

time: 1830 us -> 931 us (0.51)
  waiting for transfers between devices: 940 us -> 473 us
  matrix products: 446 us -> 126 us
  blocking collectives: 90.4 us -> 0 us
  starting transfers between devices: 11 us -> 94.4 us
  loops' own time: 79.8 us -> 0 us
  Pallas kernels: 0 us -> 34.6 us
  local copies, waits for them, and re-layouts: 118 us -> 89.3 us
    ppermute x0 -> x133, waiting for transfers between devices: none -> 473 us  [the longest x5 236 us: row_shift(): lax.ppermute(value, 'rows', [(r, (r + 2 * step) % size) for r in range(si...]
    psum x1 -> x0, waiting for transfers between devices: 464 us -> none  [on_device(): lax.psum((d_gain_one_sum[0], d_query, d_key, d_value, d_rate, d_rate_bias...]
    dot_general x842 -> x15, matrix products: 446 us -> 126 us  [the longest x5 47.5 us: right_product(): lax.dot_general(left, right, (((1,), (1,)), ((), ())), precision=lax.Prec...]
    reduce_scatter x4 -> x0, waiting for transfers between devices: 301 us -> none  [the longest x1 86.2 us: on_device(): lax.psum_scatter(right_product(d_hidden, w_out), 'heads', scatter_dimensi...]
    all_gather x3 -> x0, waiting for transfers between devices: 175 us -> none  [the longest x1 62.7 us: on_device(): whole = lax.all_gather(hidden_in, 'heads', axis=1, tiled=True)]
    ppermute x0 -> x133, starting transfers between devices: none -> 94.4 us  [the longest x98 69.6 us: shift(): return lax.ppermute(value, 'heads', pairs)]
    another operation x2 -> x0, loops' own time: 79.8 us -> none  [ttt_layer(): lax.scan(jax.checkpoint(turn), initial, (split(queries), split(keys), spl...]
    reduce_sum x341 -> x9, other arithmetic: 61.9 us -> 7 us  [the longest x1 2.54 us: on_device(): r1 = lax.rsqrt(jnp.mean(tokens * tokens, -1, keepdims=True) + epsilon)]
  transfers between devices with their start and end apart: 10 -> 133, of which waited for: 8 -> 61; matrix products, arithmetic and copies ran while one was open for 25% -> 25% of each run, Pallas kernels for 0% -> 4%
where the time goes in v1:
time: 931 us; the launch traced here: 926 us
  waiting for transfers between devices  473 us (51%)
  matrix products  126 us (14%)
  other arithmetic  104 us (11%)
  starting transfers between devices  94.4 us (10%)
  local copies, waits for them, and re-layouts  89.3 us (10%)
  Pallas kernels  34.6 us (4%)
    ppermute x5, waiting for transfers between devices, row_shift(): lax.ppermute(value, 'rows', [(r, (r + 2 * step) % size) for r in range(si...  236 us
    ppermute x98, waiting for transfers between devices, shift(): return lax.ppermute(value, 'heads', pairs)  210 us
    ppermute x98, starting transfers between devices, shift(): return lax.ppermute(value, 'heads', pairs)  69.6 us
    dot_general x5, matrix products, right_product(): lax.dot_general(left, right, (((1,), (1,)), ((), ())), precision=lax.Prec...  47.5 us
    dot_general x5, matrix products, left_product(): lax.dot_general(left, right, (((0,), (0,)), ((), ())), precision=lax.Prec...  44.5 us
    unnamed x201, local copies, waits for them, and re-layouts  35.6 us
    dot_general x5, matrix products, product(): jnp.dot(left, right, precision=lax.Precision.HIGH, preferred_element_type...  33.9 us
    ppermute x30, waiting for transfers between devices, swap(): lax.ppermute(value, axis, [(i, i ^ bit) for i in range(lax.axis_size(axis...  27.6 us
  transfers between devices with their start and end apart: 133, of which 61 were waited for; matrix products, arithmetic and copies ran while one was open for 25% of the time, Pallas kernels for 4%

profile of v1, /device:TPU:0, one launch (start us, length us, event | category | flops | bytes accessed | tf_op | source)
XLA Modules:
  0.0 925.5 jit_solution(9289173873592272002)
XLA Ops:
  33.7 13.0 %fusion.93.joined = f32[512,1028]{1,0:T(8,128)S(1)} fusion(f32[512,2048]{1,0:T(8,128)S(1)} %fusion.16, f32[2048,1028]{1,0:T(8,128)} %copy-done.31), kind=kOutput, calls=%fused_computation.359 | convolution fusion | flops 6467616768 | bytes 14721024 | tf_op jit(solution)/shard_map/dot_general | solution.py:458
  51.6 12.8 %inner_forward.1 = (f32[512,256]{1,0:T(8,128)S(1)}, f32[256,512]{1,0:T(8,128)S(1)}, f32[256,512]{1,0:T(8,128)S(1)}, f32[4,256,128]{2,1,0:T(8,128)S(1)}, f32[4,256,1]{2,1,0:T(8,128)S(1)}) custom-call(f32[512,1028]{1,0:T(8,128)S(1)} %copy-done.3, f32[512,4]{1,0:T(8,128)S(1)} %copy-done.4, f32[4,512]{1,0:T(4,128)S(1)} %copy.109.rate_t, ...), custom_call_target="tpu_custom_call" | custom-call | tf_op jit(solution)/shard_map/inner_forward/pallas_call | solution.py:182
  100.2 10.4 %collective-permute-done.52 = f32[256,256]{1,0:T(8,128)S(1)} collective-permute-done((f32[256,256]{1,0:T(8,128)}, f32[256,256]{1,0:T(8,128)S(1)}, u32[]{:S(2)}, u32[]{:S(2)}) %collective-permute-start.52) | collective-permute-done | bytes 262176 | tf_op jit(solution)/shard_map/ppermute | solution.py:493
  116.3 8.8 collective-permute-done.10
  127.5 6.7 collective-permute-done.57
  154.8 14.7 %collective-permute-done.18 = f32[256,256]{1,0:T(8,128)S(1)} collective-permute-done((f32[256,256]{1,0:T(8,128)S(1)}, f32[256,256]{1,0:T(8,128)S(1)}, u32[]{:S(2)}, u32[]{:S(2)}) %collective-permute-start.18) | collective-permute-done | bytes 262176 | tf_op jit(solution)/shard_map/ppermute | solution.py:493
  178.8 12.4 %collective-permute-done.23 = f32[256,256]{1,0:T(8,128)S(1)} collective-permute-done((f32[256,256]{1,0:T(8,128)S(1)}, f32[256,256]{1,0:T(8,128)S(1)}, u32[]{:S(2)}, u32[]{:S(2)}) %collective-permute-start.23) | collective-permute-done | bytes 262176 | tf_op jit(solution)/shard_map/ppermute | solution.py:493
  227.8 17.8 %fusion.69 = (f32[512,688]{0,1:T(8,128)}, f32[512,688]{0,1:T(8,128)S(1)}, f32[512,688]{0,1:T(8,128)}) fusion(f32[512,688]{0,1:T(8,128)S(1)} %fusion.94, f32[512,688]{0,1:T(8,128)S(1)} %fusion.95, f32[512,2048]{1,0:T(8,128)} %constant_dynamic-update-slice_fusion.32, f32[688,2048]{1,0:T(8,128)S(1)} %bitcast.121), kind=kOutput, calls=%fused_computation.170 | convolution fusion | flops 4332748800 | bytes 16875520 | tf_op jit(solution)/shard_map/dot_general | solution.py:469
  251.5 8.7 multiply_reduce_fusion.1
  269.2 6.4 collective-permute-done.64
  279.3 7.7 collective-permute-done.66
  314.8 7.5 collective-permute-done.72
  340.8 7.3 fusion.96
  434.9 21.8 %inner_backward.1 = (f32[512,256]{1,0:T(8,128)S(1)}, f32[512,256]{1,0:T(8,128)S(1)}, f32[512,256]{1,0:T(8,128)S(1)}, f32[4,512]{1,0:T(4,128)S(1)}, f32[256,128]{...) custom-call(f32[512,1028]{1,0:T(8,128)} %copy-done.2, ...), custom_call_target="tpu_custom_call" | custom-call | tf_op jit(solution)/shard_map/inner_backward/pallas_call | solution.py:407
  476.1 13.0 %fusion.19 = (f32[512]{0:T(512)S(1)}, f32[2048]{0:T(1024)S(1)}, f32[512,2048]{1,0:T(8,128)S(1)}) fusion(f32[1,512,2048]{2,1,0:T(8,128)} %param.22, f32[2048]{0:T(1024)S(1)} %bitcast.128, f32[512]{0:T(512)S(1)} %get-tuple-element.285, f32[512,1028]{1,0:T(8,128)} %get-tuple-element.233, f32[2048,1028]{1,0:T(8,128)} %copy-done.31), kind=kOutput, calls=%fused_computation.36 | convolution fusion | flops 6473905664 | bytes 18935808 | tf_op jit(solution)/shard_map/dot_general | solution.py:469
  493.0 6.1 collective-permute-done.130
  514.4 13.1 %fusion = f32[1024,1028]{0,1:T(8,128)} fusion(f32[512,1028]{1,0:T(8,128)} %copy.124, f32[512,1028]{1,0:T(8,128)} %get-tuple-element.233, f32[512,1024]{1,0:T(8,128)} %collective-permute-done.109, f32[512,1024]{1,0:T(8,128)} %get-tuple-element.165), kind=kOutput, calls=%fused_computation.11 | convolution fusion | flops 6469718016 | bytes 12615680 | tf_op jit(solution)/shard_map/dot_general | solution.py:462
  536.4 8.8 fusion.11
  548.3 8.7 fusion.22
  557.5 7.9 fusion.23
  587.2 235.5 %collective-permute-done.115 = f32[1024,256]{1,0:T(8,128)S(1)} collective-permute-done((f32[1024,256]{1,0:T(8,128)}, f32[1024,256]{1,0:T(8,128)S(1)}, u32[]{:S(2)}, u32[]{:S(2)}) %collective-permute-start.115) | collective-permute-done | bytes 1048608 | tf_op jit(solution)/shard_map/ppermute | solution.py:502
  849.2 7.0 add.908
  865.0 7.1 collective-permute-done.105
  891.5 7.5 broadcast_select_fusion.5
  (671 shorter events, 450.6 us)
Async XLA Ops:
  2.7 84.2 %collective-permute-start.49 = (f32[256,256]{1,0:T(8,128)}, f32[256,256]{1,0:T(8,128)}, u32[]{:S(2)}, u32[]{:S(2)}) collective-permute-start(f32[256,256]{1,0:T(8,128)} %get-tuple-element.239), channel_id=1, source_target_pairs={{0,1},{1,0},{2,3},{3,2},{4,5},{5,4},{6,7},{7,6},{8,9},{9,8},{10,11... | collective-permute-start | bytes 786440 | tf_op jit(solution)/shard_map/ppermute | solution.py:493
  5.7 83.4 %collective-permute-start.51 = (f32[256,256]{1,0:T(8,128)}, f32[256,256]{1,0:T(8,128)}, u32[]{:S(2)}, u32[]{:S(2)}) collective-permute-start(f32[256,256]{1,0:T(8,128)} %get-tuple-element.239), channel_id=1, source_target_pairs={{0,2},{1,3},{2,4},{3,5},{4,6},{5,7},{6,0},{7,1},{8,10},{9,11},{10,... | collective-permute-start | bytes 786440 | tf_op jit(solution)/shard_map/ppermute | solution.py:493
  7.2 76.3 %collective-permute-start.48 = (f32[256,256]{1,0:T(8,128)}, f32[256,256]{1,0:T(8,128)}, u32[]{:S(2)}, u32[]{:S(2)}) collective-permute-start(f32[256,256]{1,0:T(8,128)} %get-tuple-element.240), channel_id=1, source_target_pairs={{0,1},{1,0},{2,3},{3,2},{4,5},{5,4},{6,7},{7,6},{8,9},{9,8},{10,11... | collective-permute-start | bytes 786440 | tf_op jit(solution)/shard_map/ppermute | solution.py:493
  7.8 81.3 %collective-permute-start.50 = (f32[256,256]{1,0:T(8,128)}, f32[256,256]{1,0:T(8,128)}, u32[]{:S(2)}, u32[]{:S(2)}) collective-permute-start(f32[256,256]{1,0:T(8,128)} %get-tuple-element.240), channel_id=1, source_target_pairs={{0,2},{1,3},{2,4},{3,5},{4,6},{5,7},{6,0},{7,1},{8,10},{9,11},{10,... | collective-permute-start | bytes 786440 | tf_op jit(solution)/shard_map/ppermute | solution.py:493
  114.1 29.9 %collective-permute-start.59 = (f32[256,256]{1,0:T(8,128)S(1)}, f32[256,256]{1,0:T(8,128)S(1)}, u32[]{:S(2)}, u32[]{:S(2)}) collective-permute-start(f32[256,256]{1,0:T(8,128)S(1)} %collective-permute-done.55), channel_id=1, source_target_pairs={{0,2},{1,3},{2,4},{3,5},{4,6},{5,7},{6,0},{7,1},{8,10},{9,11},{10,... | collective-permute-start | bytes 786440 | tf_op jit(solution)/shard_map/ppermute | solution.py:493
  144.1 33.3 %collective-permute-start.60 = (f32[256,256]{1,0:T(8,128)S(1)}, f32[256,256]{1,0:T(8,128)S(1)}, u32[]{:S(2)}, u32[]{:S(2)}) collective-permute-start(f32[256,256]{1,0:T(8,128)S(1)} %collective-permute-done.58), channel_id=1, source_target_pairs={{0,1},{1,0},{2,3},{3,2},{4,5},{5,4},{6,7},{7,6},{8,9},{9,8},{10,11... | collective-permute-start | bytes 786440 | tf_op jit(solution)/shard_map/ppermute | solution.py:493
  144.3 33.8 %collective-permute-start.61 = (f32[256,256]{1,0:T(8,128)S(1)}, f32[256,256]{1,0:T(8,128)S(1)}, u32[]{:S(2)}, u32[]{:S(2)}) collective-permute-start(f32[256,256]{1,0:T(8,128)S(1)} %collective-permute-done.59), channel_id=1, source_target_pairs={{0,1},{1,0},{2,3},{3,2},{4,5},{5,4},{6,7},{7,6},{8,9},{9,8},{10,11... | collective-permute-start | bytes 786440 | tf_op jit(solution)/shard_map/ppermute | solution.py:493
  419.8 72.3 %collective-permute-start.109 = (f32[512,1024]{1,0:T(8,128)}, f32[512,1024]{1,0:T(8,128)}, u32[]{:S(2)}, u32[]{:S(2)}) collective-permute-start(f32[512,1024]{1,0:T(8,128)} %get-tuple-element.166), channel_id=1, source_target_pairs={{0,8},{8,0},{16,24},{24,16},{1,9},{9,1},{17,25},{25,17},{2,10},{10... | collective-permute-start | bytes 6291464 | tf_op jit(solution)/shard_map/ppermute | solution.py:497
  419.9 82.2 %collective-permute-start.125 = (f32[512,1024]{1,0:T(8,128)}, f32[512,1024]{1,0:T(8,128)}, u32[]{:S(2)}, u32[]{:S(2)}) collective-permute-start(f32[512,1024]{1,0:T(8,128)} %get-tuple-element.160), channel_id=1, source_target_pairs={{0,8},{8,0},{16,24},{24,16},{1,9},{9,1},{17,25},{25,17},{2,10},{10... | collective-permute-start | bytes 6291464 | tf_op jit(solution)/shard_map/ppermute | solution.py:497
  420.4 90.4 %collective-permute-start.121 = (f32[512,688]{0,1:T(8,128)}, f32[512,688]{0,1:T(8,128)}, u32[]{:S(2)}, u32[]{:S(2)}) collective-permute-start(f32[512,688]{0,1:T(8,128)} %get-tuple-element.229), channel_id=1, source_target_pairs={{0,8},{8,0},{16,24},{24,16},{1,9},{9,1},{17,25},{25,17},{2,10},{10... | collective-permute-start | bytes 4227080 | tf_op jit(solution)/shard_map/ppermute | solution.py:497
  432.0 58.1 %collective-permute-start.129 = (f32[6]{0:T(128)}, f32[6]{0:T(128)}, u32[]{:S(2)}, u32[]{:S(2)}) collective-permute-start(f32[6]{0:T(128)} %add.913), channel_id=1, source_target_pairs={{0,16},{8,24},{16,0},{24,8},{1,17},{9,25},{17,1},{25,9},{2,18},{10... | collective-permute-start | bytes 80 | tf_op jit(solution)/shard_map/ppermute | solution.py:497
  476.1 31.7 %collective-permute-start.110 = (f32[512,1028]{0,1:T(8,128)}, f32[512,1028]{0,1:T(8,128)}, u32[]{:S(2)}, u32[]{:S(2)}) collective-permute-start(f32[512,1028]{0,1:T(8,128)} %copy.123), channel_id=1, source_target_pairs={{0,8},{8,0},{16,24},{24,16},{1,9},{9,1},{17,25},{25,17},{2,10},{10... | collective-permute-start | bytes 6316040 | tf_op jit(solution)/shard_map/ppermute | solution.py:497
  501.4 45.4 %collective-permute-start.117 = (f32[512,1024]{1,0:T(8,128)}, f32[512,1024]{1,0:T(8,128)}, u32[]{:S(2)}, u32[]{:S(2)}) collective-permute-start(f32[512,1024]{1,0:T(8,128)} %get-tuple-element.162), channel_id=1, source_target_pairs={{0,8},{8,0},{16,24},{24,16},{1,9},{9,1},{17,25},{25,17},{2,10},{10... | collective-permute-start | bytes 6291464 | tf_op jit(solution)/shard_map/ppermute | solution.py:497
  507.8 57.6 %collective-permute-start.113 = (f32[512,1024]{1,0:T(8,128)}, f32[512,1024]{1,0:T(8,128)}, u32[]{:S(2)}, u32[]{:S(2)}) collective-permute-start(f32[512,1024]{1,0:T(8,128)} %get-tuple-element.164), channel_id=1, source_target_pairs={{0,8},{8,0},{16,24},{24,16},{1,9},{9,1},{17,25},{25,17},{2,10},{10... | collective-permute-start | bytes 6291464 | tf_op jit(solution)/shard_map/ppermute | solution.py:497
  510.8 46.2 %collective-permute-start.118 = (f32[512,688]{0,1:T(8,128)}, f32[512,688]{0,1:T(8,128)S(1)}, u32[]{:S(2)}, u32[]{:S(2)}) collective-permute-start(f32[512,688]{0,1:T(8,128)} %copy-done.36), channel_id=1, source_target_pairs={{0,8},{8,0},{16,24},{24,16},{1,9},{9,1},{17,25},{25,17},{2,10},{10... | collective-permute-start | bytes 4227080 | tf_op jit(solution)/shard_map/ppermute | solution.py:497
  527.5 310.5 %collective-permute-start.111 = (f32[1024,1028]{0,1:T(8,128)}, f32[1024,1028]{0,1:T(8,128)}, u32[]{:S(2)}, u32[]{:S(2)}) collective-permute-start(f32[1024,1028]{0,1:T(8,128)} %fusion), channel_id=1, source_target_pairs={{0,16},{8,24},{16,0},{24,8},{1,17},{9,25},{17,1},{25,9},{2,18},{10... | collective-permute-start | bytes 12632072 | tf_op jit(solution)/shard_map/ppermute | solution.py:502
  545.2 279.3 %collective-permute-start.126 = (f32[688,1024]{1,0:T(8,128)}, f32[688,1024]{1,0:T(8,128)}, u32[]{:S(2)}, u32[]{:S(2)}) collective-permute-start(f32[688,1024]{1,0:T(8,128)} %fusion.11), channel_id=1, source_target_pairs={{0,16},{8,24},{16,0},{24,8},{1,17},{9,25},{17,1},{25,9},{2,18},{10... | collective-permute-start | bytes 8454152 | tf_op jit(solution)/shard_map/ppermute | solution.py:502
  569.8 266.1 %collective-permute-start.119 = (f32[1024,688]{0,1:T(8,128)}, f32[1024,688]{0,1:T(8,128)}, u32[]{:S(2)}, u32[]{:S(2)}) collective-permute-start(f32[1024,688]{0,1:T(8,128)} %fusion.23), channel_id=1, source_target_pairs={{0,16},{8,24},{16,0},{24,8},{1,17},{9,25},{17,1},{25,9},{2,18},{10... | collective-permute-start | bytes 8454152 | tf_op jit(solution)/shard_map/ppermute | solution.py:502
  570.3 265.9 %collective-permute-start.122 = (f32[1024,688]{0,1:T(8,128)}, f32[1024,688]{0,1:T(8,128)}, u32[]{:S(2)}, u32[]{:S(2)}) collective-permute-start(f32[1024,688]{0,1:T(8,128)} %fusion.22), channel_id=1, source_target_pairs={{0,16},{8,24},{16,0},{24,8},{1,17},{9,25},{17,1},{25,9},{2,18},{10... | collective-permute-start | bytes 8454152 | tf_op jit(solution)/shard_map/ppermute | solution.py:502
  582.8 239.9 %collective-permute-start.115 = (f32[1024,256]{1,0:T(8,128)}, f32[1024,256]{1,0:T(8,128)S(1)}, u32[]{:S(2)}, u32[]{:S(2)}) collective-permute-start(f32[1024,256]{1,0:T(8,128)} %fusion.7), channel_id=1, source_target_pairs={{0,16},{8,24},{16,0},{24,8},{1,17},{9,25},{17,1},{25,9},{2,18},{10... | collective-permute-start | bytes 3145736 | tf_op jit(solution)/shard_map/ppermute | solution.py:502
  834.0 51.4 %collective-permute-start.127 = (f32[688,1024]{1,0:T(8,128)}, f32[688,1024]{1,0:T(8,128)}, u32[]{:S(2)}, u32[]{:S(2)}) collective-permute-start(f32[688,1024]{1,0:T(8,128)} %add.912), channel_id=1, source_target_pairs={{0,8},{8,0},{16,24},{24,16},{1,9},{9,1},{17,25},{25,17},{2,10},{10... | collective-permute-start | bytes 8454152 | tf_op jit(solution)/shard_map/ppermute | solution.py:497
  856.2 35.4 %collective-permute-start.120 = (f32[1024,688]{0,1:T(8,128)}, f32[1024,688]{0,1:T(8,128)}, u32[]{:S(2)}, u32[]{:S(2)}) collective-permute-start(f32[1024,688]{0,1:T(8,128)} %add.910), channel_id=1, source_target_pairs={{0,8},{8,0},{16,24},{24,16},{1,9},{9,1},{17,25},{25,17},{2,10},{10... | collective-permute-start | bytes 8454152 | tf_op jit(solution)/shard_map/ppermute | solution.py:497
  856.2 35.3 %collective-permute-start.123 = (f32[1024,688]{0,1:T(8,128)}, f32[1024,688]{0,1:T(8,128)}, u32[]{:S(2)}, u32[]{:S(2)}) collective-permute-start(f32[1024,688]{0,1:T(8,128)} %add.911), channel_id=1, source_target_pairs={{0,8},{8,0},{16,24},{24,16},{1,9},{9,1},{17,25},{25,17},{2,10},{10... | collective-permute-start | bytes 8454152 | tf_op jit(solution)/shard_map/ppermute | solution.py:497
  856.7 50.0 %collective-permute-start.112 = (f32[1024,1028]{0,1:T(8,128)}, f32[1024,1028]{0,1:T(8,128)}, u32[]{:S(2)}, u32[]{:S(2)}) collective-permute-start(f32[1024,1028]{0,1:T(8,128)} %add.908), channel_id=1, source_target_pairs={{0,8},{8,0},{16,24},{24,16},{1,9},{9,1},{17,25},{25,17},{2,10},{10... | collective-permute-start | bytes 12632072 | tf_op jit(solution)/shard_map/ppermute | solution.py:497
  (204 other events, 3002.1 us)

commit v2 on v1

--- a/solution.py
+++ b/solution.py
@@ -578,15 +578,65 @@
     )
 
 
-def finish(part, core, axis):
-    total = part
-    for step in range(1, lax.axis_size("rows") // 2):
-        total = total + row_shift(part, step)
+def chips_along():
+    return lax.axis_size("rows") // 2
+
+
+def other_chips(value):
+    return [row_shift(value, step) for step in range(1, chips_along())]
+
+
+def place_body(own, other, *rest, axis, widths):
+    outs, sems = rest[:-1], rest[-1]
+    core = lax.axis_index("rows") % 2
+    size = own.shape[axis]
+    copies = []
+    at = 0
+    for i, (out, width) in enumerate(zip(outs, widths)):
+        for j, ref in enumerate((own, other)):
+            start = pl.multiple_of((core if j == 0 else 1 - core) * size, 128)
+            if axis == 0:
+                src, dst = ref.at[:, pl.ds(at, width)], out.at[pl.ds(start, size), :]
+            else:
+                src, dst = ref, out.at[:, pl.ds(start, size)]
+            copies.append(pltpu.make_async_copy(src, dst, sems.at[2 * i + j]))
+        at += width
+    for copy in copies:
+        copy.start()
+    for copy in copies:
+        copy.wait()
+
+
+def place(own, other, axis, widths):
+    rows, cols = own.shape
+    if axis == 0:
+        shapes = [(2 * rows, width) for width in widths]
+    else:
+        shapes = [(rows, 2 * cols)]
+    hbm = pl.BlockSpec(memory_space=pl.ANY)
+    out = pl.pallas_call(
+        functools.partial(place_body, axis=axis, widths=widths),
+        out_shape=[jax.ShapeDtypeStruct(shape, f32) for shape in shapes],
+        in_specs=[hbm, hbm],
+        out_specs=[hbm] * len(shapes),
+        scratch_shapes=[pltpu.SemaphoreType.DMA((2 * len(shapes),))],
+        name="place",
+    )(own, other)
+    return out
+
+
+def finish(total, axis, widths=None):
     other = swap(total, "rows", 1)
-    first = core == 0
-    return jnp.concatenate(
-        [jnp.where(first, total, other), jnp.where(first, other, total)], axis
-    )
+    widths = (total.shape[1],) if widths is None else widths
+    return place(total, other, axis, widths), other
+
+
+def row_products(lefts, rights):
+    total = None
+    for left, right in zip(lefts, rights):
+        part = left_product(left, both_cores(right))
+        total = part if total is None else total + part
+    return total
 
 
 def silu_parts(a):
@@ -642,7 +692,10 @@
 
     w_joined = jnp.concatenate([w_query, w_key, w_value, w_gate_attn, w_rate], axis=1)
     r1 = lax.rsqrt(jnp.mean(tokens * tokens, -1, keepdims=True) + epsilon)
-    normed = tokens * r1 * gain_one
+    unit = tokens * r1
+    unit_pair = tokens_half(unit, core)
+    unit_pairs = [unit_pair] + other_chips(unit_pair)
+    normed = unit * gain_one
     joined = product(normed, w_joined)
     gate_pre = joined[:, 3 * span : 4 * span]
     sig = jax.nn.sigmoid(joined[:, 4 * span :] + b_rate)
@@ -662,6 +715,8 @@
     shaped = centered * post_gain + post_shift
     gate_act, gate_slope = gelu_parts(gate_pre)
     gathered = gather_columns(gate_act * shaped)
+    gathered_pair = tokens_half(gathered, core)
+    gathered_pairs = [gathered_pair] + other_chips(gathered_pair)
     attn = product(gathered, w_out)
     stream_cols = lax.dynamic_slice_in_dim(tokens, column, slab, 1)
     hidden = stream_cols + attn
@@ -669,6 +724,8 @@
 
     r2 = lax.rsqrt(jnp.mean(whole * whole, -1, keepdims=True) + epsilon)
     hnorm = whole * r2 * gain_two
+    hnorm_pair = tokens_half(hnorm, core)
+    hnorm_pairs = [hnorm_pair] + other_chips(hnorm_pair)
     a = product(hnorm, w_gate)
     c = product(hnorm, w_up)
     act, slope = silu_parts(a)
@@ -689,13 +746,12 @@
     d_hidden = grad_output + d_part[:length]
     d_gain_two = d_part[length]
 
-    hnorm_pair = tokens_half(hnorm, core)
-    g_gate = finish(left_product(hnorm_pair, both_cores(da)), core, 0)
-    g_up = finish(left_product(hnorm_pair, both_cores(dc)), core, 0)
-    g_down = finish(left_product(both_cores(m), tokens_half(dy_full, core)), core, 1)
+    (g_gate,), _ = finish(row_products(hnorm_pairs, [da] + other_chips(da)), 0)
+    (g_up,), _ = finish(row_products(hnorm_pairs, [dc] + other_chips(dc)), 0)
+    g_down = left_product(both_cores(m), tokens_half(dy_full, core))
 
     d_gated = scatter_columns(right_product(d_hidden, w_out))
-    g_out = finish(left_product(tokens_half(gathered, core), both_cores(d_hidden)), core, 0)
+    (g_out,), _ = finish(row_products(gathered_pairs, [d_hidden] + other_chips(d_hidden)), 0)
     d_shaped = d_gated * gate_act
     d_gate_pre = d_gated * shaped * gate_slope
     d_post_gain = jnp.sum(d_shaped * centered, 0)
@@ -723,7 +779,17 @@
     d_part = scatter_columns(d_tokens, jnp.concatenate([d_gain_one, pad], 0))
     d_stream = d_hidden + d_part[:length]
     d_gain_one = d_part[length]
-    g_joined = finish(left_product(tokens_half(normed, core), both_cores(d_joined)), core, 0)
+    gain_half = half_of(gain_one, core, 0)
+    g_joined = row_products(
+        [pair * gain_half for pair in unit_pairs], [d_joined] + other_chips(d_joined)
+    )
+    (g_query, g_key, g_value, g_gate_attn), other = finish(g_joined, 0, (span,) * 4)
+    ends = (g_joined[:, 4 * span :], other[:, 4 * span :])
+    g_rate = jnp.where(
+        core == 0, jnp.concatenate(ends, 0), jnp.concatenate(ends[::-1], 0)
+    )
+    g_down = sum(other_chips(g_down), g_down)
+    (g_down,), _ = finish(g_down, 1)
 
     weights = valid_mask.reshape(-1).astype(f32)[:, None]
     stats = jnp.stack(
@@ -749,10 +815,10 @@
         output.reshape(1, length, slab),
         d_stream.reshape(1, length, slab),
         parts[0],
-        g_joined[:, :span],
-        g_joined[:, span : 2 * span],
-        g_joined[:, 2 * span : 3 * span],
-        g_joined[:, 4 * span :],
+        g_query,
+        g_key,
+        g_value,
+        g_rate,
         parts[1],
         parts[2].reshape(heads, hd, hd),
         parts[3].reshape(heads, hd),
@@ -760,7 +826,7 @@
         parts[5].reshape(heads, hd),
         parts[6],
         parts[7],
-        g_joined[:, 3 * span : 4 * span],
+        g_gate_attn,
         g_out,
         parts[8],
         g_gate,

time: 931 us -> 1930 us (2.07)
  Pallas kernels: 34.6 us -> 910 us
  waiting for transfers between devices: 473 us -> 551 us
  other arithmetic: 104 us -> 60.9 us
  local copies, waits for them, and re-layouts: 89.3 us -> 127 us
  matrix products: 126 us -> 155 us
  starting transfers between devices: 94.4 us -> 114 us
    pallas_call x0 -> x5, Pallas kernels: none -> 875 us  [place(): pl.pallas_call(functools.partial(place_body, axis=axis, widths=widths), o...]
    ppermute x5 -> x8, waiting for transfers between devices: 236 us -> 325 us  [row_shift(): lax.ppermute(value, 'rows', [(r, (r + 2 * step) % size) for r in range(si...]
    dot_general x5 -> x9, matrix products: 44.5 us -> 75.3 us  [left_product(): lax.dot_general(left, right, (((0,), (0,)), ((), ())), precision=lax.Prec...]
    unnamed x201 -> x253, local copies, waits for them, and re-layouts: 35.6 us -> 44.2 us
  transfers between devices with their start and end apart: 133 -> 140, of which waited for: 61 -> 63; matrix products, arithmetic and copies ran while one was open for 25% -> 14% of each run, Pallas kernels for 4% -> 34%
where the time goes in v2:
time: 1930 us; the launch traced here: 1920 us
  Pallas kernels  910 us (47%)
  waiting for transfers between devices  551 us (29%)
  matrix products  155 us (8%)
  local copies, waits for them, and re-layouts  127 us (7%)
  starting transfers between devices  114 us (6%)
  other arithmetic  60.9 us (3%)
    pallas_call x5, Pallas kernels, place(): pl.pallas_call(functools.partial(place_body, axis=axis, widths=widths), o...  875 us
    ppermute x8, waiting for transfers between devices, row_shift(): lax.ppermute(value, 'rows', [(r, (r + 2 * step) % size) for r in range(si...  325 us
    ppermute x98, waiting for transfers between devices, shift(): return lax.ppermute(value, 'heads', pairs)  196 us
    ppermute x98, starting transfers between devices, shift(): return lax.ppermute(value, 'heads', pairs)  83.9 us
    dot_general x9, matrix products, left_product(): lax.dot_general(left, right, (((0,), (0,)), ((), ())), precision=lax.Prec...  75.3 us
    dot_general x5, matrix products, right_product(): lax.dot_general(left, right, (((1,), (1,)), ((), ())), precision=lax.Prec...  47.4 us
    unnamed x253, local copies, waits for them, and re-layouts  44.2 us
  transfers between devices with their start and end apart: 140, of which 63 were waited for; matrix products, arithmetic and copies ran while one was open for 14% of the time, Pallas kernels for 34%

profile of v2, /device:TPU:0, one launch (start us, length us, event | category | flops | bytes accessed | tf_op | source)
XLA Modules:
  0.0 1922.9 jit_solution(1059344849136244789)
XLA Ops:
  38.2 12.1 fusion.23.joined
  55.2 12.8 inner_forward.1
  146.1 13.4 collective-permute-done.18
  224.0 17.8 fusion.90
  247.7 8.5 multiply_reduce_fusion.1
  430.2 21.8 %inner_backward.1 = (f32[512,256]{1,0:T(8,128)S(1)}, f32[512,256]{1,0:T(8,128)S(1)}, f32[512,256]{1,0:T(8,128)S(1)}, f32[4,512]{1,0:T(4,128)S(1)}, f32[256,128]{...) custom-call(f32[512,1028]{1,0:T(8,128)} %copy-done.2, ...), custom_call_target="tpu_custom_call" | custom-call | tf_op jit(solution)/shard_map/inner_backward/pallas_call | solution.py:407
  464.7 13.2 fusion.18
  502.2 8.6 fusion.11
  549.9 32.1 %collective-permute-done.133 = f32[688,1024]{1,0:T(8,128)} collective-permute-done((f32[688,1024]{1,0:T(8,128)}, f32[688,1024]{1,0:T(8,128)}, u32[]{:S(2)}, u32[]{:S(2)}) %collective-permute-start.133) | collective-permute-done | bytes 2818080 | tf_op jit(solution)/shard_map/ppermute | solution.py:502
  583.1 44.1 %collective-permute-done.112 = f32[512,1028]{0,1:T(8,128)} collective-permute-done((f32[512,1028]{0,1:T(8,128)}, f32[512,1028]{0,1:T(8,128)}, u32[]{:S(2)}, u32[]{:S(2)}) %collective-permute-start.112) | collective-permute-done | bytes 2105376 | tf_op jit(solution)/shard_map/ppermute | solution.py:502
  638.5 8.1 collective-permute-done.101
  661.4 8.7 fusion.33
  681.4 155.8 %collective-permute-done.128 = f32[512,688]{0,1:T(8,128)} collective-permute-done((f32[512,688]{0,1:T(8,128)}, f32[512,688]{0,1:T(8,128)}, u32[]{:S(2)}, u32[]{:S(2)}) %collective-permute-start.128) | collective-permute-done | bytes 1409056 | tf_op jit(solution)/shard_map/ppermute | solution.py:502
  840.5 10.0 fusion.7
  850.6 86.6 %collective-permute-done.118 = f32[512,256]{1,0:T(8,128)S(1)} collective-permute-done((f32[512,256]{1,0:T(8,128)S(1)}, f32[512,256]{1,0:T(8,128)S(1)}, u32[]{:S(2)}, u32[]{:S(2)}) %collective-permute-start.118) | collective-permute-done | bytes 524320 | tf_op jit(solution)/shard_map/ppermute | solution.py:502
  938.5 10.8 fusion.4
  950.5 8.4 fusion.50
  962.8 8.8 fusion.47
  975.3 9.9 collective-permute-done.107
  1014.1 64.6 %place.6 = f32[2048,256]{1,0:T(8,128)} custom-call(f32[1024,256]{1,0:T(8,128)} %convolution_add_fusion.1.own, f32[1024,256]{1,0:T(8,128)} %copy-done.66), custom_call_target="tpu_custom_call" | custom-call | tf_op jit(solution)/shard_map/place/pallas_call | solution.py:617
  1078.8 171.9 %place.9 = f32[688,2048]{1,0:T(8,128)} custom-call(f32[688,1024]{1,0:T(8,128)} %add.913.own, f32[688,1024]{1,0:T(8,128)} %collective-permute-done.134.other), custom_call_target="tpu_custom_call" | custom-call | tf_op jit(solution)/shard_map/place/pallas_call | solution.py:617
  1260.5 191.7 %place.7 = f32[2048,688]{1,0:T(8,128)} custom-call(f32[1024,688]{1,0:T(8,128)} %copy.151.own, f32[1024,688]{1,0:T(8,128)} %copy.152.other), custom_call_target="tpu_custom_call" | custom-call | tf_op jit(solution)/shard_map/place/pallas_call | solution.py:617
  1462.0 191.7 %place.8 = f32[2048,688]{1,0:T(8,128)} custom-call(f32[1024,688]{1,0:T(8,128)} %copy.153.own, f32[1024,688]{1,0:T(8,128)} %copy.154.other), custom_call_target="tpu_custom_call" | custom-call | tf_op jit(solution)/shard_map/place/pallas_call | solution.py:617
  1665.8 255.3 %place.5 = (f32[2048,256]{1,0:T(8,128)}, f32[2048,256]{1,0:T(8,128)}, f32[2048,256]{1,0:T(8,128)}, f32[2048,256]{1,0:T(8,128)}) custom-call(f32[1024,1028]{1,0:T(8,128)} %copy.149.own, f32[1024,1028]{1,0:T(8,128)} %copy.150.other), custom_call_target="tpu_custom_call" | custom-call | tf_op jit(solution)/shard_map/place/pallas_call | solution.py:617
  (745 shorter events, 551.7 us)
Async XLA Ops:
  2.7 84.4 %collective-permute-start.48 = (f32[256,256]{1,0:T(8,128)}, f32[256,256]{1,0:T(8,128)}, u32[]{:S(2)}, u32[]{:S(2)}) collective-permute-start(f32[256,256]{1,0:T(8,128)} %get-tuple-element.234), channel_id=1, source_target_pairs={{0,1},{1,0},{2,3},{3,2},{4,5},{5,4},{6,7},{7,6},{8,9},{9,8},{10,11... | collective-permute-start | bytes 786440 | tf_op jit(solution)/shard_map/ppermute | solution.py:493
  5.7 87.0 %collective-permute-start.50 = (f32[256,256]{1,0:T(8,128)}, f32[256,256]{1,0:T(8,128)}, u32[]{:S(2)}, u32[]{:S(2)}) collective-permute-start(f32[256,256]{1,0:T(8,128)} %get-tuple-element.234), channel_id=1, source_target_pairs={{0,2},{1,3},{2,4},{3,5},{4,6},{5,7},{6,0},{7,1},{8,10},{9,11},{10,... | collective-permute-start | bytes 786440 | tf_op jit(solution)/shard_map/ppermute | solution.py:493
  7.2 83.3 %collective-permute-start.49 = (f32[256,256]{1,0:T(8,128)}, f32[256,256]{1,0:T(8,128)}, u32[]{:S(2)}, u32[]{:S(2)}) collective-permute-start(f32[256,256]{1,0:T(8,128)} %get-tuple-element.233), channel_id=1, source_target_pairs={{0,1},{1,0},{2,3},{3,2},{4,5},{5,4},{6,7},{7,6},{8,9},{9,8},{10,11... | collective-permute-start | bytes 786440 | tf_op jit(solution)/shard_map/ppermute | solution.py:493
  7.8 86.6 %collective-permute-start.51 = (f32[256,256]{1,0:T(8,128)}, f32[256,256]{1,0:T(8,128)}, u32[]{:S(2)}, u32[]{:S(2)}) collective-permute-start(f32[256,256]{1,0:T(8,128)} %get-tuple-element.233), channel_id=1, source_target_pairs={{0,2},{1,3},{2,4},{3,5},{4,6},{5,7},{6,0},{7,1},{8,10},{9,11},{10,... | collective-permute-start | bytes 786440 | tf_op jit(solution)/shard_map/ppermute | solution.py:493
  415.7 66.0 %collective-permute-start.109 = (f32[512,1024]{1,0:T(8,128)}, f32[512,1024]{1,0:T(8,128)}, u32[]{:S(2)}, u32[]{:S(2)}) collective-permute-start(f32[512,1024]{1,0:T(8,128)} %get-tuple-element.162), channel_id=1, source_target_pairs={{0,8},{8,0},{16,24},{24,16},{1,9},{9,1},{17,25},{25,17},{2,10},{10... | collective-permute-start | bytes 6291464 | tf_op jit(solution)/shard_map/ppermute | solution.py:497
  415.7 74.1 %collective-permute-start.132 = (f32[512,1024]{1,0:T(8,128)}, f32[512,1024]{1,0:T(8,128)}, u32[]{:S(2)}, u32[]{:S(2)}) collective-permute-start(f32[512,1024]{1,0:T(8,128)} %get-tuple-element.156), channel_id=1, source_target_pairs={{0,8},{8,0},{16,24},{24,16},{1,9},{9,1},{17,25},{25,17},{2,10},{10... | collective-permute-start | bytes 6291464 | tf_op jit(solution)/shard_map/ppermute | solution.py:497
  416.3 94.6 %collective-permute-start.115 = (f32[512,1024]{1,0:T(8,128)}, f32[512,1024]{1,0:T(8,128)}, u32[]{:S(2)}, u32[]{:S(2)}) collective-permute-start(f32[512,1024]{1,0:T(8,128)} %get-tuple-element.160), channel_id=1, source_target_pairs={{0,8},{8,0},{16,24},{24,16},{1,9},{9,1},{17,25},{25,17},{2,10},{10... | collective-permute-start | bytes 6291464 | tf_op jit(solution)/shard_map/ppermute | solution.py:497
  416.4 78.5 %collective-permute-start.131 = (f32[512,688]{0,1:T(8,128)}, f32[512,688]{0,1:T(8,128)}, u32[]{:S(2)}, u32[]{:S(2)}) collective-permute-start(f32[512,688]{0,1:T(8,128)} %get-tuple-element.227), channel_id=1, source_target_pairs={{0,8},{8,0},{16,24},{24,16},{1,9},{9,1},{17,25},{25,17},{2,10},{10... | collective-permute-start | bytes 4227080 | tf_op jit(solution)/shard_map/ppermute | solution.py:497
  428.7 50.1 %collective-permute-start.135 = (f32[6]{0:T(128)}, f32[6]{0:T(128)}, u32[]{:S(2)}, u32[]{:S(2)}) collective-permute-start(f32[6]{0:T(128)} %stack.83), channel_id=1, source_target_pairs={{0,8},{8,0},{16,24},{24,16},{1,9},{9,1},{17,25},{25,17},{2,10},{10... | collective-permute-start | bytes 80 | tf_op jit(solution)/shard_map/ppermute | solution.py:497
  510.7 71.2 %collective-permute-start.133 = (f32[688,1024]{1,0:T(8,128)}, f32[688,1024]{1,0:T(8,128)}, u32[]{:S(2)}, u32[]{:S(2)}) collective-permute-start(f32[688,1024]{1,0:T(8,128)} %fusion.11), channel_id=1, source_target_pairs={{0,16},{8,24},{16,0},{24,8},{1,17},{9,25},{17,1},{25,9},{2,18},{10... | collective-permute-start | bytes 8454152 | tf_op jit(solution)/shard_map/ppermute | solution.py:502
  526.9 100.4 %collective-permute-start.112 = (f32[512,1028]{0,1:T(8,128)}, f32[512,1028]{0,1:T(8,128)}, u32[]{:S(2)}, u32[]{:S(2)}) collective-permute-start(f32[512,1028]{0,1:T(8,128)} %copy.146), channel_id=1, source_target_pairs={{0,16},{8,24},{16,0},{24,8},{1,17},{9,25},{17,1},{25,9},{2,18},{10... | collective-permute-start | bytes 6316040 | tf_op jit(solution)/shard_map/ppermute | solution.py:502
  533.4 303.8 %collective-permute-start.111 = (f32[1024,1024]{1,0:T(8,128)}, f32[1024,1024]{1,0:T(8,128)}, u32[]{:S(2)}, u32[]{:S(2)}) collective-permute-start(f32[1024,1024]{1,0:T(8,128)} %pad_maximum_fusion), channel_id=1, source_target_pairs={{0,16},{8,24},{16,0},{24,8},{1,17},{9,25},{17,1},{25,9},{2,18},{10... | collective-permute-start | bytes 12582920 | tf_op jit(solution)/shard_map/ppermute | solution.py:502
  541.7 128.3 %collective-permute-start.110 = (f32[512,1028]{0,1:T(8,128)S(1)}, f32[512,1028]{0,1:T(8,128)S(1)}, u32[]{:S(2)}, u32[]{:S(2)}) collective-permute-start(f32[512,1028]{0,1:T(8,128)S(1)} %copy-done.52), channel_id=1, source_target_pairs={{0,8},{8,0},{16,24},{24,16},{1,9},{9,1},{17,25},{25,17},{2,10},{10... | collective-permute-start | bytes 6316040 | tf_op jit(solution)/shard_map/ppermute | solution.py:497
  546.2 404.3 %collective-permute-start.123 = (f32[1024,1024]{1,0:T(8,128)}, f32[1024,1024]{1,0:T(8,128)}, u32[]{:S(2)}, u32[]{:S(2)}) collective-permute-start(f32[1024,1024]{1,0:T(8,128)} %pad_maximum_fusion.2), channel_id=1, source_target_pairs={{0,16},{8,24},{16,0},{24,8},{1,17},{9,25},{17,1},{25,9},{2,18},{10... | collective-permute-start | bytes 12582920 | tf_op jit(solution)/shard_map/ppermute | solution.py:502
  627.2 212.1 %collective-permute-start.113 = (f32[512,1028]{0,1:T(8,128)}, f32[512,1028]{0,1:T(8,128)}, u32[]{:S(2)}, u32[]{:S(2)}) collective-permute-start(f32[512,1028]{0,1:T(8,128)} %collective-permute-done.112), channel_id=1, source_target_pairs={{0,8},{8,0},{16,24},{24,16},{1,9},{9,1},{17,25},{25,17},{2,10},{10... | collective-permute-start | bytes 6316040 | tf_op jit(solution)/shard_map/ppermute | solution.py:497
  646.6 190.6 %collective-permute-start.128 = (f32[512,688]{0,1:T(8,128)}, f32[512,688]{0,1:T(8,128)}, u32[]{:S(2)}, u32[]{:S(2)}) collective-permute-start(f32[512,688]{0,1:T(8,128)} %get-tuple-element.225), channel_id=1, source_target_pairs={{0,16},{8,24},{16,0},{24,8},{1,17},{9,25},{17,1},{25,9},{2,18},{10... | collective-permute-start | bytes 4227080 | tf_op jit(solution)/shard_map/ppermute | solution.py:502
  670.0 305.1 %collective-permute-start.117 = (f32[1024,1024]{1,0:T(8,128)}, f32[1024,1024]{1,0:T(8,128)}, u32[]{:S(2)}, u32[]{:S(2)}) collective-permute-start(f32[1024,1024]{1,0:T(8,128)} %pad_maximum_fusion.1), channel_id=1, source_target_pairs={{0,16},{8,24},{16,0},{24,8},{1,17},{9,25},{17,1},{25,9},{2,18},{10... | collective-permute-start | bytes 12582920 | tf_op jit(solution)/shard_map/ppermute | solution.py:502
  837.2 112.4 %collective-permute-start.125 = (f32[512,688]{0,1:T(8,128)}, f32[512,688]{0,1:T(8,128)S(1)}, u32[]{:S(2)}, u32[]{:S(2)}) collective-permute-start(f32[512,688]{0,1:T(8,128)} %copy-done.58), channel_id=1, source_target_pairs={{0,8},{8,0},{16,24},{24,16},{1,9},{9,1},{17,25},{25,17},{2,10},{10... | collective-permute-start | bytes 4227080 | tf_op jit(solution)/shard_map/ppermute | solution.py:497
  837.2 100.0 %collective-permute-start.118 = (f32[512,256]{1,0:T(8,128)S(1)}, f32[512,256]{1,0:T(8,128)S(1)}, u32[]{:S(2)}, u32[]{:S(2)}) collective-permute-start(f32[512,256]{1,0:T(8,128)S(1)} %copy-done.38), channel_id=1, source_target_pairs={{0,16},{8,24},{16,0},{24,8},{1,17},{9,25},{17,1},{25,9},{2,18},{10... | collective-permute-start | bytes 1572872 | tf_op jit(solution)/shard_map/ppermute | solution.py:502
  839.3 97.9 %collective-permute-start.104 = (f32[264,256]{1,0:T(8,128)S(1)}, f32[264,256]{1,0:T(8,128)S(1)}, u32[]{:S(2)}, u32[]{:S(2)}) collective-permute-start(f32[264,256]{1,0:T(8,128)S(1)} %copy-done.78), channel_id=1, source_target_pairs={{0,1},{1,0},{2,3},{3,2},{4,5},{5,4},{6,7},{7,6},{8,9},{9,8},{10,11... | collective-permute-start | bytes 811016 | tf_op jit(solution)/shard_map/ppermute | solution.py:493
  949.3 710.7 %collective-permute-start.114 = (f32[1024,1028]{0,1:T(8,128)}, f32[1024,1028]{0,1:T(8,128)}, u32[]{:S(2)}, u32[]{:S(2)}) collective-permute-start(f32[1024,1028]{0,1:T(8,128)} %fusion.4), channel_id=1, source_target_pairs={{0,8},{8,0},{16,24},{24,16},{1,9},{9,1},{17,25},{25,17},{2,10},{10... | collective-permute-start | bytes 12632072 | tf_op jit(solution)/shard_map/ppermute | solution.py:497
  971.6 107.2 %collective-permute-start.134 = (f32[688,1024]{1,0:T(8,128)}, f32[688,1024]{1,0:T(8,128)}, u32[]{:S(2)}, u32[]{:S(2)}) collective-permute-start(f32[688,1024]{1,0:T(8,128)} %add.913.own), channel_id=1, source_target_pairs={{0,8},{8,0},{16,24},{24,16},{1,9},{9,1},{17,25},{25,17},{2,10},{10... | collective-permute-start | bytes 8454152 | tf_op jit(solution)/shard_map/ppermute | solution.py:497
  971.7 285.4 %collective-permute-start.126 = (f32[1024,688]{0,1:T(8,128)}, f32[1024,688]{0,1:T(8,128)}, u32[]{:S(2)}, u32[]{:S(2)}) collective-permute-start(f32[1024,688]{0,1:T(8,128)} %fusion.50), channel_id=1, source_target_pairs={{0,8},{8,0},{16,24},{24,16},{1,9},{9,1},{17,25},{25,17},{2,10},{10... | collective-permute-start | bytes 8454152 | tf_op jit(solution)/shard_map/ppermute | solution.py:497
  972.2 486.4 %collective-permute-start.130 = (f32[1024,688]{0,1:T(8,128)}, f32[1024,688]{0,1:T(8,128)}, u32[]{:S(2)}, u32[]{:S(2)}) collective-permute-start(f32[1024,688]{0,1:T(8,128)} %fusion.47), channel_id=1, source_target_pairs={{0,8},{8,0},{16,24},{24,16},{1,9},{9,1},{17,25},{25,17},{2,10},{10... | collective-permute-start | bytes 8454152 | tf_op jit(solution)/shard_map/ppermute | solution.py:497
  (238 other events, 5718.9 us)

commit v3 on v2

--- a/solution.py
+++ b/solution.py
@@ -517,7 +517,7 @@
     return butterfly(jnp.where(place, value[None], 0.0), "heads")
 
 
-def gather_columns(value, parts=2):
+def gather_columns(value, hooks=(), parts=2):
     deep, across = heads_grid()
     z, x = heads_place()
     rows, cols = value.shape
@@ -527,6 +527,8 @@
     for dz in range(deep):
         if dz:
             moving = [shift(item, 1, 0) for item in moving]
+            if dz <= len(hooks):
+                moving[0] = hooks[dz - 1](moving[0])
         side = moving
         for dx in range(across):
             if dx:
@@ -537,7 +539,7 @@
     return out
 
 
-def scatter_columns(value, extra=None, parts=2):
+def scatter_columns(value, extra=None, hooks=(), parts=2):
     deep, across = heads_grid()
     z, x = heads_place()
     rows, width = value.shape
@@ -553,7 +555,9 @@
         return block
 
     total = [None] * parts
-    for dz in list(range(1, deep)) + [0]:
+    for turn, dz in enumerate(list(range(1, deep)) + [0]):
+        if 1 <= turn <= len(hooks):
+            total[0] = hooks[turn - 1](total[0])
         for i in range(parts):
             here = None
             for dx in list(range(1, across)) + [0]:
@@ -586,57 +590,76 @@
     return [row_shift(value, step) for step in range(1, chips_along())]
 
 
-def place_body(own, other, *rest, axis, widths):
-    outs, sems = rest[:-1], rest[-1]
-    core = lax.axis_index("rows") % 2
-    size = own.shape[axis]
-    copies = []
+def place_body(core, own, other, *outs, axis, widths):
+    first = core[0] == 0
     at = 0
-    for i, (out, width) in enumerate(zip(outs, widths)):
-        for j, ref in enumerate((own, other)):
-            start = pl.multiple_of((core if j == 0 else 1 - core) * size, 128)
-            if axis == 0:
-                src, dst = ref.at[:, pl.ds(at, width)], out.at[pl.ds(start, size), :]
-            else:
-                src, dst = ref, out.at[:, pl.ds(start, size)]
-            copies.append(pltpu.make_async_copy(src, dst, sems.at[2 * i + j]))
+    for out, width in zip(outs, widths):
+        mine, its = (own[:, at : at + width], other[:, at : at + width]) if axis == 0 else (own[...], other[...])
+        low = jnp.where(first, mine, its)
+        high = jnp.where(first, its, mine)
+        if axis == 0:
+            out[0] = low
+            out[1] = high
+        else:
+            out[:, : low.shape[1]] = low
+            out[:, low.shape[1] :] = high
         at += width
-    for copy in copies:
-        copy.start()
-    for copy in copies:
-        copy.wait()
-
-
-def place(own, other, axis, widths):
+
+
+def place(own, other, core, axis, widths):
     rows, cols = own.shape
+    steps = max(n for n in (1, 2, 4) if rows % (8 * n) == 0)
+    size = rows // steps
+    part = pl.BlockSpec((size, cols), lambda i: (i, 0))
     if axis == 0:
-        shapes = [(2 * rows, width) for width in widths]
+        shapes = [(2, rows, width) for width in widths]
+        specs = [pl.BlockSpec((2, size, width), lambda i: (0, i, 0)) for width in widths]
     else:
         shapes = [(rows, 2 * cols)]
-    hbm = pl.BlockSpec(memory_space=pl.ANY)
+        specs = [pl.BlockSpec((size, 2 * cols), lambda i: (i, 0))]
     out = pl.pallas_call(
         functools.partial(place_body, axis=axis, widths=widths),
+        grid=(steps,),
         out_shape=[jax.ShapeDtypeStruct(shape, f32) for shape in shapes],
-        in_specs=[hbm, hbm],
-        out_specs=[hbm] * len(shapes),
-        scratch_shapes=[pltpu.SemaphoreType.DMA((2 * len(shapes),))],
+        in_specs=[pl.BlockSpec(memory_space=pltpu.SMEM), part, part],
+        out_specs=specs,
+        compiler_params=pltpu.CompilerParams(vmem_limit_bytes=48 << 20),
         name="place",
-    )(own, other)
-    return out
-
-
-def finish(total, axis, widths=None):
-    other = swap(total, "rows", 1)
+    )(core.reshape(1).astype(jnp.int32), own, other)
+    return [o.reshape(2 * rows, -1) if axis == 0 else o for o in out]
+
+
+def finish(total, core, axis, widths=None):
     widths = (total.shape[1],) if widths is None else widths
-    return place(total, other, axis, widths), other
+    return place(total, swap(total, "rows", 1), core, axis, widths)
 
 
 def row_products(lefts, rights):
     total = None
     for left, right in zip(lefts, rights):
-        part = left_product(left, both_cores(right))
+        part = left_product(left, right)
         total = part if total is None else total + part
     return total
+
+
+class Along:
+    def __init__(self, value, parts=4):
+        size = value.shape[0] // parts
+        self.own = value
+        self.pieces = [
+            [row_shift(value[i * size : (i + 1) * size], step) for i in range(parts)]
+            for step in range(1, chips_along())
+        ]
+
+    def tie(self, i, main):
+        for step in self.pieces:
+            main, step[i] = lax.optimization_barrier((main, step[i]))
+        return main
+
+    def all(self):
+        return [self.own] + [
+            step[0] if len(step) == 1 else jnp.concatenate(step, 0) for step in self.pieces
+        ]
 
 
 def silu_parts(a):
@@ -690,17 +713,21 @@
     grad_output = cotangent.reshape(length, slab)
     dy_full = gather_columns(grad_output)
 
-    w_joined = jnp.concatenate([w_query, w_key, w_value, w_gate_attn, w_rate], axis=1)
+    w_joined = jnp.concatenate([w_query, w_key, w_value, w_gate_attn], axis=1)
     r1 = lax.rsqrt(jnp.mean(tokens * tokens, -1, keepdims=True) + epsilon)
     unit = tokens * r1
-    unit_pair = tokens_half(unit, core)
-    unit_pairs = [unit_pair] + other_chips(unit_pair)
+    unit_y = Along(tokens_half(unit, core))
     normed = unit * gain_one
     joined = product(normed, w_joined)
-    gate_pre = joined[:, 3 * span : 4 * span]
-    sig = jax.nn.sigmoid(joined[:, 4 * span :] + b_rate)
-    rate = sig / hd
-    rate_t = rate.T
+    rate_pre = lax.dot_general(
+        w_rate, normed, (((0,), (1,)), ((), ())), precision=lax.Precision.HIGH,
+        preferred_element_type=f32,
+    )
+    joined = unit_y.tie(0, joined)
+    gate_pre = joined[:, 3 * span :]
+    sig = jax.nn.sigmoid(rate_pre + b_rate[:, None])
+    rate_t = sig / hd
+    rate = rate_t.T
     seg = jnp.cumsum(doc_starts.reshape(length)).astype(f32)
     seg, seg_t = seg[:, None], seg[None]
     w0, b0 = state_in(inner_weight, inner_bias)
@@ -708,33 +735,38 @@
     mixed, *saved = ttt_forward(
         joined, rate, rate_t, seg, seg_t, w0, b0, gain_col, shift_col, hd, heads
     )
+    mixed = unit_y.tie(1, mixed)
     row_sums = butterfly(jnp.stack([jnp.sum(mixed, 1), jnp.sum(mixed * mixed, 1)]), "heads")
     row_mean = row_sums[0] / total_span
     inv_std = lax.rsqrt(row_sums[1] / total_span - row_mean * row_mean + epsilon)[:, None]
     centered = (mixed - row_mean[:, None]) * inv_std
     shaped = centered * post_gain + post_shift
     gate_act, gate_slope = gelu_parts(gate_pre)
-    gathered = gather_columns(gate_act * shaped)
-    gathered_pair = tokens_half(gathered, core)
-    gathered_pairs = [gathered_pair] + other_chips(gathered_pair)
+    gathered = gather_columns(
+        gate_act * shaped,
+        [functools.partial(unit_y.tie, 2), functools.partial(unit_y.tie, 3)],
+    )
+    gathered_y = Along(tokens_half(gathered, core))
     attn = product(gathered, w_out)
     stream_cols = lax.dynamic_slice_in_dim(tokens, column, slab, 1)
     hidden = stream_cols + attn
-    whole = gather_columns(hidden)
+    whole = gather_columns(
+        hidden, [lambda v: v, functools.partial(gathered_y.tie, 0)],
+    )
 
     r2 = lax.rsqrt(jnp.mean(whole * whole, -1, keepdims=True) + epsilon)
     hnorm = whole * r2 * gain_two
-    hnorm_pair = tokens_half(hnorm, core)
-    hnorm_pairs = [hnorm_pair] + other_chips(hnorm_pair)
+    hnorm_y = Along(tokens_half(hnorm, core))
     a = product(hnorm, w_gate)
+    a = gathered_y.tie(1, a)
     c = product(hnorm, w_up)
     act, slope = silu_parts(a)
     m = act * c
-    ffn = scatter_columns(product(m, w_down))
-    output = hidden + ffn
+    ffn_part = gathered_y.tie(2, product(m, w_down))
     dm = right_product(dy_full, w_down)
     da = dm * c * slope
     dc = dm * act
+    da_y, dc_y = Along(da, 1), Along(dc, 1)
     dhnorm = right_product(da, w_gate) + right_product(dc, w_up)
     d_gain_two = jnp.sum(dhnorm * whole * r2, 0, keepdims=True)
     weighted = dhnorm * gain_two
@@ -742,16 +774,31 @@
         whole * weighted, -1, keepdims=True
     )
     pad = jnp.zeros((7, width), f32)
-    d_part = scatter_columns(d_whole, jnp.concatenate([d_gain_two, pad], 0))
+    d_part = scatter_columns(
+        d_whole,
+        jnp.concatenate([d_gain_two, pad], 0),
+        [
+            functools.partial(gathered_y.tie, 3),
+            functools.partial(hnorm_y.tie, 0),
+            functools.partial(hnorm_y.tie, 1),
+        ],
+    )
     d_hidden = grad_output + d_part[:length]
     d_gain_two = d_part[length]
-
-    (g_gate,), _ = finish(row_products(hnorm_pairs, [da] + other_chips(da)), 0)
-    (g_up,), _ = finish(row_products(hnorm_pairs, [dc] + other_chips(dc)), 0)
+    d_hidden_y = Along(d_hidden, 1)
     g_down = left_product(both_cores(m), tokens_half(dy_full, core))
 
-    d_gated = scatter_columns(right_product(d_hidden, w_out))
-    (g_out,), _ = finish(row_products(gathered_pairs, [d_hidden] + other_chips(d_hidden)), 0)
+    d_gated = scatter_columns(
+        right_product(d_hidden, w_out),
+        None,
+        [
+            functools.partial(hnorm_y.tie, 2),
+            functools.partial(hnorm_y.tie, 3),
+            functools.partial(da_y.tie, 0),
+        ],
+    )
+    ffn = scatter_columns(ffn_part)
+    output = hidden + ffn
     d_shaped = d_gated * gate_act
     d_gate_pre = d_gated * shaped * gate_slope
     d_post_gain = jnp.sum(d_shaped * centered, 0)
@@ -767,10 +814,15 @@
     dq, dk, dv, d_rate, dw, db, dg, dsh = ttt_backward(
         joined, rate_t, seg, seg_t, w0, b0, gain_col, shift_col, saved, d_mixed, hd, heads
     )
+    dq = d_hidden_y.tie(0, dc_y.tie(0, dq))
     d_inner_weight, d_inner_bias = state_back(dw, db, heads, hd)
-    d_rate_pre = d_rate.T * rate * (1.0 - sig)
-    d_joined = jnp.concatenate([dq, dk, dv, d_gate_pre, d_rate_pre], 1)
-    d_normed = right_product(d_joined, w_joined)
+    d_rate_pre = d_rate * rate_t * (1.0 - sig)
+    d_joined = jnp.concatenate([dq, dk, dv, d_gate_pre], 1)
+    d_joined_y, d_rate_y = Along(d_joined, 1), Along(d_rate_pre, 1)
+    d_normed = right_product(d_joined, w_joined) + lax.dot_general(
+        d_rate_pre, w_rate, (((0,), (1,)), ((), ())), precision=lax.Precision.HIGH,
+        preferred_element_type=f32,
+    )
     d_gain_one = jnp.sum(d_normed * tokens * r1, 0, keepdims=True)
     weighted = d_normed * gain_one
     d_tokens = r1 * weighted - tokens * (r1 * r1 * r1) * jnp.mean(
@@ -779,17 +831,25 @@
     d_part = scatter_columns(d_tokens, jnp.concatenate([d_gain_one, pad], 0))
     d_stream = d_hidden + d_part[:length]
     d_gain_one = d_part[length]
+
+    def cores(values):
+        return [both_cores(value) for value in values]
+
+    (g_gate,) = finish(row_products(cores(da_y.all()), hnorm_y.all()), core, 1)
+    (g_up,) = finish(row_products(cores(dc_y.all()), hnorm_y.all()), core, 1)
+    (g_out,) = finish(row_products(gathered_y.all(), cores(d_hidden_y.all())), core, 0)
+    (g_down,) = finish(sum(other_chips(g_down), g_down), core, 1)
     gain_half = half_of(gain_one, core, 0)
-    g_joined = row_products(
-        [pair * gain_half for pair in unit_pairs], [d_joined] + other_chips(d_joined)
-    )
-    (g_query, g_key, g_value, g_gate_attn), other = finish(g_joined, 0, (span,) * 4)
-    ends = (g_joined[:, 4 * span :], other[:, 4 * span :])
-    g_rate = jnp.where(
-        core == 0, jnp.concatenate(ends, 0), jnp.concatenate(ends[::-1], 0)
-    )
-    g_down = sum(other_chips(g_down), g_down)
-    (g_down,), _ = finish(g_down, 1)
+    normed_pairs = [pair * gain_half for pair in unit_y.all()]
+    g_query, g_key, g_value, g_gate_attn = finish(
+        row_products(normed_pairs, cores(d_joined_y.all())), core, 0, (span,) * 4
+    )
+    g_rate = None
+    for pair, d in zip(normed_pairs, d_rate_y.all()):
+        part = product(jnp.concatenate([d, swap(d, "rows", 1)], 1), pair)
+        g_rate = part if g_rate is None else g_rate + part
+    ends = (g_rate, swap(g_rate, "rows", 1))
+    g_rate = jnp.where(core == 0, jnp.concatenate(ends, 1), jnp.concatenate(ends[::-1], 1))
 
     weights = valid_mask.reshape(-1).astype(f32)[:, None]
     stats = jnp.stack(
@@ -802,7 +862,7 @@
     stats = butterfly(butterfly(stats, "rows"), "heads")
     rms_values = jnp.sqrt(stats[:5] / (stats[5] * width))
     small = [
-        d_gain_one, jnp.sum(d_rate_pre, 0), d_inner_weight, d_inner_bias, dg, dsh,
+        d_gain_one, jnp.sum(d_rate_pre, 1), d_inner_weight, d_inner_bias, dg, dsh,
         d_post_gain, d_post_shift, d_gain_two,
     ]
     packed = butterfly(jnp.concatenate([item.reshape(-1) for item in small]), "rows")
@@ -818,7 +878,7 @@
         g_query,
         g_key,
         g_value,
-        g_rate,
+        g_rate.T,
         parts[1],
         parts[2].reshape(heads, hd, hd),
         parts[3].reshape(heads, hd),
@@ -829,8 +889,8 @@
         g_gate_attn,
         g_out,
         parts[8],
-        g_gate,
-        g_up,
+        g_gate.T,
+        g_up.T,
         g_down,
         rms_values,
     )

time: 1930 us -> 842 us (0.44)
  Pallas kernels: 910 us -> 58.8 us
  waiting for transfers between devices: 551 us -> 362 us
  local copies, waits for them, and re-layouts: 127 us -> 73.4 us
  starting transfers between devices: 114 us -> 146 us
  other arithmetic: 60.9 us -> 39.5 us
    pallas_call x5, Pallas kernels: 875 us -> 24.2 us  [place(): pl.pallas_call(functools.partial(place_body, axis=axis, widths=widths), g...]
    ppermute x8 -> x18, waiting for transfers between devices: 325 us -> 113 us  [row_shift(): lax.ppermute(value, 'rows', [(r, (r + 2 * step) % size) for r in range(si...]
    unnamed x253 -> x235, local copies, waits for them, and re-layouts: 44.2 us -> 12.6 us
    ppermute x34 -> x37, waiting for transfers between devices: 29.7 us -> 49.4 us  [swap(): lax.ppermute(value, axis, [(i, i ^ bit) for i in range(lax.axis_size(axis...]
  transfers between devices with their start and end apart: 140 -> 153, of which waited for: 63 -> 71; matrix products, arithmetic and copies ran while one was open for 14% -> 31% of each run, Pallas kernels for 34% -> 6%
where the time goes in v3:
time: 842 us; the launch traced here: 832 us
  waiting for transfers between devices  362 us (43%)
  matrix products  149 us (18%)
  starting transfers between devices  146 us (17%)
  local copies, waits for them, and re-layouts  73.4 us (9%)
  Pallas kernels  58.8 us (7%)
  other arithmetic  39.5 us (5%)
    ppermute x98, waiting for transfers between devices, shift(): return lax.ppermute(value, 'heads', pairs)  199 us
    ppermute x18, waiting for transfers between devices, row_shift(): lax.ppermute(value, 'rows', [(r, (r + 2 * step) % size) for r in range(si...  113 us
    ppermute x98, starting transfers between devices, shift(): return lax.ppermute(value, 'heads', pairs)  101 us
    dot_general x9, matrix products, left_product(): lax.dot_general(left, right, (((0,), (0,)), ((), ())), precision=lax.Prec...  66.7 us
    ppermute x37, waiting for transfers between devices, swap(): lax.ppermute(value, axis, [(i, i ^ bit) for i in range(lax.axis_size(axis...  49.4 us
    dot_general x7, matrix products, product(): jnp.dot(left, right, precision=lax.Precision.HIGH, preferred_element_type...  38.5 us
    dot_general x5, matrix products, right_product(): lax.dot_general(left, right, (((1,), (1,)), ((), ())), precision=lax.Prec...  38.5 us
    pallas_call x5, Pallas kernels, place(): pl.pallas_call(functools.partial(place_body, axis=axis, widths=widths), g...  24.2 us
  transfers between devices with their start and end apart: 153, of which 71 were waited for; matrix products, arithmetic and copies ran while one was open for 31% of the time, Pallas kernels for 6%

profile of v3, /device:TPU:0, one launch (start us, length us, event | category | flops | bytes accessed | tf_op | source)
XLA Modules:
  0.0 832.3 jit_solution(5472984862530330557)
XLA Ops:
  44.2 12.5 %fusion.38.joined = f32[512,1024]{1,0:T(8,128)} fusion(f32[2048,1024]{1,0:T(8,128)} %constant_dynamic-update-slice_fusion.24, f32[512,2048]{1,0:T(8,128)} %bitcast_multiply_fusion.3, f32[2048]{0:T(1024)S(1)} %bitcast.136), kind=kOutput, calls=%fused_computation.51 | convolution fusion | flops 6443499520 | bytes 14688256 | tf_op jit(solution)/shard_map/dot_general | solution.py:458
  83.6 12.8 %inner_forward.1 = (f32[512,256]{1,0:T(8,128)S(1)}, f32[256,512]{1,0:T(8,128)S(1)}, f32[256,512]{1,0:T(8,128)S(1)}, f32[4,256,128]{2,1,0:T(8,128)S(1)}, f32[4,256,1]{2,1,0:T(8,128)S(1)}) custom-call(f32[512,1024]{1,0:T(8,128)S(1)} %copy-done.2, f32[512,4]{1,0:T(8,128)S(1)} %copy-done.3, f32[4,512]{1,0:T(4,128)S(1)} %get-tuple-element.261.rate_t, ...), custom_call_target="tpu_custom_call" | custom-call | tf_op jit(solution)/shard_map/inner_forward/pallas_call | solution.py:182
  143.3 11.8 %collective-permute-done.17 = f32[256,1024]{1,0:T(8,128)S(1)} collective-permute-done((f32[256,1024]{1,0:T(8,128)S(1)}, f32[256,1024]{1,0:T(8,128)S(1)}, u32[]{:S(2)}, u32[]{:S(2)}) %collective-permute-start.17) | collective-permute-done | bytes 1048608 | tf_op jit(solution)/shard_map/ppermute | solution.py:502
  158.6 7.4 collective-permute-done.21
  201.2 8.9 %collective-permute-done.33 = f32[256,256]{1,0:T(8,128)S(1)} collective-permute-done((f32[256,256]{1,0:T(8,128)S(1)}, f32[256,256]{1,0:T(8,128)S(1)}, u32[]{:S(2)}, u32[]{:S(2)}) %collective-permute-start.33) | collective-permute-done | bytes 262176 | tf_op jit(solution)/shard_map/ppermute | solution.py:493
  223.3 9.6 %collective-permute-done.38 = f32[256,256]{1,0:T(8,128)S(1)} collective-permute-done((f32[256,256]{1,0:T(8,128)S(1)}, f32[256,256]{1,0:T(8,128)S(1)}, u32[]{:S(2)}, u32[]{:S(2)}) %collective-permute-start.38) | collective-permute-done | bytes 262176 | tf_op jit(solution)/shard_map/ppermute | solution.py:493
  248.6 9.7 %fusion.125 = (f32[512,688]{0,1:T(8,128)S(1)}, f32[512,688]{0,1:T(8,128)}, f32[512,688]{0,1:T(8,128)}) fusion(f32[512,688]{0,1:T(8,128)} %fusion.167, f32[512,688]{0,1:T(8,128)} %fusion.168, f32[512,2048]{1,0:T(8,128)} %constant_dynamic-update-slice_fusion.32, f32[688,2048]{1,0:T(8,128)S(1)} %bitcast.129), kind=kOutput, calls=%fused_computation.187 | convolution fusion | flops 4332748800 | bytes 16875520 | tf_op jit(solution)/shard_map/dot_general | solution.py:469
  258.2 8.9 %fusion.170 = f32[512,2048]{1,0:T(8,128)} fusion(f32[512,688]{0,1:T(8,128)} %get-tuple-element.211, f32[2048,688]{0,1:T(8,128)S(1)} %bitcast.127), kind=kOutput, calls=%fused_computation.402 | convolution fusion | flops 4328521728 | bytes 11239424 | tf_op jit(solution)/shard_map/dot_general | solution.py:469
  267.1 8.4 %multiply_reduce_fusion.1 = (f32[512]{0:T(512)S(1)}, f32[2048]{0:T(1024)S(1)}, f32[512,2048]{1,0:T(8,128)S(1)}) fusion(f32[512,2048]{1,0:T(8,128)S(1)} %constant_dynamic-update-slice_fusion.40, f32[2048]{0:T(1024)S(1)} %bitcast.142, f32[512]{0:T(512)S(1)} %get-tuple-element.270, f32[512,2048]{1,0:T(8,128)} %fusion.170, ...), kind=kOutput, calls=%fused_computation.46 | convolution fusion | flops 4335859200 | bytes 19648512 | tf_op jit(solution)/shard_map/dot_general | solution.py:469
  289.9 14.5 %collective-permute-done.72 = f32[256,1024]{1,0:T(8,128)} collective-permute-done((f32[256,1024]{1,0:T(8,128)S(1)}, f32[256,1024]{1,0:T(8,128)}, u32[]{:S(2)}, u32[]{:S(2)}) %collective-permute-start.72) | collective-permute-done | bytes 1048608 | tf_op jit(solution)/shard_map/ppermute | solution.py:502
  304.4 9.1 %collective-permute-done.73 = f32[256,256]{1,0:T(8,128)S(1)} collective-permute-done((f32[256,256]{1,0:T(8,128)S(1)}, f32[256,256]{1,0:T(8,128)S(1)}, u32[]{:S(2)}, u32[]{:S(2)}) %collective-permute-start.73) | collective-permute-done | bytes 262176 | tf_op jit(solution)/shard_map/ppermute | solution.py:493
  314.5 7.3 collective-permute-done.76
  336.0 7.2 collective-permute-done.81
  356.8 7.7 collective-permute-done.84
  418.5 20.5 %collective-permute-done.42 = f32[256,1024]{1,0:T(8,128)S(1)} collective-permute-done((f32[256,1024]{1,0:T(8,128)S(1)}, f32[256,1024]{1,0:T(8,128)S(1)}, u32[]{:S(2)}, u32[]{:S(2)}) %collective-permute-start.42) | collective-permute-done | bytes 1048608 | tf_op jit(solution)/shard_map/ppermute | solution.py:502
  483.4 8.8 %fusion.26 = f32[688,1024]{1,0:T(8,128)} fusion(f32[512,1024]{1,0:T(8,128)} %collective-permute-done.145, f32[512,1024]{1,0:T(8,128)S(1)} %copy-done.53, f32[512,688]{0,1:T(8,128)} %collective-permute-done.144, f32[512,688]{0,1:T(8,128)} %get-tuple-element.212), kind=kOutput, calls=%fused_computation.29 | convolution fusion | flops 4330274816 | bytes 9830400 | tf_op jit(solution)/shard_map/dot_general | solution.py:462
  518.0 21.8 %inner_backward.1 = (f32[512,256]{1,0:T(8,128)S(1)}, f32[512,256]{1,0:T(8,128)S(1)}, f32[512,256]{1,0:T(8,128)S(1)}, f32[4,512]{1,0:T(4,128)S(1)}, f32[256,128]{...) custom-call(f32[512,1024]{1,0:T(8,128)} %fusion.38.joined, ...), custom_call_target="tpu_custom_call" | custom-call | tf_op jit(solution)/shard_map/inner_backward/pallas_call | solution.py:407
  539.9 54.6 %collective-permute-done.110 = f32[512,256]{1,0:T(8,128)} collective-permute-done((f32[512,256]{1,0:T(8,128)S(1)}, f32[512,256]{1,0:T(8,128)}, u32[]{:S(2)}, u32[]{:S(2)}) %collective-permute-start.110) | collective-permute-done | bytes 524320 | tf_op jit(solution)/shard_map/ppermute | solution.py:502
  595.1 9.6 %fusion.153 = f32[512,2048]{1,0:T(8,128)S(1)} fusion(f32[2048,1024]{1,0:T(8,128)} %constant_dynamic-update-slice_fusion.24, f32[512,256]{1,0:T(8,128)} %get-tuple-element.209, f32[512,256]{1,0:T(8,128)S(1)} %get-tuple-element.90, f32[512,256]{1,0:T(8,128)S(1)} %get-tuple-element.89, f32[512,256]{1,0:T(8,128)S(1)} %get-tuple-element.88), kind=kOutput, calls=%fused_computation.386 | convolution fusion | flops 6444023808 | bytes 14680064 | tf_op jit(solution)/shard_map/dot_general | solution.py:469
  637.8 24.5 %collective-permute-done.149 = f32[6]{0:T(128)S(1)} collective-permute-done((f32[6]{0:T(128)S(1)}, f32[6]{0:T(128)S(1)}, u32[]{:S(2)}, u32[]{:S(2)}) %collective-permute-start.149) | collective-permute-done | bytes 56 | tf_op jit(solution)/shard_map/ppermute | solution.py:497
  719.5 10.9 %fusion = f32[1024,1024]{1,0:T(8,128)} fusion(f32[512,1024]{1,0:T(8,128)} %collective-permute-done.127, f32[512,256]{1,0:T(8,128)S(1)} %copy-done.58, f32[512,256]{1,0:T(8,128)S(1)} %copy-done.17, f32[512,256]{1,0:T(8,128)S(1)} %copy-done.15, f32[512,256]{1,0:T(8,128)S(1)} %copy-done.13, f32[512,1024]{1,0:T(8,128)S(1)} %copy-done.47, ...), kind=kOutput, calls=%fused_computation.1 | convolution fusion | flops 6448742400 | bytes 12587008 | tf_op jit(solution)/shard_map/dot_general | solution.py:462
  731.6 12.0 %fusion.67.own = f32[1024,1024]{1,0:T(8,128)} fusion(f32[1024,1024]{1,0:T(8,128)} %fusion, f32[512,1024]{1,0:T(8,128)} %collective-permute-done.129, f32[512,1024]{1,0:T(8,128)} %collective-permute-done.128, f32[256,1024]{1,0:T(8,128)} %copy-done.100, f32[256,1024]{1,0:T(8,128)S(1)} %copy-done.99, f32[256,1024]{1,0:T(8,128)} %collective-permute-done.4, ...), kind=kOutput, calls=%fused_computation.83 | convolution fusion | flops 6448742400 | bytes 16781312 | tf_op jit(solution)/shard_map/dot_general | solution.py:462
  764.7 9.8 %collective-permute-done.121 = f32[264,256]{1,0:T(8,128)S(1)} collective-permute-done((f32[264,256]{1,0:T(8,128)S(1)}, f32[264,256]{1,0:T(8,128)S(1)}, u32[]{:S(2)}, u32[]{:S(2)}) %collective-permute-start.121) | collective-permute-done | bytes 270368 | tf_op jit(solution)/shard_map/ppermute | solution.py:493
  825.0 7.1 place.5
  (749 shorter events, 512.6 us)
Async XLA Ops:
  2.7 55.8 %collective-permute-start.57 = (f32[256,256]{1,0:T(8,128)}, f32[256,256]{1,0:T(8,128)}, u32[]{:S(2)}, u32[]{:S(2)}) collective-permute-start(f32[256,256]{1,0:T(8,128)} %get-tuple-element.221), channel_id=1, source_target_pairs={{0,1},{1,0},{2,3},{3,2},{4,5},{5,4},{6,7},{7,6},{8,9},{9,8},{10,11... | collective-permute-start | bytes 786440 | tf_op jit(solution)/shard_map/ppermute | solution.py:493
  5.6 53.4 %collective-permute-start.59 = (f32[256,256]{1,0:T(8,128)}, f32[256,256]{1,0:T(8,128)}, u32[]{:S(2)}, u32[]{:S(2)}) collective-permute-start(f32[256,256]{1,0:T(8,128)} %get-tuple-element.221), channel_id=1, source_target_pairs={{0,2},{1,3},{2,4},{3,5},{4,6},{5,7},{6,0},{7,1},{8,10},{9,11},{10,... | collective-permute-start | bytes 786440 | tf_op jit(solution)/shard_map/ppermute | solution.py:493
  7.2 55.0 %collective-permute-start.58 = (f32[256,256]{1,0:T(8,128)}, f32[256,256]{1,0:T(8,128)}, u32[]{:S(2)}, u32[]{:S(2)}) collective-permute-start(f32[256,256]{1,0:T(8,128)} %get-tuple-element.220), channel_id=1, source_target_pairs={{0,1},{1,0},{2,3},{3,2},{4,5},{5,4},{6,7},{7,6},{8,9},{9,8},{10,11... | collective-permute-start | bytes 786440 | tf_op jit(solution)/shard_map/ppermute | solution.py:493
  7.8 54.5 %collective-permute-start.60 = (f32[256,256]{1,0:T(8,128)}, f32[256,256]{1,0:T(8,128)}, u32[]{:S(2)}, u32[]{:S(2)}) collective-permute-start(f32[256,256]{1,0:T(8,128)} %get-tuple-element.220), channel_id=1, source_target_pairs={{0,2},{1,3},{2,4},{3,5},{4,6},{5,7},{6,0},{7,1},{8,10},{9,11},{10,... | collective-permute-start | bytes 786440 | tf_op jit(solution)/shard_map/ppermute | solution.py:493
  62.3 47.6 %collective-permute-start.11 = (f32[512,1024]{1,0:T(8,128)}, f32[512,1024]{1,0:T(8,128)S(1)}, u32[]{:S(2)}, u32[]{:S(2)}) collective-permute-start(f32[512,1024]{1,0:T(8,128)} %get-tuple-element.140), channel_id=1, source_target_pairs={{0,8},{8,0},{16,24},{24,16},{1,9},{9,1},{17,25},{25,17},{2,10},{10... | collective-permute-start | bytes 6291464 | tf_op jit(solution)/shard_map/ppermute | solution.py:497
  218.3 57.2 %collective-permute-start.41 = (f32[512,1024]{1,0:T(8,128)}, f32[512,1024]{1,0:T(8,128)}, u32[]{:S(2)}, u32[]{:S(2)}) collective-permute-start(f32[512,1024]{1,0:T(8,128)} %get-tuple-element.138), channel_id=1, source_target_pairs={{0,8},{8,0},{16,24},{24,16},{1,9},{9,1},{17,25},{25,17},{2,10},{10... | collective-permute-start | bytes 6291464 | tf_op jit(solution)/shard_map/ppermute | solution.py:497
  248.0 65.6 %collective-permute-start.75 = (f32[256,1024]{1,0:T(8,128)}, f32[256,1024]{1,0:T(8,128)}, u32[]{:S(2)}, u32[]{:S(2)}) collective-permute-start(f32[256,1024]{1,0:T(8,128)} %get-tuple-element.184), channel_id=1, source_target_pairs={{0,16},{8,24},{16,0},{24,8},{1,17},{9,25},{17,1},{25,9},{2,18},{10... | collective-permute-start | bytes 3145736 | tf_op jit(solution)/shard_map/ppermute | solution.py:502
  392.0 47.0 %collective-permute-start.42 = (f32[256,1024]{1,0:T(8,128)S(1)}, f32[256,1024]{1,0:T(8,128)S(1)}, u32[]{:S(2)}, u32[]{:S(2)}) collective-permute-start(f32[256,1024]{1,0:T(8,128)S(1)} %copy-done.72), channel_id=1, source_target_pairs={{0,16},{8,24},{16,0},{24,8},{1,17},{9,25},{17,1},{25,9},{2,18},{10... | collective-permute-start | bytes 3145736 | tf_op jit(solution)/shard_map/ppermute | solution.py:502
  402.4 52.6 %collective-permute-start.96 = (f32[512,688]{0,1:T(8,128)S(1)}, f32[512,688]{0,1:T(8,128)}, u32[]{:S(2)}, u32[]{:S(2)}) collective-permute-start(f32[512,688]{0,1:T(8,128)S(1)} %copy-done.38), channel_id=1, source_target_pairs={{0,16},{8,24},{16,0},{24,8},{1,17},{9,25},{17,1},{25,9},{2,18},{10... | collective-permute-start | bytes 4227080 | tf_op jit(solution)/shard_map/ppermute | solution.py:502
  412.1 69.1 %collective-permute-start.145 = (f32[512,1024]{1,0:T(8,128)}, f32[512,1024]{1,0:T(8,128)}, u32[]{:S(2)}, u32[]{:S(2)}) collective-permute-start(f32[512,1024]{1,0:T(8,128)} %get-tuple-element.134), channel_id=1, source_target_pairs={{0,8},{8,0},{16,24},{24,16},{1,9},{9,1},{17,25},{25,17},{2,10},{10... | collective-permute-start | bytes 6291464 | tf_op jit(solution)/shard_map/ppermute | solution.py:497
  492.2 47.7 %collective-permute-start.109 = (f32[512,688]{0,1:T(8,128)S(1)}, f32[512,688]{0,1:T(8,128)S(1)}, u32[]{:S(2)}, u32[]{:S(2)}) collective-permute-start(f32[512,688]{0,1:T(8,128)S(1)} %copy-done.36), channel_id=1, source_target_pairs={{0,16},{8,24},{16,0},{24,8},{1,17},{9,25},{17,1},{25,9},{2,18},{10... | collective-permute-start | bytes 4227080 | tf_op jit(solution)/shard_map/ppermute | solution.py:502
  509.8 171.4 %collective-permute-start.146 = (f32[688,1024]{1,0:T(8,128)}, f32[688,1024]{1,0:T(8,128)}, u32[]{:S(2)}, u32[]{:S(2)}) collective-permute-start(f32[688,1024]{1,0:T(8,128)} %fusion.26), channel_id=1, source_target_pairs={{0,16},{8,24},{16,0},{24,8},{1,17},{9,25},{17,1},{25,9},{2,18},{10... | collective-permute-start | bytes 8454152 | tf_op jit(solution)/shard_map/ppermute | solution.py:502
  510.4 84.1 %collective-permute-start.110 = (f32[512,256]{1,0:T(8,128)S(1)}, f32[512,256]{1,0:T(8,128)}, u32[]{:S(2)}, u32[]{:S(2)}) collective-permute-start(f32[512,256]{1,0:T(8,128)S(1)} %copy-done.43), channel_id=1, source_target_pairs={{0,16},{8,24},{16,0},{24,8},{1,17},{9,25},{17,1},{25,9},{2,18},{10... | collective-permute-start | bytes 1572872 | tf_op jit(solution)/shard_map/ppermute | solution.py:502
  514.9 101.0 %collective-permute-start.48 = (f32[256,256]{1,0:T(8,128)}, f32[256,256]{1,0:T(8,128)S(1)}, u32[]{:S(2)}, u32[]{:S(2)}) collective-permute-start(f32[256,256]{1,0:T(8,128)} %get-tuple-element.194), channel_id=1, source_target_pairs={{0,2},{1,3},{2,4},{3,5},{4,6},{5,7},{6,0},{7,1},{8,10},{9,11},{10,... | collective-permute-start | bytes 786440 | tf_op jit(solution)/shard_map/ppermute | solution.py:493
  618.2 85.9 %collective-permute-start.128 = (f32[512,1024]{1,0:T(8,128)}, f32[512,1024]{1,0:T(8,128)}, u32[]{:S(2)}, u32[]{:S(2)}) collective-permute-start(f32[512,1024]{1,0:T(8,128)} %pad_maximum_fusion.3), channel_id=1, source_target_pairs={{0,16},{8,24},{16,0},{24,8},{1,17},{9,25},{17,1},{25,9},{2,18},{10... | collective-permute-start | bytes 6291464 | tf_op jit(solution)/shard_map/ppermute | solution.py:502
  622.5 52.8 %collective-permute-start.112 = (f32[256,256]{1,0:T(8,128)}, f32[256,256]{1,0:T(8,128)}, u32[]{:S(2)}, u32[]{:S(2)}) collective-permute-start(f32[256,256]{1,0:T(8,128)} %get-tuple-element.155), channel_id=1, source_target_pairs={{0,2},{1,3},{2,4},{3,5},{4,6},{5,7},{6,0},{7,1},{8,10},{9,11},{10,... | collective-permute-start | bytes 786440 | tf_op jit(solution)/shard_map/ppermute | solution.py:493
  628.4 46.9 %collective-permute-start.113 = (f32[256,256]{1,0:T(8,128)}, f32[256,256]{1,0:T(8,128)}, u32[]{:S(2)}, u32[]{:S(2)}) collective-permute-start(f32[256,256]{1,0:T(8,128)} %get-tuple-element.154), channel_id=1, source_target_pairs={{0,1},{1,0},{2,3},{3,2},{4,5},{5,4},{6,7},{7,6},{8,9},{9,8},{10,11... | collective-permute-start | bytes 786440 | tf_op jit(solution)/shard_map/ppermute | solution.py:493
  704.1 45.4 %collective-permute-start.141 = (f32[512,688]{0,1:T(8,128)S(1)}, f32[512,688]{0,1:T(8,128)S(1)}, u32[]{:S(2)}, u32[]{:S(2)}) collective-permute-start(f32[512,688]{0,1:T(8,128)S(1)} %copy-done.37), channel_id=1, source_target_pairs={{0,8},{8,0},{16,24},{24,16},{1,9},{9,1},{17,25},{25,17},{2,10},{10... | collective-permute-start | bytes 4227080 | tf_op jit(solution)/shard_map/ppermute | solution.py:497
  705.8 56.5 %collective-permute-start.135 = (f32[512,256]{1,0:T(8,128)S(1)}, f32[512,256]{1,0:T(8,128)S(1)}, u32[]{:S(2)}, u32[]{:S(2)}) collective-permute-start(f32[512,256]{1,0:T(8,128)S(1)} %copy-done.44), channel_id=1, source_target_pairs={{0,8},{8,0},{16,24},{24,16},{1,9},{9,1},{17,25},{25,17},{2,10},{10... | collective-permute-start | bytes 1572872 | tf_op jit(solution)/shard_map/ppermute | solution.py:497
  712.2 51.5 %collective-permute-start.136 = (f32[512,256]{1,0:T(8,128)}, f32[512,256]{1,0:T(8,128)}, u32[]{:S(2)}, u32[]{:S(2)}) collective-permute-start(f32[512,256]{1,0:T(8,128)} %collective-permute-done.110), channel_id=1, source_target_pairs={{0,8},{8,0},{16,24},{24,16},{1,9},{9,1},{17,25},{25,17},{2,10},{10... | collective-permute-start | bytes 1572872 | tf_op jit(solution)/shard_map/ppermute | solution.py:497
  743.6 81.4 %collective-permute-start.130 = (f32[1024,1024]{1,0:T(8,128)}, f32[1024,1024]{1,0:T(8,128)}, u32[]{:S(2)}, u32[]{:S(2)}) collective-permute-start(f32[1024,1024]{1,0:T(8,128)} %fusion.67.own), channel_id=1, source_target_pairs={{0,8},{8,0},{16,24},{24,16},{1,9},{9,1},{17,25},{25,17},{2,10},{10... | collective-permute-start | bytes 12582920 | tf_op jit(solution)/shard_map/ppermute | solution.py:497
  762.4 49.3 %collective-permute-start.147 = (f32[688,1024]{1,0:T(8,128)S(1)}, f32[688,1024]{1,0:T(8,128)}, u32[]{:S(2)}, u32[]{:S(2)}) collective-permute-start(f32[688,1024]{1,0:T(8,128)S(1)} %add.928.own), channel_id=1, source_target_pairs={{0,8},{8,0},{16,24},{24,16},{1,9},{9,1},{17,25},{25,17},{2,10},{10... | collective-permute-start | bytes 8454152 | tf_op jit(solution)/shard_map/ppermute | solution.py:497
  763.5 52.3 %collective-permute-start.140 = (f32[688,1024]{1,0:T(8,128)}, f32[688,1024]{1,0:T(8,128)}, u32[]{:S(2)}, u32[]{:S(2)}) collective-permute-start(f32[688,1024]{1,0:T(8,128)} %fusion.74.own), channel_id=1, source_target_pairs={{0,8},{8,0},{16,24},{24,16},{1,9},{9,1},{17,25},{25,17},{2,10},{10... | collective-permute-start | bytes 8454152 | tf_op jit(solution)/shard_map/ppermute | solution.py:497
  763.7 56.7 %collective-permute-start.143 = (f32[688,1024]{1,0:T(8,128)}, f32[688,1024]{1,0:T(8,128)}, u32[]{:S(2)}, u32[]{:S(2)}) collective-permute-start(f32[688,1024]{1,0:T(8,128)} %fusion.77.own), channel_id=1, source_target_pairs={{0,8},{8,0},{16,24},{24,16},{1,9},{9,1},{17,25},{25,17},{2,10},{10... | collective-permute-start | bytes 8454152 | tf_op jit(solution)/shard_map/ppermute | solution.py:497
  (244 other events, 4452.8 us)

commit v4 on v3

--- a/solution.py
+++ b/solution.py
@@ -517,54 +517,67 @@
     return butterfly(jnp.where(place, value[None], 0.0), "heads")
 
 
-def gather_columns(value, hooks=(), parts=2):
+class Held:
+    def __init__(self, value):
+        self.value = value
+
+
+def meet(values, held=()):
+    out = lax.optimization_barrier(tuple(values) + tuple(item.value for item in held))
+    for item, value in zip(held, out[len(values) :]):
+        item.value = value
+    return list(out[: len(values)])
+
+
+def meet_one(value, *held):
+    return meet([value], held)[0]
+
+
+def turn(hooks, index):
+    return hooks[index] if index < len(hooks) else ()
+
+
+def gather_columns(value, hooks=()):
     deep, across = heads_grid()
     z, x = heads_place()
     rows, cols = value.shape
-    size = rows // parts
     out = jnp.zeros((rows, cols * deep * across), value.dtype)
-    moving = [value[i * size : (i + 1) * size] for i in range(parts)]
+    here = value
     for dz in range(deep):
-        if dz:
-            moving = [shift(item, 1, 0) for item in moving]
-            if dz <= len(hooks):
-                moving[0] = hooks[dz - 1](moving[0])
-        side = moving
-        for dx in range(across):
-            if dx:
-                side = [shift(item, 0, 1) for item in side]
+        moved = [shift(here, 0, dx) for dx in range(1, across)]
+        if dz + 1 < deep:
+            moved.append(shift(here, 1, 0))
+        moved = meet(moved, turn(hooks, dz))
+        for dx, side in enumerate([here] + moved[: across - 1]):
             column = ((z - dz) % deep * across + (x - dx) % across) * cols
-            for i in range(parts):
-                out = lax.dynamic_update_slice(out, side[i], (i * size, column))
+            out = lax.dynamic_update_slice(out, side, (0, column))
+        here = moved[-1]
     return out
 
 
-def scatter_columns(value, extra=None, hooks=(), parts=2):
+def scatter_columns(value, extra=None, hooks=()):
     deep, across = heads_grid()
     z, x = heads_place()
     rows, width = value.shape
     cols = width // (deep * across)
-    size = rows // parts
-
-    def piece(i, dz, dx):
+
+    def piece(dz, dx):
         column = ((z - dz) % deep * across + (x - dx) % across) * cols
-        block = lax.dynamic_slice(value, (i * size, column), (size, cols))
-        if extra is not None and i == parts - 1:
+        block = lax.dynamic_slice(value, (0, column), (rows, cols))
+        if extra is not None:
             tail = lax.dynamic_slice(extra, (0, column), (extra.shape[0], cols))
             block = jnp.concatenate([block, tail], 0)
         return block
 
-    total = [None] * parts
-    for turn, dz in enumerate(list(range(1, deep)) + [0]):
-        if 1 <= turn <= len(hooks):
-            total[0] = hooks[turn - 1](total[0])
-        for i in range(parts):
-            here = None
-            for dx in list(range(1, across)) + [0]:
-                block = piece(i, dz, dx)
-                here = block if here is None else shift(here, 0, 1) + block
-            total[i] = here if total[i] is None else shift(total[i], 1, 0) + here
-    return jnp.concatenate(total, 0)
+    total = None
+    for index, dz in enumerate(list(range(1, deep)) + [0]):
+        moved = [shift(piece(dz, dx), 0, dx) for dx in range(1, across)]
+        if total is not None:
+            moved.append(shift(total, 1, 0))
+        total = piece(dz, 0)
+        for item in meet(moved, turn(hooks, index)):
+            total = total + item
+    return total
 
 
 def half_of(value, index, axis):
@@ -646,19 +659,19 @@
     def __init__(self, value, parts=4):
         size = value.shape[0] // parts
         self.own = value
-        self.pieces = [
-            [row_shift(value[i * size : (i + 1) * size], step) for i in range(parts)]
+        self.steps = [
+            [Held(row_shift(value[i * size : (i + 1) * size], step)) for i in range(parts)]
             for step in range(1, chips_along())
         ]
 
-    def tie(self, i, main):
-        for step in self.pieces:
-            main, step[i] = lax.optimization_barrier((main, step[i]))
-        return main
+    def __getitem__(self, i):
+        return [step[i] for step in self.steps]
 
     def all(self):
         return [self.own] + [
-            step[0] if len(step) == 1 else jnp.concatenate(step, 0) for step in self.pieces
+            step[0].value if len(step) == 1
+            else jnp.concatenate([item.value for item in step], 0)
+            for step in self.steps
         ]
 
 
@@ -711,7 +724,7 @@
     gain_one = gains[:, 0].reshape(width)
     gain_two = gains[:, 1].reshape(width)
     grad_output = cotangent.reshape(length, slab)
-    dy_full = gather_columns(grad_output)
+    dy_held = Held(gather_columns(grad_output))
 
     w_joined = jnp.concatenate([w_query, w_key, w_value, w_gate_attn], axis=1)
     r1 = lax.rsqrt(jnp.mean(tokens * tokens, -1, keepdims=True) + epsilon)
@@ -723,7 +736,7 @@
         w_rate, normed, (((0,), (1,)), ((), ())), precision=lax.Precision.HIGH,
         preferred_element_type=f32,
     )
-    joined = unit_y.tie(0, joined)
+    joined = meet_one(joined, *unit_y[0])
     gate_pre = joined[:, 3 * span :]
     sig = jax.nn.sigmoid(rate_pre + b_rate[:, None])
     rate_t = sig / hd
@@ -735,70 +748,78 @@
     mixed, *saved = ttt_forward(
         joined, rate, rate_t, seg, seg_t, w0, b0, gain_col, shift_col, hd, heads
     )
-    mixed = unit_y.tie(1, mixed)
+    mixed = meet_one(mixed, *unit_y[1], dy_held)
     row_sums = butterfly(jnp.stack([jnp.sum(mixed, 1), jnp.sum(mixed * mixed, 1)]), "heads")
     row_mean = row_sums[0] / total_span
     inv_std = lax.rsqrt(row_sums[1] / total_span - row_mean * row_mean + epsilon)[:, None]
     centered = (mixed - row_mean[:, None]) * inv_std
     shaped = centered * post_gain + post_shift
     gate_act, gate_slope = gelu_parts(gate_pre)
-    gathered = gather_columns(
-        gate_act * shaped,
-        [functools.partial(unit_y.tie, 2), functools.partial(unit_y.tie, 3)],
-    )
+    gathered = gather_columns(gate_act * shaped, [unit_y[2], (), unit_y[3]])
     gathered_y = Along(tokens_half(gathered, core))
     attn = product(gathered, w_out)
     stream_cols = lax.dynamic_slice_in_dim(tokens, column, slab, 1)
     hidden = stream_cols + attn
-    whole = gather_columns(
-        hidden, [lambda v: v, functools.partial(gathered_y.tie, 0)],
-    )
+    whole = gather_columns(hidden, [(), (), gathered_y[0], gathered_y[1]])
+    dy_full = dy_held.value
 
     r2 = lax.rsqrt(jnp.mean(whole * whole, -1, keepdims=True) + epsilon)
     hnorm = whole * r2 * gain_two
     hnorm_y = Along(tokens_half(hnorm, core))
     a = product(hnorm, w_gate)
-    a = gathered_y.tie(1, a)
+    a = meet_one(a, *gathered_y[2])
     c = product(hnorm, w_up)
     act, slope = silu_parts(a)
     m = act * c
-    ffn_part = gathered_y.tie(2, product(m, w_down))
-    dm = right_product(dy_full, w_down)
+    dm = meet_one(right_product(dy_full, w_down), *gathered_y[3])
     da = dm * c * slope
     dc = dm * act
     da_y, dc_y = Along(da, 1), Along(dc, 1)
     dhnorm = right_product(da, w_gate) + right_product(dc, w_up)
+    dhnorm = meet_one(dhnorm, *hnorm_y[0])
     d_gain_two = jnp.sum(dhnorm * whole * r2, 0, keepdims=True)
     weighted = dhnorm * gain_two
     d_whole = r2 * weighted - whole * (r2 * r2 * r2) * jnp.mean(
         whole * weighted, -1, keepdims=True
     )
     pad = jnp.zeros((7, width), f32)
+    da_pair, dc_pair = both_cores(da), both_cores(dc)
+    own_gate = Held(left_product(da_pair, hnorm_y.own))
+    own_up = Held(left_product(dc_pair, hnorm_y.own))
+    own_down = Held(left_product(both_cores(m), tokens_half(dy_full, core)))
+    ffn_part = Held(product(m, w_down))
     d_part = scatter_columns(
         d_whole,
         jnp.concatenate([d_gain_two, pad], 0),
-        [
-            functools.partial(gathered_y.tie, 3),
-            functools.partial(hnorm_y.tie, 0),
-            functools.partial(hnorm_y.tie, 1),
-        ],
+        [[*hnorm_y[1], ffn_part], [*hnorm_y[2], own_gate], [*hnorm_y[3], own_up], [*da_y[0], own_down]],
     )
     d_hidden = grad_output + d_part[:length]
     d_gain_two = d_part[length]
     d_hidden_y = Along(d_hidden, 1)
-    g_down = left_product(both_cores(m), tokens_half(dy_full, core))
+    own_out = Held(left_product(gathered_y.own, both_cores(d_hidden)))
 
     d_gated = scatter_columns(
         right_product(d_hidden, w_out),
         None,
-        [
-            functools.partial(hnorm_y.tie, 2),
-            functools.partial(hnorm_y.tie, 3),
-            functools.partial(da_y.tie, 0),
-        ],
-    )
-    ffn = scatter_columns(ffn_part)
-    output = hidden + ffn
+        [[], [*dc_y[0], own_out], [*d_hidden_y[0]]],
+    )
+    d_gated = meet_one(d_gated, ffn_part, own_down)
+    down_y = [Held(item) for item in other_chips(own_down.value)]
+    deep, across = heads_grid()
+    z, x = heads_place()
+
+    def tile_set(dx):
+        return jnp.concatenate(
+            [
+                lax.dynamic_slice_in_dim(
+                    ffn_part.value, (i * across + (x - dx) % across) * slab, slab, 1
+                )
+                for i in range(deep)
+            ],
+            1,
+        )
+
+    ffn_x = [Held(shift(tile_set(dx), 0, dx)) for dx in range(1, across)]
     d_shaped = d_gated * gate_act
     d_gate_pre = d_gated * shaped * gate_slope
     d_post_gain = jnp.sum(d_shaped * centered, 0)
@@ -814,7 +835,15 @@
     dq, dk, dv, d_rate, dw, db, dg, dsh = ttt_backward(
         joined, rate_t, seg, seg_t, w0, b0, gain_col, shift_col, saved, d_mixed, hd, heads
     )
-    dq = d_hidden_y.tie(0, dc_y.tie(0, dq))
+    dq = meet_one(dq, *ffn_x)
+    ffn_sum = tile_set(0)
+    for item in ffn_x:
+        ffn_sum = ffn_sum + item.value
+    ffn = None
+    for dz in list(range(1, deep)) + [0]:
+        part = lax.dynamic_slice_in_dim(ffn_sum, (z - dz) % deep * slab, slab, 1)
+        ffn = part if ffn is None else shift(ffn, 1, 0) + part
+    output = hidden + ffn
     d_inner_weight, d_inner_bias = state_back(dw, db, heads, hd)
     d_rate_pre = d_rate * rate_t * (1.0 - sig)
     d_joined = jnp.concatenate([dq, dk, dv, d_gate_pre], 1)
@@ -828,22 +857,35 @@
     d_tokens = r1 * weighted - tokens * (r1 * r1 * r1) * jnp.mean(
         tokens * weighted, -1, keepdims=True
     )
-    d_part = scatter_columns(d_tokens, jnp.concatenate([d_gain_one, pad], 0))
+
+    def cores(values):
+        return [both_cores(value) for value in values]
+
+    def total(own, lefts, rights):
+        for left, right in zip(lefts[1:], rights[1:]):
+            own = own + left_product(left, right)
+        return Held(own)
+
+    gain_half = half_of(gain_one, core, 0)
+    normed_pairs = [pair * gain_half for pair in unit_y.all()]
+    own_joined = Held(left_product(normed_pairs[0], both_cores(d_joined)))
+    all_gate = total(own_gate.value, cores(da_y.all()), hnorm_y.all())
+    all_up = total(own_up.value, cores(dc_y.all()), hnorm_y.all())
+    all_out = total(own_out.value, gathered_y.all(), cores(d_hidden_y.all()))
+    d_part = scatter_columns(
+        d_tokens,
+        jnp.concatenate([d_gain_one, pad], 0),
+        [[own_joined], [all_gate, *down_y], [all_up, *d_joined_y[0], *d_rate_y[0]], [all_out]],
+    )
     d_stream = d_hidden + d_part[:length]
     d_gain_one = d_part[length]
 
-    def cores(values):
-        return [both_cores(value) for value in values]
-
-    (g_gate,) = finish(row_products(cores(da_y.all()), hnorm_y.all()), core, 1)
-    (g_up,) = finish(row_products(cores(dc_y.all()), hnorm_y.all()), core, 1)
-    (g_out,) = finish(row_products(gathered_y.all(), cores(d_hidden_y.all())), core, 0)
-    (g_down,) = finish(sum(other_chips(g_down), g_down), core, 1)
-    gain_half = half_of(gain_one, core, 0)
-    normed_pairs = [pair * gain_half for pair in unit_y.all()]
-    g_query, g_key, g_value, g_gate_attn = finish(
-        row_products(normed_pairs, cores(d_joined_y.all())), core, 0, (span,) * 4
-    )
+    (g_gate,) = finish(all_gate.value, core, 1)
+    (g_up,) = finish(all_up.value, core, 1)
+    (g_out,) = finish(all_out.value, core, 0)
+    (g_down,) = finish(sum((item.value for item in down_y), own_down.value), core, 1)
+    all_joined = total(own_joined.value, normed_pairs, cores(d_joined_y.all()))
+    g_query, g_key, g_value, g_gate_attn = finish(all_joined.value, core, 0, (span,) * 4)
     g_rate = None
     for pair, d in zip(normed_pairs, d_rate_y.all()):
         part = product(jnp.concatenate([d, swap(d, "rows", 1)], 1), pair)
@@ -859,11 +901,10 @@
         ]
         + [jnp.sum(weights) / lax.axis_size("heads")]
     )
-    stats = butterfly(butterfly(stats, "rows"), "heads")
-    rms_values = jnp.sqrt(stats[:5] / (stats[5] * width))
+    stats = butterfly(stats, "heads")
     small = [
         d_gain_one, jnp.sum(d_rate_pre, 1), d_inner_weight, d_inner_bias, dg, dsh,
-        d_post_gain, d_post_shift, d_gain_two,
+        d_post_gain, d_post_shift, d_gain_two, stats,
     ]
     packed = butterfly(jnp.concatenate([item.reshape(-1) for item in small]), "rows")
     parts = []
@@ -871,6 +912,8 @@
     for item in small:
         parts.append(packed[at : at + item.size])
         at += item.size
+    stats = parts[9]
+    rms_values = jnp.sqrt(stats[:5] / (stats[5] * width))
     return (
         output.reshape(1, length, slab),
         d_stream.reshape(1, length, slab),

time: 842 us -> 797 us (0.947)
  starting transfers between devices: 146 us -> 77.5 us
  local copies, waits for them, and re-layouts: 73.4 us -> 93 us
  other arithmetic: 39.5 us -> 57.4 us
  waiting for transfers between devices: 362 us -> 347 us
    ppermute x98 -> x46, starting transfers between devices: 101 us -> 42.3 us  [shift(): return lax.ppermute(value, 'heads', pairs)]
    ppermute x98 -> x46, waiting for transfers between devices: 199 us -> 182 us  [shift(): return lax.ppermute(value, 'heads', pairs)]
    add x13 -> x20, other arithmetic: 8.8 us -> 23.3 us  [the longest x4 7.08 us: total(): own = own + left_product(left, right)]
    ppermute x37 -> x35, waiting for transfers between devices: 49.4 us -> 62.4 us  [swap(): lax.ppermute(value, axis, [(i, i ^ bit) for i in range(lax.axis_size(axis...]
    ppermute x18, waiting for transfers between devices: 113 us -> 103 us  [row_shift(): lax.ppermute(value, 'rows', [(r, (r + 2 * step) % size) for r in range(si...]
    ppermute x37 -> x35, starting transfers between devices: 24.1 us -> 14.3 us  [swap(): lax.ppermute(value, axis, [(i, i ^ bit) for i in range(lax.axis_size(axis...]
    dynamic_slice x12 -> x0, other arithmetic: 8.89 us -> none  [piece(): block = lax.dynamic_slice(value, (i * size, column), (size, cols))]
    dynamic_update_slice x46 -> x22, local copies, waits for them, and re-layouts: 16.3 us -> 25 us  [gather_columns(): out = lax.dynamic_update_slice(out, side, (0, column))]
  transfers between devices with their start and end apart: 153 -> 99, of which waited for: 71 -> 53; matrix products, arithmetic and copies ran while one was open for 31% -> 35% of each run, Pallas kernels for 6% -> 7%
where the time goes in v4:
time: 797 us; the launch traced here: 790 us
  waiting for transfers between devices  347 us (44%)
  matrix products  152 us (19%)
  local copies, waits for them, and re-layouts  93 us (12%)
  starting transfers between devices  77.5 us (10%)
  Pallas kernels  59 us (7%)
  other arithmetic  57.4 us (7%)
    ppermute x46, waiting for transfers between devices, shift(): return lax.ppermute(value, 'heads', pairs)  182 us
    ppermute x18, waiting for transfers between devices, row_shift(): lax.ppermute(value, 'rows', [(r, (r + 2 * step) % size) for r in range(si...  103 us
    dot_general x9, matrix products, left_product(): lax.dot_general(left, right, (((0,), (0,)), ((), ())), precision=lax.Prec...  69.3 us
    ppermute x35, waiting for transfers between devices, swap(): lax.ppermute(value, axis, [(i, i ^ bit) for i in range(lax.axis_size(axis...  62.4 us
    dot_general x7, matrix products, product(): jnp.dot(left, right, precision=lax.Precision.HIGH, preferred_element_type...  44.9 us
    ppermute x46, starting transfers between devices, shift(): return lax.ppermute(value, 'heads', pairs)  42.3 us
    dot_general x5, matrix products, right_product(): lax.dot_general(left, right, (((1,), (1,)), ((), ())), precision=lax.Prec...  33.1 us
    dynamic_update_slice x22, local copies, waits for them, and re-layouts, gather_columns(): out = lax.dynamic_update_slice(out, side, (0, column))  25 us
  transfers between devices with their start and end apart: 99, of which 53 were waited for; matrix products, arithmetic and copies ran while one was open for 35% of the time, Pallas kernels for 7%

profile of v4, /device:TPU:0, one launch (start us, length us, event | category | flops | bytes accessed | tf_op | source)
XLA Modules:
  0.0 790.2 jit_solution(1833475054273735897)
XLA Ops:
  41.2 11.6 %fusion.38.joined = f32[512,1024]{1,0:T(8,128)} fusion(f32[2048,1024]{1,0:T(8,128)} %constant_dynamic-update-slice_fusion.24, f32[512,2048]{1,0:T(8,128)} %bitcast_multiply_fusion.3, f32[2048]{0:T(1024)S(1)} %bitcast.132), kind=kOutput, calls=%fused_computation.51 | convolution fusion | flops 6443499520 | bytes 14688256 | tf_op jit(solution)/shard_map/dot_general | solution.py:458
  62.2 10.2 %collective-permute-done.10 = f32[512,256]{1,0:T(8,128)} collective-permute-done((f32[512,256]{1,0:T(8,128)}, f32[512,256]{1,0:T(8,128)}, u32[]{:S(2)}, u32[]{:S(2)}) %collective-permute-start.10) | collective-permute-done | bytes 524320 | tf_op jit(solution)/shard_map/ppermute | solution.py:493
  77.4 12.8 %inner_forward.1 = (f32[512,256]{1,0:T(8,128)S(1)}, f32[256,512]{1,0:T(8,128)S(1)}, f32[256,512]{1,0:T(8,128)S(1)}, f32[4,256,128]{2,1,0:T(8,128)S(1)}, f32[4,256,1]{2,1,0:T(8,128)S(1)}) custom-call(f32[512,1024]{1,0:T(8,128)S(1)} %copy-done.2, f32[512,4]{1,0:T(8,128)S(1)} %copy-done.4, f32[4,512]{1,0:T(4,128)S(1)} %get-tuple-element.319.rate_t, ...), custom_call_target="tpu_custom_call" | custom-call | tf_op jit(solution)/shard_map/inner_forward/pallas_call | solution.py:182
  199.2 9.1 %collective-permute-done.27 = f32[512,256]{1,0:T(8,128)S(1)} collective-permute-done((f32[512,256]{1,0:T(8,128)S(1)}, f32[512,256]{1,0:T(8,128)S(1)}, u32[]{:S(2)}, u32[]{:S(2)}) %collective-permute-start.27) | collective-permute-done | bytes 524320 | tf_op jit(solution)/shard_map/ppermute | solution.py:493
  251.4 8.3 %fusion.152 = f32[512,688]{0,1:T(8,128)} fusion(f32[512,2048]{1,0:T(8,128)S(1)} %multiply_multiply_fusion, f32[2048,688]{0,1:T(8,128)} %param.41), kind=kOutput, calls=%fused_computation.338 | convolution fusion | flops 4328521728 | bytes 11239424 | tf_op jit(solution)/shard_map/dot_general | solution.py:458
  259.7 8.0 %collective-permute-done.35 = f32[256,1024]{1,0:T(8,128)} collective-permute-done((f32[256,1024]{1,0:T(8,128)}, f32[256,1024]{1,0:T(8,128)}, u32[]{:S(2)}, u32[]{:S(2)}) %collective-permute-start.35) | collective-permute-done | bytes 1048608 | tf_op jit(solution)/shard_map/ppermute | solution.py:502
  267.6 22.5 %collective-permute-done.36 = f32[256,1024]{1,0:T(8,128)} collective-permute-done((f32[256,1024]{1,0:T(8,128)}, f32[256,1024]{1,0:T(8,128)}, u32[]{:S(2)}, u32[]{:S(2)}) %collective-permute-start.36) | collective-permute-done | bytes 1048608 | tf_op jit(solution)/shard_map/ppermute | solution.py:502
  295.2 8.6 %fusion.154 = f32[512,2048]{1,0:T(8,128)} fusion(f32[512,688]{0,1:T(8,128)} %get-tuple-element.278, f32[2048,688]{0,1:T(8,128)S(1)} %bitcast.121), kind=kOutput, calls=%fused_computation.340 | convolution fusion | flops 4328521728 | bytes 11239424 | tf_op jit(solution)/shard_map/dot_general | solution.py:469
  339.9 12.6 %collective-permute-done.43 = f32[520,256]{1,0:T(8,128)S(1)} collective-permute-done((f32[520,256]{1,0:T(8,128)S(1)}, f32[520,256]{1,0:T(8,128)S(1)}, u32[]{:S(2)}, u32[]{:S(2)}) %collective-permute-start.43) | collective-permute-done | bytes 532512 | tf_op jit(solution)/shard_map/ppermute | solution.py:493
  354.5 8.7 %fusion.41 = f32[688,1024]{1,0:T(8,128)} fusion(f32[512,1024]{1,0:T(8,128)} %collective-permute-done.44, f32[512,1024]{1,0:T(8,128)S(1)} %copy-done.40, f32[512,688]{0,1:T(8,128)} %collective-permute-done.46, f32[512,688]{0,1:T(8,128)} %get-tuple-element.278), kind=kOutput, calls=%fused_computation.54 | convolution fusion | flops 4330274816 | bytes 9830400 | tf_op jit(solution)/shard_map/dot_general | solution.py:462
  366.1 8.6 %fusion.40 = f32[688,1024]{1,0:T(8,128)} fusion(f32[512,1024]{1,0:T(8,128)} %collective-permute-done.44, f32[512,1024]{1,0:T(8,128)S(1)} %copy-done.40, f32[512,688]{0,1:T(8,128)} %collective-permute-done.49, f32[512,688]{0,1:T(8,128)} %get-tuple-element.279), kind=kOutput, calls=%fused_computation.53 | convolution fusion | flops 4330274816 | bytes 9830400 | tf_op jit(solution)/shard_map/dot_general | solution.py:462
  380.5 8.4 %collective-permute-done.47 = f32[520,256]{1,0:T(8,128)S(1)} collective-permute-done((f32[520,256]{1,0:T(8,128)S(1)}, f32[520,256]{1,0:T(8,128)S(1)}, u32[]{:S(2)}, u32[]{:S(2)}) %collective-permute-start.47) | collective-permute-done | bytes 532512 | tf_op jit(solution)/shard_map/ppermute | solution.py:493
  396.2 14.1 %collective-permute-done.51 = f32[512,688]{0,1:T(8,128)} collective-permute-done((f32[512,688]{0,1:T(8,128)}, f32[512,688]{0,1:T(8,128)}, u32[]{:S(2)}, u32[]{:S(2)}) %collective-permute-start.51) | collective-permute-done | bytes 1409056 | tf_op jit(solution)/shard_map/ppermute | solution.py:502
  414.0 13.4 %collective-permute-done.57 = f32[512,256]{1,0:T(8,128)S(1)} collective-permute-done((f32[512,256]{1,0:T(8,128)S(1)}, f32[512,256]{1,0:T(8,128)S(1)}, u32[]{:S(2)}, u32[]{:S(2)}) %collective-permute-start.57) | collective-permute-done | bytes 524320 | tf_op jit(solution)/shard_map/ppermute | solution.py:493
  459.3 8.3 %collective-permute-done.54 = f32[512,256]{1,0:T(8,128)S(1)} collective-permute-done((f32[512,256]{1,0:T(8,128)S(1)}, f32[512,256]{1,0:T(8,128)S(1)}, u32[]{:S(2)}, u32[]{:S(2)}) %collective-permute-start.54) | collective-permute-done | bytes 524320 | tf_op jit(solution)/shard_map/ppermute | solution.py:493
  482.2 33.8 %collective-permute-done.64 = f32[2,512]{1,0:T(2,128)S(1)} collective-permute-done((f32[2,512]{1,0:T(2,128)S(1)}, f32[2,512]{1,0:T(2,128)S(1)}, u32[]{:S(2)}, u32[]{:S(2)}) %collective-permute-start.64) | collective-permute-done | bytes 4128 | tf_op jit(solution)/shard_map/ppermute | solution.py:497
  524.7 22.2 %inner_backward.1 = (f32[512,256]{1,0:T(8,128)S(1)}, f32[512,256]{1,0:T(8,128)S(1)}, f32[512,256]{1,0:T(8,128)S(1)}, f32[4,512]{1,0:T(4,128)S(1)}, f32[256,128]{...) custom-call(f32[512,1024]{1,0:T(8,128)} %fusion.38.joined, ...), custom_call_target="tpu_custom_call" | custom-call | tf_op jit(solution)/shard_map/inner_backward/pallas_call | solution.py:407
  547.9 9.9 %fusion.138 = f32[512,2048]{1,0:T(8,128)S(1)} fusion(f32[2048,1024]{1,0:T(8,128)} %constant_dynamic-update-slice_fusion.24, f32[512,256]{1,0:T(8,128)} %copy-done.46, f32[512,256]{1,0:T(8,128)S(1)} %get-tuple-element.166, f32[512,256]{1,0:T(8,128)S(1)} %get-tuple-element.165, f32[512,256]{1,0:T(8,128)S(1)} %get-tuple-element.164), kind=kOutput, calls=%fused_computation.326 | convolution fusion | flops 6444023808 | bytes 14680064 | tf_op jit(solution)/shard_map/dot_general | solution.py:469
  566.0 10.3 %fusion.8 = f32[1024,1024]{1,0:T(8,128)} fusion(f32[512,1024]{1,0:T(8,128)S(1)} %collective-permute-done.75, f32[512,256]{1,0:T(8,128)S(1)} %copy-done.47, f32[512,256]{1,0:T(8,128)S(1)} %get-tuple-element.166, f32[512,256]{1,0:T(8,128)S(1)} %get-tuple-element.165, f32[512,256]{1,0:T(8,128)S(1)} %get-tuple-element.164, ...), kind=kOutput, calls=%fused_computation.10 | convolution fusion | flops 6448742400 | bytes 12587008 | tf_op jit(solution)/shard_map/dot_general | solution.py:462
  605.7 25.0 %collective-permute-done.82 = f32[4,512]{1,0:T(4,128)S(1)} collective-permute-done((f32[4,512]{1,0:T(4,128)S(1)}, f32[4,512]{1,0:T(4,128)S(1)}, u32[]{:S(2)}, u32[]{:S(2)}) %collective-permute-start.82) | collective-permute-done | bytes 8224 | tf_op jit(solution)/shard_map/ppermute | solution.py:502
  639.2 14.1 %collective-permute-done.68 = f32[512,256]{1,0:T(8,128)S(1)} collective-permute-done((f32[512,256]{1,0:T(8,128)}, f32[512,256]{1,0:T(8,128)S(1)}, u32[]{:S(2)}, u32[]{:S(2)}) %collective-permute-start.68) | collective-permute-done | bytes 524320 | tf_op jit(solution)/shard_map/ppermute | solution.py:493
  655.4 10.4 %fusion.26 = f32[1024,1024]{1,0:T(8,128)S(1)} fusion(f32[512,1024]{1,0:T(8,128)} %collective-permute-done.90, f32[512,1024]{1,0:T(8,128)} %collective-permute-done.81, f32[256,1024]{1,0:T(8,128)} %collective-permute-done.23, f32[256,1024]{1,0:T(8,128)} %copy-done.88, f32[256,1024]{1,0:T(8,128)} %collective-permute-done.4, ...), kind=kOutput, calls=%fused_computation.29 | convolution fusion | flops 6447693824 | bytes 12587008 | tf_op jit(solution)/shard_map/dot_general | solution.py:462
  683.0 13.2 %collective-permute-done.70 = f32[512,256]{1,0:T(8,128)} collective-permute-done((f32[512,256]{1,0:T(8,128)}, f32[512,256]{1,0:T(8,128)}, u32[]{:S(2)}, u32[]{:S(2)}) %collective-permute-start.70) | collective-permute-done | bytes 524320 | tf_op jit(solution)/shard_map/ppermute | solution.py:493
  733.5 8.2 %collective-permute-done.83 = f32[520,256]{1,0:T(8,128)} collective-permute-done((f32[520,256]{1,0:T(8,128)}, f32[520,256]{1,0:T(8,128)}, u32[]{:S(2)}, u32[]{:S(2)}) %collective-permute-start.83) | collective-permute-done | bytes 532512 | tf_op jit(solution)/shard_map/ppermute | solution.py:493
  (582 shorter events, 473.9 us)
Async XLA Ops:
  0.7 38.5 %collective-permute-start.5 = (f32[512,256]{1,0:T(8,128)}, f32[512,256]{1,0:T(8,128)}, u32[]{:S(2)}, u32[]{:S(2)}) collective-permute-start(f32[512,256]{1,0:T(8,128)} %bitcast.129), channel_id=1, source_target_pairs={{0,1},{1,0},{2,3},{3,2},{4,5},{5,4},{6,7},{7,6},{8,9},{9,8},{10,11... | collective-permute-start | bytes 1572872 | tf_op jit(solution)/shard_map/ppermute | solution.py:493
  14.3 60.5 %collective-permute-start.3 = (f32[256,1024]{1,0:T(8,128)}, f32[256,1024]{1,0:T(8,128)}, u32[]{:S(2)}, u32[]{:S(2)}) collective-permute-start(f32[256,1024]{1,0:T(8,128)} %get-tuple-element.275), channel_id=1, source_target_pairs={{0,16},{8,24},{16,0},{24,8},{1,17},{9,25},{17,1},{25,9},{2,18},{10... | collective-permute-start | bytes 3145736 | tf_op jit(solution)/shard_map/ppermute | solution.py:502
  16.5 82.4 %collective-permute-start.4 = (f32[256,1024]{1,0:T(8,128)}, f32[256,1024]{1,0:T(8,128)}, u32[]{:S(2)}, u32[]{:S(2)}) collective-permute-start(f32[256,1024]{1,0:T(8,128)} %get-tuple-element.274), channel_id=1, source_target_pairs={{0,16},{8,24},{16,0},{24,8},{1,17},{9,25},{17,1},{25,9},{2,18},{10... | collective-permute-start | bytes 3145736 | tf_op jit(solution)/shard_map/ppermute | solution.py:502
  39.1 67.8 %collective-permute-start.17 = (f32[512,1024]{1,0:T(8,128)}, f32[512,1024]{1,0:T(8,128)}, u32[]{:S(2)}, u32[]{:S(2)}) collective-permute-start(f32[512,1024]{1,0:T(8,128)} %get-tuple-element.241), channel_id=1, source_target_pairs={{0,8},{8,0},{16,24},{24,16},{1,9},{9,1},{17,25},{25,17},{2,10},{10... | collective-permute-start | bytes 6291464 | tf_op jit(solution)/shard_map/ppermute | solution.py:497
  242.8 47.3 %collective-permute-start.36 = (f32[256,1024]{1,0:T(8,128)}, f32[256,1024]{1,0:T(8,128)}, u32[]{:S(2)}, u32[]{:S(2)}) collective-permute-start(f32[256,1024]{1,0:T(8,128)} %get-tuple-element.283), channel_id=1, source_target_pairs={{0,16},{8,24},{16,0},{24,8},{1,17},{9,25},{17,1},{25,9},{2,18},{10... | collective-permute-start | bytes 3145736 | tf_op jit(solution)/shard_map/ppermute | solution.py:502
  243.3 87.6 %collective-permute-start.44 = (f32[512,1024]{1,0:T(8,128)}, f32[512,1024]{1,0:T(8,128)}, u32[]{:S(2)}, u32[]{:S(2)}) collective-permute-start(f32[512,1024]{1,0:T(8,128)} %get-tuple-element.269), channel_id=1, source_target_pairs={{0,8},{8,0},{16,24},{24,16},{1,9},{9,1},{17,25},{25,17},{2,10},{10... | collective-permute-start | bytes 6291464 | tf_op jit(solution)/shard_map/ppermute | solution.py:497
  243.3 69.3 %collective-permute-start.37 = (f32[256,1024]{1,0:T(8,128)}, f32[256,1024]{1,0:T(8,128)}, u32[]{:S(2)}, u32[]{:S(2)}) collective-permute-start(f32[256,1024]{1,0:T(8,128)} %get-tuple-element.271), channel_id=1, source_target_pairs={{0,16},{8,24},{16,0},{24,8},{1,17},{9,25},{17,1},{25,9},{2,18},{10... | collective-permute-start | bytes 3145736 | tf_op jit(solution)/shard_map/ppermute | solution.py:502
  244.9 85.5 %collective-permute-start.42 = (f32[256,1024]{1,0:T(8,128)}, f32[256,1024]{1,0:T(8,128)}, u32[]{:S(2)}, u32[]{:S(2)}) collective-permute-start(f32[256,1024]{1,0:T(8,128)} %get-tuple-element.270), channel_id=1, source_target_pairs={{0,16},{8,24},{16,0},{24,8},{1,17},{9,25},{17,1},{25,9},{2,18},{10... | collective-permute-start | bytes 3145736 | tf_op jit(solution)/shard_map/ppermute | solution.py:502
  294.7 70.2 %collective-permute-start.49 = (f32[512,688]{0,1:T(8,128)}, f32[512,688]{0,1:T(8,128)}, u32[]{:S(2)}, u32[]{:S(2)}) collective-permute-start(f32[512,688]{0,1:T(8,128)} %get-tuple-element.279), channel_id=1, source_target_pairs={{0,8},{8,0},{16,24},{24,16},{1,9},{9,1},{17,25},{25,17},{2,10},{10... | collective-permute-start | bytes 4227080 | tf_op jit(solution)/shard_map/ppermute | solution.py:497
  294.7 59.2 %collective-permute-start.46 = (f32[512,688]{0,1:T(8,128)}, f32[512,688]{0,1:T(8,128)}, u32[]{:S(2)}, u32[]{:S(2)}) collective-permute-start(f32[512,688]{0,1:T(8,128)} %get-tuple-element.278), channel_id=1, source_target_pairs={{0,8},{8,0},{16,24},{24,16},{1,9},{9,1},{17,25},{25,17},{2,10},{10... | collective-permute-start | bytes 4227080 | tf_op jit(solution)/shard_map/ppermute | solution.py:497
  339.8 49.5 %collective-permute-start.53 = (f32[512,1024]{1,0:T(8,128)S(1)}, f32[512,1024]{1,0:T(8,128)S(1)}, u32[]{:S(2)}, u32[]{:S(2)}) collective-permute-start(f32[512,1024]{1,0:T(8,128)S(1)} %get-tuple-element.267), channel_id=1, source_target_pairs={{0,8},{8,0},{16,24},{24,16},{1,9},{9,1},{17,25},{25,17},{2,10},{10... | collective-permute-start | bytes 6291464 | tf_op jit(solution)/shard_map/ppermute | solution.py:497
  364.1 46.2 %collective-permute-start.51 = (f32[512,688]{0,1:T(8,128)}, f32[512,688]{0,1:T(8,128)}, u32[]{:S(2)}, u32[]{:S(2)}) collective-permute-start(f32[512,688]{0,1:T(8,128)} %get-tuple-element.278), channel_id=1, source_target_pairs={{0,16},{8,24},{16,0},{24,8},{1,17},{9,25},{17,1},{25,9},{2,18},{10... | collective-permute-start | bytes 4227080 | tf_op jit(solution)/shard_map/ppermute | solution.py:502
  389.3 51.2 %collective-permute-start.59 = (f32[512,688]{0,1:T(8,128)}, f32[512,688]{0,1:T(8,128)}, u32[]{:S(2)}, u32[]{:S(2)}) collective-permute-start(f32[512,688]{0,1:T(8,128)} %get-tuple-element.279), channel_id=1, source_target_pairs={{0,16},{8,24},{16,0},{24,8},{1,17},{9,25},{17,1},{25,9},{2,18},{10... | collective-permute-start | bytes 4227080 | tf_op jit(solution)/shard_map/ppermute | solution.py:502
  474.7 72.9 %collective-permute-start.67 = (f32[512,1024]{1,0:T(8,128)S(1)}, f32[512,1024]{1,0:T(8,128)S(1)}, u32[]{:S(2)}, u32[]{:S(2)}) collective-permute-start(f32[512,1024]{1,0:T(8,128)S(1)} %pad_maximum_fusion.3), channel_id=1, source_target_pairs={{0,1},{1,0},{2,3},{3,2},{4,5},{5,4},{6,7},{7,6},{8,9},{9,8},{10,11... | collective-permute-start | bytes 6291464 | tf_op jit(solution)/shard_map/ppermute | solution.py:493
  521.8 58.4 %collective-permute-start.77 = (f32[512,688]{0,1:T(8,128)}, f32[512,688]{0,1:T(8,128)}, u32[]{:S(2)}, u32[]{:S(2)}) collective-permute-start(f32[512,688]{0,1:T(8,128)} %collective-permute-done.51), channel_id=1, source_target_pairs={{0,8},{8,0},{16,24},{24,16},{1,9},{9,1},{17,25},{25,17},{2,10},{10... | collective-permute-start | bytes 4227080 | tf_op jit(solution)/shard_map/ppermute | solution.py:497
  521.8 74.1 %collective-permute-start.80 = (f32[512,688]{0,1:T(8,128)}, f32[512,688]{0,1:T(8,128)}, u32[]{:S(2)}, u32[]{:S(2)}) collective-permute-start(f32[512,688]{0,1:T(8,128)} %collective-permute-done.59), channel_id=1, source_target_pairs={{0,8},{8,0},{16,24},{24,16},{1,9},{9,1},{17,25},{25,17},{2,10},{10... | collective-permute-start | bytes 4227080 | tf_op jit(solution)/shard_map/ppermute | solution.py:497
  522.3 71.2 %collective-permute-start.78 = (f32[688,1024]{1,0:T(8,128)}, f32[688,1024]{1,0:T(8,128)}, u32[]{:S(2)}, u32[]{:S(2)}) collective-permute-start(f32[688,1024]{1,0:T(8,128)} %fusion), channel_id=1, source_target_pairs={{0,16},{8,24},{16,0},{24,8},{1,17},{9,25},{17,1},{25,9},{2,18},{10... | collective-permute-start | bytes 8454152 | tf_op jit(solution)/shard_map/ppermute | solution.py:502
  558.0 72.7 %collective-permute-start.81 = (f32[512,1024]{1,0:T(8,128)S(1)}, f32[512,1024]{1,0:T(8,128)}, u32[]{:S(2)}, u32[]{:S(2)}) collective-permute-start(f32[512,1024]{1,0:T(8,128)S(1)} %pad_maximum_fusion.4), channel_id=1, source_target_pairs={{0,16},{8,24},{16,0},{24,8},{1,17},{9,25},{17,1},{25,9},{2,18},{10... | collective-permute-start | bytes 6291464 | tf_op jit(solution)/shard_map/ppermute | solution.py:502
  593.0 37.7 %collective-permute-start.72 = (f32[520,256]{1,0:T(8,128)S(1)}, f32[520,256]{1,0:T(8,128)S(1)}, u32[]{:S(2)}, u32[]{:S(2)}) collective-permute-start(f32[520,256]{1,0:T(8,128)S(1)} %pad_maximum_fusion.10), channel_id=1, source_target_pairs={{0,1},{1,0},{2,3},{3,2},{4,5},{5,4},{6,7},{7,6},{8,9},{9,8},{10,11... | collective-permute-start | bytes 1597448 | tf_op jit(solution)/shard_map/ppermute | solution.py:493
  595.3 36.2 %collective-permute-start.79 = (f32[520,256]{1,0:T(8,128)S(1)}, f32[520,256]{1,0:T(8,128)S(1)}, u32[]{:S(2)}, u32[]{:S(2)}) collective-permute-start(f32[520,256]{1,0:T(8,128)S(1)} %fusion.95), channel_id=1, source_target_pairs={{0,2},{1,3},{2,4},{3,5},{4,6},{5,7},{6,0},{7,1},{8,10},{9,11},{10,... | collective-permute-start | bytes 1597448 | tf_op jit(solution)/shard_map/ppermute | solution.py:493
  668.9 114.0 %collective-permute-start.91 = (f32[1024,1024]{1,0:T(8,128)}, f32[1024,1024]{1,0:T(8,128)}, u32[]{:S(2)}, u32[]{:S(2)}) collective-permute-start(f32[1024,1024]{1,0:T(8,128)} %add.699.own), channel_id=1, source_target_pairs={{0,8},{8,0},{16,24},{24,16},{1,9},{9,1},{17,25},{25,17},{2,10},{10... | collective-permute-start | bytes 12582920 | tf_op jit(solution)/shard_map/ppermute | solution.py:497
  711.6 57.8 %collective-permute-start.98 = (f32[688,1024]{1,0:T(8,128)}, f32[688,1024]{1,0:T(8,128)}, u32[]{:S(2)}, u32[]{:S(2)}) collective-permute-start(f32[688,1024]{1,0:T(8,128)} %add.701.own), channel_id=1, source_target_pairs={{0,8},{8,0},{16,24},{24,16},{1,9},{9,1},{17,25},{25,17},{2,10},{10... | collective-permute-start | bytes 8454152 | tf_op jit(solution)/shard_map/ppermute | solution.py:497
  711.7 62.4 %collective-permute-start.96 = (f32[688,1024]{1,0:T(8,128)S(1)}, f32[688,1024]{1,0:T(8,128)}, u32[]{:S(2)}, u32[]{:S(2)}) collective-permute-start(f32[688,1024]{1,0:T(8,128)S(1)} %add.684.own), channel_id=1, source_target_pairs={{0,8},{8,0},{16,24},{24,16},{1,9},{9,1},{17,25},{25,17},{2,10},{10... | collective-permute-start | bytes 8454152 | tf_op jit(solution)/shard_map/ppermute | solution.py:497
  712.2 66.0 %collective-permute-start.97 = (f32[688,1024]{1,0:T(8,128)}, f32[688,1024]{1,0:T(8,128)}, u32[]{:S(2)}, u32[]{:S(2)}) collective-permute-start(f32[688,1024]{1,0:T(8,128)} %add.687.own), channel_id=1, source_target_pairs={{0,8},{8,0},{16,24},{24,16},{1,9},{9,1},{17,25},{25,17},{2,10},{10... | collective-permute-start | bytes 8454152 | tf_op jit(solution)/shard_map/ppermute | solution.py:497
  (175 other events, 3218.8 us)

commit v5 on v4

--- a/solution.py
+++ b/solution.py
@@ -534,7 +534,8 @@
 
 
 def turn(hooks, index):
-    return hooks[index] if index < len(hooks) else ()
+    hook = hooks[index] if index < len(hooks) else ()
+    return hook() if callable(hook) else hook
 
 
 def gather_columns(value, hooks=()):
@@ -542,16 +543,22 @@
     z, x = heads_place()
     rows, cols = value.shape
     out = jnp.zeros((rows, cols * deep * across), value.dtype)
-    here = value
+    here, ready = value, [(0, 0, value)]
     for dz in range(deep):
         moved = [shift(here, 0, dx) for dx in range(1, across)]
         if dz + 1 < deep:
             moved.append(shift(here, 1, 0))
-        moved = meet(moved, turn(hooks, dz))
-        for dx, side in enumerate([here] + moved[: across - 1]):
-            column = ((z - dz) % deep * across + (x - dx) % across) * cols
-            out = lax.dynamic_update_slice(out, side, (0, column))
-        here = moved[-1]
+        for oz, ox, item in ready:
+            column = ((z - oz) % deep * across + (x - ox) % across) * cols
+            out = lax.dynamic_update_slice(out, item, (0, column))
+        *moved, out = meet(moved + [out], turn(hooks, dz))
+        ready = [(dz, dx, moved[dx - 1]) for dx in range(1, across)]
+        if dz + 1 < deep:
+            here = moved[-1]
+            ready.append((dz + 1, 0, here))
+    for oz, ox, item in ready:
+        column = ((z - oz) % deep * across + (x - ox) % across) * cols
+        out = lax.dynamic_update_slice(out, item, (0, column))
     return out
 
 
@@ -748,35 +755,58 @@
     mixed, *saved = ttt_forward(
         joined, rate, rate_t, seg, seg_t, w0, b0, gain_col, shift_col, hd, heads
     )
-    mixed = meet_one(mixed, *unit_y[1], dy_held)
+    mixed = meet_one(mixed, *unit_y[1])
     row_sums = butterfly(jnp.stack([jnp.sum(mixed, 1), jnp.sum(mixed * mixed, 1)]), "heads")
+    row_sums = meet_one(row_sums, *unit_y[2], dy_held)
     row_mean = row_sums[0] / total_span
     inv_std = lax.rsqrt(row_sums[1] / total_span - row_mean * row_mean + epsilon)[:, None]
     centered = (mixed - row_mean[:, None]) * inv_std
     shaped = centered * post_gain + post_shift
     gate_act, gate_slope = gelu_parts(gate_pre)
-    gathered = gather_columns(gate_act * shaped, [unit_y[2], (), unit_y[3]])
+    gathered = gather_columns(gate_act * shaped, [(), unit_y[3]])
     gathered_y = Along(tokens_half(gathered, core))
     attn = product(gathered, w_out)
     stream_cols = lax.dynamic_slice_in_dim(tokens, column, slab, 1)
     hidden = stream_cols + attn
-    whole = gather_columns(hidden, [(), (), gathered_y[0], gathered_y[1]])
+    whole = gather_columns(hidden, [(), gathered_y[0], gathered_y[1]])
     dy_full = dy_held.value
 
     r2 = lax.rsqrt(jnp.mean(whole * whole, -1, keepdims=True) + epsilon)
     hnorm = whole * r2 * gain_two
     hnorm_y = Along(tokens_half(hnorm, core))
     a = product(hnorm, w_gate)
-    a = meet_one(a, *gathered_y[2])
     c = product(hnorm, w_up)
     act, slope = silu_parts(a)
     m = act * c
-    dm = meet_one(right_product(dy_full, w_down), *gathered_y[3])
+    ffn_part = product(m, w_down)
+    deep, across = heads_grid()
+    z, x = heads_place()
+
+    def tile_set(dx):
+        return jnp.concatenate(
+            [
+                lax.dynamic_slice_in_dim(
+                    ffn_part, (i * across + (x - dx) % across) * slab, slab, 1
+                )
+                for i in range(deep)
+            ],
+            1,
+        )
+
+    ffn_x = [Held(shift(tile_set(dx), 0, dx)) for dx in range(1, across)]
+    dm = meet_one(right_product(dy_full, w_down), *gathered_y[2])
     da = dm * c * slope
     dc = dm * act
     da_y, dc_y = Along(da, 1), Along(dc, 1)
     dhnorm = right_product(da, w_gate) + right_product(dc, w_up)
-    dhnorm = meet_one(dhnorm, *hnorm_y[0])
+    dhnorm = meet_one(dhnorm, *gathered_y[3], *ffn_x)
+    ffn_sum = tile_set(0)
+    for item in ffn_x:
+        ffn_sum = ffn_sum + item.value
+
+    def ffn_tile(dz):
+        return lax.dynamic_slice_in_dim(ffn_sum, (z - dz) % deep * slab, slab, 1)
+
     d_gain_two = jnp.sum(dhnorm * whole * r2, 0, keepdims=True)
     weighted = dhnorm * gain_two
     d_whole = r2 * weighted - whole * (r2 * r2 * r2) * jnp.mean(
@@ -787,44 +817,38 @@
     own_gate = Held(left_product(da_pair, hnorm_y.own))
     own_up = Held(left_product(dc_pair, hnorm_y.own))
     own_down = Held(left_product(both_cores(m), tokens_half(dy_full, core)))
-    ffn_part = Held(product(m, w_down))
+    ffn_step = Held(shift(ffn_tile(1), 1, 0))
     d_part = scatter_columns(
         d_whole,
         jnp.concatenate([d_gain_two, pad], 0),
-        [[*hnorm_y[1], ffn_part], [*hnorm_y[2], own_gate], [*hnorm_y[3], own_up], [*da_y[0], own_down]],
+        [[ffn_step], [*hnorm_y[0], *hnorm_y[1]], [*hnorm_y[2], own_gate], [own_up]],
     )
     d_hidden = grad_output + d_part[:length]
     d_gain_two = d_part[length]
     d_hidden_y = Along(d_hidden, 1)
     own_out = Held(left_product(gathered_y.own, both_cores(d_hidden)))
+    ffn_step = Held(shift(ffn_step.value + ffn_tile(2 % deep), 1, 0) if deep > 2 else ffn_step.value)
 
     d_gated = scatter_columns(
         right_product(d_hidden, w_out),
         None,
-        [[], [*dc_y[0], own_out], [*d_hidden_y[0]]],
-    )
-    d_gated = meet_one(d_gated, ffn_part, own_down)
+        [[*hnorm_y[3], own_down], [*da_y[0], ffn_step], [*dc_y[0], own_out], [*d_hidden_y[0]]],
+    )
+    d_gated = meet_one(d_gated, own_down)
     down_y = [Held(item) for item in other_chips(own_down.value)]
-    deep, across = heads_grid()
-    z, x = heads_place()
-
-    def tile_set(dx):
-        return jnp.concatenate(
-            [
-                lax.dynamic_slice_in_dim(
-                    ffn_part.value, (i * across + (x - dx) % across) * slab, slab, 1
-                )
-                for i in range(deep)
-            ],
-            1,
-        )
-
-    ffn_x = [Held(shift(tile_set(dx), 0, dx)) for dx in range(1, across)]
+    ffn = ffn_step.value
+    for dz in range(3, deep):
+        ffn = shift(ffn + ffn_tile(dz), 1, 0)
+    ffn = Held(ffn + ffn_tile(0))
     d_shaped = d_gated * gate_act
     d_gate_pre = d_gated * shaped * gate_slope
     d_post_gain = jnp.sum(d_shaped * centered, 0)
     d_post_shift = jnp.sum(d_shaped, 0)
     d_center = d_shaped * post_gain
+    gain_half = half_of(gain_one, core, 0)
+    normed_pairs = [pair * gain_half for pair in unit_y.all()]
+    d_gate_y = Along(d_gate_pre, 1)
+    own_attn = Held(left_product(normed_pairs[0], both_cores(d_gate_pre)))
     back_sums = butterfly(
         jnp.stack([jnp.sum(d_center, 1), jnp.sum(d_center * centered, 1)]), "heads"
     )
@@ -835,19 +859,14 @@
     dq, dk, dv, d_rate, dw, db, dg, dsh = ttt_backward(
         joined, rate_t, seg, seg_t, w0, b0, gain_col, shift_col, saved, d_mixed, hd, heads
     )
-    dq = meet_one(dq, *ffn_x)
-    ffn_sum = tile_set(0)
-    for item in ffn_x:
-        ffn_sum = ffn_sum + item.value
-    ffn = None
-    for dz in list(range(1, deep)) + [0]:
-        part = lax.dynamic_slice_in_dim(ffn_sum, (z - dz) % deep * slab, slab, 1)
-        ffn = part if ffn is None else shift(ffn, 1, 0) + part
-    output = hidden + ffn
+    dq = meet_one(dq, *down_y, *d_gate_y[0], own_attn, ffn)
+    output = hidden + ffn.value
+    ffn = ffn.value
     d_inner_weight, d_inner_bias = state_back(dw, db, heads, hd)
     d_rate_pre = d_rate * rate_t * (1.0 - sig)
-    d_joined = jnp.concatenate([dq, dk, dv, d_gate_pre], 1)
-    d_joined_y, d_rate_y = Along(d_joined, 1), Along(d_rate_pre, 1)
+    d_three = jnp.concatenate([dq, dk, dv], 1)
+    d_three_y, d_rate_y = Along(d_three, 1), Along(d_rate_pre, 1)
+    d_joined = jnp.concatenate([d_three, d_gate_pre], 1)
     d_normed = right_product(d_joined, w_joined) + lax.dot_general(
         d_rate_pre, w_rate, (((0,), (1,)), ((), ())), precision=lax.Precision.HIGH,
         preferred_element_type=f32,
@@ -866,33 +885,11 @@
             own = own + left_product(left, right)
         return Held(own)
 
-    gain_half = half_of(gain_one, core, 0)
-    normed_pairs = [pair * gain_half for pair in unit_y.all()]
-    own_joined = Held(left_product(normed_pairs[0], both_cores(d_joined)))
+    own_three = Held(left_product(normed_pairs[0], both_cores(d_three)))
+    all_attn = total(own_attn.value, normed_pairs, cores(d_gate_y.all()))
     all_gate = total(own_gate.value, cores(da_y.all()), hnorm_y.all())
     all_up = total(own_up.value, cores(dc_y.all()), hnorm_y.all())
     all_out = total(own_out.value, gathered_y.all(), cores(d_hidden_y.all()))
-    d_part = scatter_columns(
-        d_tokens,
-        jnp.concatenate([d_gain_one, pad], 0),
-        [[own_joined], [all_gate, *down_y], [all_up, *d_joined_y[0], *d_rate_y[0]], [all_out]],
-    )
-    d_stream = d_hidden + d_part[:length]
-    d_gain_one = d_part[length]
-
-    (g_gate,) = finish(all_gate.value, core, 1)
-    (g_up,) = finish(all_up.value, core, 1)
-    (g_out,) = finish(all_out.value, core, 0)
-    (g_down,) = finish(sum((item.value for item in down_y), own_down.value), core, 1)
-    all_joined = total(own_joined.value, normed_pairs, cores(d_joined_y.all()))
-    g_query, g_key, g_value, g_gate_attn = finish(all_joined.value, core, 0, (span,) * 4)
-    g_rate = None
-    for pair, d in zip(normed_pairs, d_rate_y.all()):
-        part = product(jnp.concatenate([d, swap(d, "rows", 1)], 1), pair)
-        g_rate = part if g_rate is None else g_rate + part
-    ends = (g_rate, swap(g_rate, "rows", 1))
-    g_rate = jnp.where(core == 0, jnp.concatenate(ends, 1), jnp.concatenate(ends[::-1], 1))
-
     weights = valid_mask.reshape(-1).astype(f32)[:, None]
     stats = jnp.stack(
         [
@@ -901,7 +898,35 @@
         ]
         + [jnp.sum(weights) / lax.axis_size("heads")]
     )
-    stats = butterfly(stats, "heads")
+    late = []
+
+    def last_hook():
+        late.append(total(own_three.value, normed_pairs, cores(d_three_y.all())))
+        return [late[0], *d_rate_y[0]]
+
+    across_slabs = jnp.tile(jnp.pad(stats, (0, slab - stats.size)), width // slab)[None]
+    d_part = scatter_columns(
+        d_tokens,
+        jnp.concatenate([d_gain_one, across_slabs, pad[1:]], 0),
+        [[own_three], [all_gate, all_attn], [all_up, all_out, *d_three_y[0]], last_hook],
+    )
+    d_stream = d_hidden + d_part[:length]
+    d_gain_one = d_part[length]
+    stats = d_part[length + 1, : stats.size]
+
+    (g_gate,) = finish(all_gate.value, core, 1)
+    (g_up,) = finish(all_up.value, core, 1)
+    (g_out,) = finish(all_out.value, core, 0)
+    (g_down,) = finish(sum((item.value for item in down_y), own_down.value), core, 1)
+    (g_gate_attn,) = finish(all_attn.value, core, 0)
+    g_query, g_key, g_value = finish(late[0].value, core, 0, (span,) * 3)
+    g_rate = None
+    for pair, d in zip(normed_pairs, d_rate_y.all()):
+        part = product(jnp.concatenate([d, swap(d, "rows", 1)], 1), pair)
+        g_rate = part if g_rate is None else g_rate + part
+    ends = (g_rate, swap(g_rate, "rows", 1))
+    g_rate = jnp.where(core == 0, jnp.concatenate(ends, 1), jnp.concatenate(ends[::-1], 1))
+
     small = [
         d_gain_one, jnp.sum(d_rate_pre, 1), d_inner_weight, d_inner_bias, dg, dsh,
         d_post_gain, d_post_shift, d_gain_two, stats,

time: 797 us -> 740 us (0.928)
  waiting for transfers between devices: 347 us -> 261 us
  local copies, waits for them, and re-layouts: 93 us -> 115 us
    ppermute x46, waiting for transfers between devices: 182 us -> 118 us  [shift(): return lax.ppermute(value, 'heads', pairs)]
    ppermute x35, waiting for transfers between devices: 62.4 us -> 20.8 us  [swap(): lax.ppermute(value, axis, [(i, i ^ bit) for i in range(lax.axis_size(axis...]
    ppermute x18 -> x19, waiting for transfers between devices: 103 us -> 122 us  [row_shift(): lax.ppermute(value, 'rows', [(r, (r + 2 * step) % size) for r in range(si...]
    ppermute x18 -> x19, starting transfers between devices: 20.9 us -> 14.8 us  [row_shift(): lax.ppermute(value, 'rows', [(r, (r + 2 * step) % size) for r in range(si...]
    unnamed x205 -> x249, local copies, waits for them, and re-layouts: 21 us -> 26.4 us
    dot_general x9 -> x11, matrix products: 69.3 us -> 74.4 us  [left_product(): lax.dot_general(left, right, (((0,), (0,)), ((), ())), precision=lax.Prec...]
    pallas_call x5 -> x6, Pallas kernels: 24 us -> 26.5 us  [place(): pl.pallas_call(functools.partial(place_body, axis=axis, widths=widths), g...]
  transfers between devices with their start and end apart: 99 -> 100, of which waited for: 53 -> 48; matrix products, arithmetic and copies ran while one was open for 35% -> 38% of each run, Pallas kernels for 7% -> 8%
where the time goes in v5:
time: 740 us; the launch traced here: 732 us
  waiting for transfers between devices  261 us (35%)
  matrix products  154 us (21%)
  local copies, waits for them, and re-layouts  115 us (16%)
  starting transfers between devices  76.1 us (10%)
  Pallas kernels  61.2 us (8%)
  other arithmetic  59.7 us (8%)
    ppermute x19, waiting for transfers between devices, row_shift(): lax.ppermute(value, 'rows', [(r, (r + 2 * step) % size) for r in range(si...  122 us
    ppermute x46, waiting for transfers between devices, shift(): return lax.ppermute(value, 'heads', pairs)  118 us
    dot_general x11, matrix products, left_product(): lax.dot_general(left, right, (((0,), (0,)), ((), ())), precision=lax.Prec...  74.4 us
    ppermute x46, starting transfers between devices, shift(): return lax.ppermute(value, 'heads', pairs)  40.8 us
    dot_general x7, matrix products, product(): jnp.dot(left, right, precision=lax.Precision.HIGH, preferred_element_type...  40 us
    dot_general x5, matrix products, right_product(): lax.dot_general(left, right, (((1,), (1,)), ((), ())), precision=lax.Prec...  35.1 us
    dynamic_update_slice x22, local copies, waits for them, and re-layouts, gather_columns(): out = lax.dynamic_update_slice(out, item, (0, column))  31.8 us
    pallas_call x6, Pallas kernels, place(): pl.pallas_call(functools.partial(place_body, axis=axis, widths=widths), g...  26.5 us
  transfers between devices with their start and end apart: 100, of which 48 were waited for; matrix products, arithmetic and copies ran while one was open for 38% of the time, Pallas kernels for 8%

profile of v5, /device:TPU:0, one launch (start us, length us, event | category | flops | bytes accessed | tf_op | source)
XLA Modules:
  0.0 731.7 jit_solution(8240653985874056708)
XLA Ops:
  45.0 12.5 %fusion.24.joined = f32[512,1024]{1,0:T(8,128)} fusion(f32[2048,1024]{1,0:T(8,128)} %constant_dynamic-update-slice_fusion, f32[512,2048]{1,0:T(8,128)} %bitcast_multiply_fusion.3, f32[2048]{0:T(1024)S(1)} %bitcast.141), kind=kOutput, calls=%fused_computation.37 | convolution fusion | flops 6443499520 | bytes 14688256 | tf_op jit(solution)/shard_map/dot_general | solution.py:458
  76.2 12.8 %inner_forward.1 = (f32[512,256]{1,0:T(8,128)S(1)}, f32[256,512]{1,0:T(8,128)S(1)}, f32[256,512]{1,0:T(8,128)S(1)}, f32[4,256,128]{2,1,0:T(8,128)S(1)}, f32[4,256,1]{2,1,0:T(8,128)S(1)}) custom-call(f32[512,1024]{1,0:T(8,128)S(1)} %copy-done.2, f32[512,4]{1,0:T(8,128)S(1)} %copy-done.4, f32[4,512]{1,0:T(4,128)S(1)} %get-tuple-element.357.rate_t, ...), custom_call_target="tpu_custom_call" | custom-call | tf_op jit(solution)/shard_map/inner_forward/pallas_call | solution.py:182
  126.9 7.2 collective-permute-done.17
  152.4 10.6 %collective-permute-done.22 = f32[512,256]{1,0:T(8,128)S(1)} collective-permute-done((f32[512,256]{1,0:T(8,128)S(1)}, f32[512,256]{1,0:T(8,128)S(1)}, u32[]{:S(2)}, u32[]{:S(2)}) %collective-permute-start.22) | collective-permute-done | bytes 524320 | tf_op jit(solution)/shard_map/ppermute | solution.py:493
  187.9 7.7 %collective-permute-done.25 = f32[512,256]{1,0:T(8,128)S(1)} collective-permute-done((f32[512,256]{1,0:T(8,128)S(1)}, f32[512,256]{1,0:T(8,128)S(1)}, u32[]{:S(2)}, u32[]{:S(2)}) %collective-permute-start.25) | collective-permute-done | bytes 524320 | tf_op jit(solution)/shard_map/ppermute | solution.py:493
  230.5 8.1 %fusion.162 = f32[512,688]{0,1:T(8,128)S(1)} fusion(f32[512,2048]{1,0:T(8,128)} %constant_dynamic-update-slice_fusion.27, f32[688,2048]{1,0:T(8,128)} %param.42), kind=kOutput, calls=%fused_computation.353 | convolution fusion | flops 4328521728 | bytes 11239424 | tf_op jit(solution)/shard_map/dot_general | solution.py:469
  261.4 9.5 %collective-permute-done.35 = f32[256,1024]{1,0:T(8,128)S(1)} collective-permute-done((f32[256,1024]{1,0:T(8,128)S(1)}, f32[256,1024]{1,0:T(8,128)S(1)}, u32[]{:S(2)}, u32[]{:S(2)}) %collective-permute-start.35) | collective-permute-done | bytes 1048608 | tf_op jit(solution)/shard_map/ppermute | solution.py:502
  274.2 7.0 fusion.166
  289.1 8.0 %fusion.165 = f32[512,2048]{1,0:T(8,128)S(1)} fusion(f32[512,688]{0,1:T(8,128)} %get-tuple-element.315, f32[2048,688]{0,1:T(8,128)} %param.40), kind=kOutput, calls=%fused_computation.356 | convolution fusion | flops 4328521728 | bytes 11239424 | tf_op jit(solution)/shard_map/dot_general | solution.py:469
  307.2 21.4 %collective-permute-done.37 = f32[512,1024]{1,0:T(8,128)} collective-permute-done((f32[512,1024]{1,0:T(8,128)}, f32[512,1024]{1,0:T(8,128)}, u32[]{:S(2)}, u32[]{:S(2)}) %collective-permute-start.37) | collective-permute-done | bytes 2097184 | tf_op jit(solution)/shard_map/ppermute | solution.py:493
  351.7 15.4 %collective-permute-done.44 = f32[256,1024]{1,0:T(8,128)S(1)} collective-permute-done((f32[256,1024]{1,0:T(8,128)S(1)}, f32[256,1024]{1,0:T(8,128)S(1)}, u32[]{:S(2)}, u32[]{:S(2)}) %collective-permute-start.44) | collective-permute-done | bytes 1048608 | tf_op jit(solution)/shard_map/ppermute | solution.py:502
  367.3 22.3 %collective-permute-done.45 = f32[256,1024]{1,0:T(8,128)S(1)} collective-permute-done((f32[256,1024]{1,0:T(8,128)S(1)}, f32[256,1024]{1,0:T(8,128)S(1)}, u32[]{:S(2)}, u32[]{:S(2)}) %collective-permute-start.45) | collective-permute-done | bytes 1048608 | tf_op jit(solution)/shard_map/ppermute | solution.py:502
  396.5 7.7 %fusion.27 = f32[688,1024]{1,0:T(8,128)} fusion(f32[512,1024]{1,0:T(8,128)S(1)} %collective-permute-done.47, f32[512,1024]{1,0:T(8,128)S(1)} %get-tuple-element.297, f32[512,688]{0,1:T(8,128)S(1)} %collective-permute-done.49, f32[512,688]{0,1:T(8,128)} %get-tuple-element.315), kind=kOutput, calls=%fused_computation.40 | convolution fusion | flops 4330274816 | bytes 9830400 | tf_op jit(solution)/shard_map/dot_general | solution.py:462
  409.2 6.3 fusion.26
  431.5 9.4 %fusion = f32[688,1024]{1,0:T(8,128)} fusion(f32[512,1024]{1,0:T(8,128)} %collective-permute-done.58, f32[512,1024]{1,0:T(8,128)} %get-tuple-element.287, f32[512,688]{0,1:T(8,128)} %collective-permute-done.57, f32[512,688]{0,1:T(8,128)} %get-tuple-element.314), kind=kOutput, calls=%fused_computation.1 | convolution fusion | flops 4330274816 | bytes 9830400 | tf_op jit(solution)/shard_map/dot_general | solution.py:462
  441.1 24.3 %collective-permute-done.56 = f32[256,1024]{1,0:T(8,128)} collective-permute-done((f32[256,1024]{1,0:T(8,128)}, f32[256,1024]{1,0:T(8,128)}, u32[]{:S(2)}, u32[]{:S(2)}) %collective-permute-start.56) | collective-permute-done | bytes 1048608 | tf_op jit(solution)/shard_map/ppermute | solution.py:502
  468.3 11.2 %collective-permute-done.54 = f32[512,256]{1,0:T(8,128)S(1)} collective-permute-done((f32[512,256]{1,0:T(8,128)S(1)}, f32[512,256]{1,0:T(8,128)S(1)}, u32[]{:S(2)}, u32[]{:S(2)}) %collective-permute-start.54) | collective-permute-done | bytes 524320 | tf_op jit(solution)/shard_map/ppermute | solution.py:493
  499.6 6.7 collective-permute-done.66
  538.7 21.8 %inner_backward.1 = (f32[512,256]{1,0:T(8,128)S(1)}, f32[512,256]{1,0:T(8,128)S(1)}, f32[512,256]{1,0:T(8,128)S(1)}, f32[4,512]{1,0:T(4,128)S(1)}, f32[256,128]{...) custom-call(f32[512,1024]{1,0:T(8,128)} %fusion.24.joined, ...), custom_call_target="tpu_custom_call" | custom-call | tf_op jit(solution)/shard_map/inner_backward/pallas_call | solution.py:407
  567.3 18.3 %collective-permute-done.71 = f32[512,256]{1,0:T(8,128)S(1)} collective-permute-done((f32[512,256]{1,0:T(8,128)S(1)}, f32[512,256]{1,0:T(8,128)S(1)}, u32[]{:S(2)}, u32[]{:S(2)}) %collective-permute-start.71) | collective-permute-done | bytes 524320 | tf_op jit(solution)/shard_map/ppermute | solution.py:502
  592.0 10.0 %fusion.55 = f32[512,2048]{1,0:T(8,128)S(1)} fusion(f32[2048,1024]{1,0:T(8,128)} %constant_dynamic-update-slice_fusion, f32[512,256]{1,0:T(8,128)} %copy-done.65, f32[512,256]{1,0:T(8,128)S(1)} %get-tuple-element.202, f32[512,256]{1,0:T(8,128)S(1)} %get-tuple-element.201, f32[512,256]{1,0:T(8,128)S(1)} %get-tuple-element.200), kind=kOutput, calls=%fused_computation.72 | convolution fusion | flops 6444023808 | bytes 14680064 | tf_op jit(solution)/shard_map/dot_general | solution.py:469
  612.7 8.1 %fusion.28 = f32[1024,768]{1,0:T(8,128)S(1)} fusion(f32[512,768]{1,0:T(8,128)S(1)} %collective-permute-done.78, f32[512,768]{1,0:T(8,128)S(1)} %constant_dynamic-update-slice_fusion.4, f32[512,1024]{1,0:T(8,128)} %collective-permute-done.8, f32[512,1024]{1,0:T(8,128)S(1)} %copy-done.29, f32[1024]{0:T(1024)S(1)} %copy-done.83), kind=kOutput, calls=%fused_computation.42 | convolution fusion | flops 4834721792 | bytes 10489856 | tf_op jit(solution)/shard_map/dot_general | solution.py:462
  623.3 7.5 %fusion.45 = f32[688,1024]{1,0:T(8,128)S(1)} fusion(f32[1024,1024]{1,0:T(8,128)S(1)} %constant_dynamic-update-slice_fusion.7, f32[512,688]{0,1:T(8,128)} %collective-permute-done.80, f32[512,688]{0,1:T(8,128)} %collective-permute-done.60), kind=kOutput, calls=%fused_computation.60 | convolution fusion | flops 4329226240 | bytes 9830400 | tf_op jit(solution)/shard_map/dot_general | solution.py:462
  665.3 7.9 %fusion.32 = f32[1024,768]{1,0:T(8,128)S(1)} fusion(f32[512,768]{1,0:T(8,128)S(1)} %collective-permute-done.87, f32[512,768]{1,0:T(8,128)S(1)} %collective-permute-done.85, f32[256,1024]{1,0:T(8,128)S(1)} %copy-done.101, f32[256,1024]{1,0:T(8,128)} %collective-permute-done.9, f32[256,1024]{1,0:T(8,128)} %collective-permute-done.4, ...), kind=kOutput, calls=%fused_computation.46 | convolution fusion | flops 4836818944 | bytes 10489856 | tf_op jit(solution)/shard_map/dot_general | solution.py:462
  (635 shorter events, 445.3 us)
Async XLA Ops:
  0.7 56.8 %collective-permute-start.10 = (f32[512,256]{1,0:T(8,128)}, f32[512,256]{1,0:T(8,128)}, u32[]{:S(2)}, u32[]{:S(2)}) collective-permute-start(f32[512,256]{1,0:T(8,128)} %bitcast.137), channel_id=1, source_target_pairs={{0,1},{1,0},{2,3},{3,2},{4,5},{5,4},{6,7},{7,6},{8,9},{9,8},{10,11... | collective-permute-start | bytes 1572872 | tf_op jit(solution)/shard_map/ppermute | solution.py:493
  3.7 53.8 %collective-permute-start.11 = (f32[512,256]{1,0:T(8,128)}, f32[512,256]{1,0:T(8,128)}, u32[]{:S(2)}, u32[]{:S(2)}) collective-permute-start(f32[512,256]{1,0:T(8,128)} %bitcast.138), channel_id=1, source_target_pairs={{0,2},{1,3},{2,4},{3,5},{4,6},{5,7},{6,0},{7,1},{8,10},{9,11},{10,... | collective-permute-start | bytes 1572872 | tf_op jit(solution)/shard_map/ppermute | solution.py:493
  15.6 58.1 %collective-permute-start.3 = (f32[256,1024]{1,0:T(8,128)}, f32[256,1024]{1,0:T(8,128)}, u32[]{:S(2)}, u32[]{:S(2)}) collective-permute-start(f32[256,1024]{1,0:T(8,128)} %get-tuple-element.312), channel_id=1, source_target_pairs={{0,16},{8,24},{16,0},{24,8},{1,17},{9,25},{17,1},{25,9},{2,18},{10... | collective-permute-start | bytes 3145736 | tf_op jit(solution)/shard_map/ppermute | solution.py:502
  21.9 72.1 %collective-permute-start.8 = (f32[512,1024]{1,0:T(8,128)}, f32[512,1024]{1,0:T(8,128)}, u32[]{:S(2)}, u32[]{:S(2)}) collective-permute-start(f32[512,1024]{1,0:T(8,128)} %get-tuple-element.278), channel_id=1, source_target_pairs={{0,8},{8,0},{16,24},{24,16},{1,9},{9,1},{17,25},{25,17},{2,10},{10... | collective-permute-start | bytes 6291464 | tf_op jit(solution)/shard_map/ppermute | solution.py:497
  44.4 47.9 %collective-permute-start.4 = (f32[256,1024]{1,0:T(8,128)}, f32[256,1024]{1,0:T(8,128)}, u32[]{:S(2)}, u32[]{:S(2)}) collective-permute-start(f32[256,1024]{1,0:T(8,128)} %get-tuple-element.311), channel_id=1, source_target_pairs={{0,16},{8,24},{16,0},{24,8},{1,17},{9,25},{17,1},{25,9},{2,18},{10... | collective-permute-start | bytes 3145736 | tf_op jit(solution)/shard_map/ppermute | solution.py:502
  209.5 36.3 %collective-permute-start.34 = (f32[512,1024]{1,0:T(8,128)}, f32[512,1024]{1,0:T(8,128)}, u32[]{:S(2)}, u32[]{:S(2)}) collective-permute-start(f32[512,1024]{1,0:T(8,128)} %get-tuple-element.282), channel_id=1, source_target_pairs={{0,8},{8,0},{16,24},{24,16},{1,9},{9,1},{17,25},{25,17},{2,10},{10... | collective-permute-start | bytes 6291464 | tf_op jit(solution)/shard_map/ppermute | solution.py:497
  284.5 44.1 %collective-permute-start.37 = (f32[512,1024]{1,0:T(8,128)}, f32[512,1024]{1,0:T(8,128)}, u32[]{:S(2)}, u32[]{:S(2)}) collective-permute-start(f32[512,1024]{1,0:T(8,128)} %pad_maximum_fusion.3), channel_id=1, source_target_pairs={{0,1},{1,0},{2,3},{3,2},{4,5},{5,4},{6,7},{7,6},{8,9},{9,8},{10,11... | collective-permute-start | bytes 6291464 | tf_op jit(solution)/shard_map/ppermute | solution.py:493
  289.0 61.4 %collective-permute-start.47 = (f32[512,1024]{1,0:T(8,128)S(1)}, f32[512,1024]{1,0:T(8,128)S(1)}, u32[]{:S(2)}, u32[]{:S(2)}) collective-permute-start(f32[512,1024]{1,0:T(8,128)S(1)} %get-tuple-element.298), channel_id=1, source_target_pairs={{0,8},{8,0},{16,24},{24,16},{1,9},{9,1},{17,25},{25,17},{2,10},{10... | collective-permute-start | bytes 6291464 | tf_op jit(solution)/shard_map/ppermute | solution.py:497
  341.2 48.4 %collective-permute-start.45 = (f32[256,1024]{1,0:T(8,128)S(1)}, f32[256,1024]{1,0:T(8,128)S(1)}, u32[]{:S(2)}, u32[]{:S(2)}) collective-permute-start(f32[256,1024]{1,0:T(8,128)S(1)} %get-tuple-element.299), channel_id=1, source_target_pairs={{0,16},{8,24},{16,0},{24,8},{1,17},{9,25},{17,1},{25,9},{2,18},{10... | collective-permute-start | bytes 3145736 | tf_op jit(solution)/shard_map/ppermute | solution.py:502
  345.3 50.9 %collective-permute-start.49 = (f32[512,688]{0,1:T(8,128)}, f32[512,688]{0,1:T(8,128)S(1)}, u32[]{:S(2)}, u32[]{:S(2)}) collective-permute-start(f32[512,688]{0,1:T(8,128)} %get-tuple-element.315), channel_id=1, source_target_pairs={{0,8},{8,0},{16,24},{24,16},{1,9},{9,1},{17,25},{25,17},{2,10},{10... | collective-permute-start | bytes 4227080 | tf_op jit(solution)/shard_map/ppermute | solution.py:497
  348.7 40.9 %collective-permute-start.40 = (f32[520,256]{1,0:T(8,128)S(1)}, f32[520,256]{1,0:T(8,128)S(1)}, u32[]{:S(2)}, u32[]{:S(2)}) collective-permute-start(f32[520,256]{1,0:T(8,128)S(1)} %pad_maximum_fusion.6), channel_id=1, source_target_pairs={{0,1},{1,0},{2,3},{3,2},{4,5},{5,4},{6,7},{7,6},{8,9},{9,8},{10,11... | collective-permute-start | bytes 1597448 | tf_op jit(solution)/shard_map/ppermute | solution.py:493
  350.4 40.7 %collective-permute-start.43 = (f32[520,256]{1,0:T(8,128)S(1)}, f32[520,256]{1,0:T(8,128)S(1)}, u32[]{:S(2)}, u32[]{:S(2)}) collective-permute-start(f32[520,256]{1,0:T(8,128)S(1)} %maximum_add_fusion.4), channel_id=1, source_target_pairs={{0,2},{1,3},{2,4},{3,5},{4,6},{5,7},{6,0},{7,1},{8,10},{9,11},{10,... | collective-permute-start | bytes 1597448 | tf_op jit(solution)/shard_map/ppermute | solution.py:493
  367.1 39.4 %collective-permute-start.48 = (f32[256,1024]{1,0:T(8,128)S(1)}, f32[256,1024]{1,0:T(8,128)S(1)}, u32[]{:S(2)}, u32[]{:S(2)}) collective-permute-start(f32[256,1024]{1,0:T(8,128)S(1)} %get-tuple-element.318), channel_id=1, source_target_pairs={{0,16},{8,24},{16,0},{24,8},{1,17},{9,25},{17,1},{25,9},{2,18},{10... | collective-permute-start | bytes 3145736 | tf_op jit(solution)/shard_map/ppermute | solution.py:502
  408.8 59.5 %collective-permute-start.60 = (f32[512,688]{0,1:T(8,128)}, f32[512,688]{0,1:T(8,128)}, u32[]{:S(2)}, u32[]{:S(2)}) collective-permute-start(f32[512,688]{0,1:T(8,128)} %get-tuple-element.315), channel_id=1, source_target_pairs={{0,16},{8,24},{16,0},{24,8},{1,17},{9,25},{17,1},{25,9},{2,18},{10... | collective-permute-start | bytes 4227080 | tf_op jit(solution)/shard_map/ppermute | solution.py:502
  418.6 46.8 %collective-permute-start.56 = (f32[256,1024]{1,0:T(8,128)}, f32[256,1024]{1,0:T(8,128)}, u32[]{:S(2)}, u32[]{:S(2)}) collective-permute-start(f32[256,1024]{1,0:T(8,128)} %get-tuple-element.317), channel_id=1, source_target_pairs={{0,16},{8,24},{16,0},{24,8},{1,17},{9,25},{17,1},{25,9},{2,18},{10... | collective-permute-start | bytes 3145736 | tf_op jit(solution)/shard_map/ppermute | solution.py:502
  431.4 64.1 %collective-permute-start.63 = (f32[512,688]{0,1:T(8,128)}, f32[512,688]{0,1:T(8,128)S(1)}, u32[]{:S(2)}, u32[]{:S(2)}) collective-permute-start(f32[512,688]{0,1:T(8,128)} %get-tuple-element.316), channel_id=1, source_target_pairs={{0,16},{8,24},{16,0},{24,8},{1,17},{9,25},{17,1},{25,9},{2,18},{10... | collective-permute-start | bytes 4227080 | tf_op jit(solution)/shard_map/ppermute | solution.py:502
  514.6 71.0 %collective-permute-start.70 = (f32[688,1024]{1,0:T(8,128)}, f32[688,1024]{1,0:T(8,128)}, u32[]{:S(2)}, u32[]{:S(2)}) collective-permute-start(f32[688,1024]{1,0:T(8,128)} %fusion), channel_id=1, source_target_pairs={{0,16},{8,24},{16,0},{24,8},{1,17},{9,25},{17,1},{25,9},{2,18},{10... | collective-permute-start | bytes 8454152 | tf_op jit(solution)/shard_map/ppermute | solution.py:502
  526.0 96.8 %collective-permute-start.80 = (f32[512,688]{0,1:T(8,128)}, f32[512,688]{0,1:T(8,128)}, u32[]{:S(2)}, u32[]{:S(2)}) collective-permute-start(f32[512,688]{0,1:T(8,128)} %collective-permute-done.60), channel_id=1, source_target_pairs={{0,8},{8,0},{16,24},{24,16},{1,9},{9,1},{17,25},{25,17},{2,10},{10... | collective-permute-start | bytes 4227080 | tf_op jit(solution)/shard_map/ppermute | solution.py:497
  536.5 49.1 %collective-permute-start.71 = (f32[512,256]{1,0:T(8,128)S(1)}, f32[512,256]{1,0:T(8,128)S(1)}, u32[]{:S(2)}, u32[]{:S(2)}) collective-permute-start(f32[512,256]{1,0:T(8,128)S(1)} %get-tuple-element.313), channel_id=1, source_target_pairs={{0,16},{8,24},{16,0},{24,8},{1,17},{9,25},{17,1},{25,9},{2,18},{10... | collective-permute-start | bytes 1572872 | tf_op jit(solution)/shard_map/ppermute | solution.py:502
  610.7 43.2 %collective-permute-start.83 = (f32[512,688]{0,1:T(8,128)S(1)}, f32[512,688]{0,1:T(8,128)S(1)}, u32[]{:S(2)}, u32[]{:S(2)}) collective-permute-start(f32[512,688]{0,1:T(8,128)S(1)} %copy-done.54), channel_id=1, source_target_pairs={{0,8},{8,0},{16,24},{24,16},{1,9},{9,1},{17,25},{25,17},{2,10},{10... | collective-permute-start | bytes 4227080 | tf_op jit(solution)/shard_map/ppermute | solution.py:497
  611.0 49.9 %collective-permute-start.85 = (f32[512,768]{1,0:T(8,128)S(1)}, f32[512,768]{1,0:T(8,128)S(1)}, u32[]{:S(2)}, u32[]{:S(2)}) collective-permute-start(f32[512,768]{1,0:T(8,128)S(1)} %constant_dynamic-update-slice_fusion.4), channel_id=1, source_target_pairs={{0,16},{8,24},{16,0},{24,8},{1,17},{9,25},{17,1},{25,9},{2,18},{10... | collective-permute-start | bytes 4718600 | tf_op jit(solution)/shard_map/ppermute | solution.py:502
  679.6 45.9 %collective-permute-start.91 = (f32[1024,768]{1,0:T(8,128)}, f32[1024,768]{1,0:T(8,128)}, u32[]{:S(2)}, u32[]{:S(2)}) collective-permute-start(f32[1024,768]{1,0:T(8,128)} %add.686.own), channel_id=1, source_target_pairs={{0,8},{8,0},{16,24},{24,16},{1,9},{9,1},{17,25},{25,17},{2,10},{10... | collective-permute-start | bytes 9437192 | tf_op jit(solution)/shard_map/ppermute | solution.py:497
  680.2 36.8 %collective-permute-start.97 = (f32[688,1024]{1,0:T(8,128)S(1)}, f32[688,1024]{1,0:T(8,128)}, u32[]{:S(2)}, u32[]{:S(2)}) collective-permute-start(f32[688,1024]{1,0:T(8,128)S(1)} %add.678.own), channel_id=1, source_target_pairs={{0,8},{8,0},{16,24},{24,16},{1,9},{9,1},{17,25},{25,17},{2,10},{10... | collective-permute-start | bytes 8454152 | tf_op jit(solution)/shard_map/ppermute | solution.py:497
  680.7 40.6 %collective-permute-start.98 = (f32[688,1024]{1,0:T(8,128)}, f32[688,1024]{1,0:T(8,128)}, u32[]{:S(2)}, u32[]{:S(2)}) collective-permute-start(f32[688,1024]{1,0:T(8,128)} %add.682.own), channel_id=1, source_target_pairs={{0,8},{8,0},{16,24},{24,16},{1,9},{9,1},{17,25},{25,17},{2,10},{10... | collective-permute-start | bytes 8454152 | tf_op jit(solution)/shard_map/ppermute | solution.py:497
  (196 other events, 3170.4 us)

commit v6 on v5

--- a/solution.py
+++ b/solution.py
@@ -663,12 +663,12 @@
 
 
 class Along:
-    def __init__(self, value, parts=4):
-        size = value.shape[0] // parts
+    def __init__(self, value, parts=4, axis=0):
         self.own = value
+        self.axis = axis
+        pieces = jnp.split(value, parts, axis)
         self.steps = [
-            [Held(row_shift(value[i * size : (i + 1) * size], step)) for i in range(parts)]
-            for step in range(1, chips_along())
+            [Held(row_shift(piece, step)) for piece in pieces] for step in range(1, chips_along())
         ]
 
     def __getitem__(self, i):
@@ -677,7 +677,7 @@
     def all(self):
         return [self.own] + [
             step[0].value if len(step) == 1
-            else jnp.concatenate([item.value for item in step], 0)
+            else jnp.concatenate([item.value for item in step], self.axis)
             for step in self.steps
         ]
 
@@ -764,16 +764,16 @@
     shaped = centered * post_gain + post_shift
     gate_act, gate_slope = gelu_parts(gate_pre)
     gathered = gather_columns(gate_act * shaped, [(), unit_y[3]])
-    gathered_y = Along(tokens_half(gathered, core))
+    gathered_pair = tokens_half(gathered, core)
     attn = product(gathered, w_out)
     stream_cols = lax.dynamic_slice_in_dim(tokens, column, slab, 1)
     hidden = stream_cols + attn
-    whole = gather_columns(hidden, [(), gathered_y[0], gathered_y[1]])
+    whole = gather_columns(hidden)
     dy_full = dy_held.value
 
     r2 = lax.rsqrt(jnp.mean(whole * whole, -1, keepdims=True) + epsilon)
     hnorm = whole * r2 * gain_two
-    hnorm_y = Along(tokens_half(hnorm, core))
+    hnorm_y = Along(tokens_half(hnorm, core), 8)
     a = product(hnorm, w_gate)
     c = product(hnorm, w_up)
     act, slope = silu_parts(a)
@@ -782,30 +782,32 @@
     deep, across = heads_grid()
     z, x = heads_place()
 
-    def tile_set(dx):
-        return jnp.concatenate(
-            [
-                lax.dynamic_slice_in_dim(
-                    ffn_part, (i * across + (x - dx) % across) * slab, slab, 1
-                )
-                for i in range(deep)
-            ],
-            1,
-        )
-
-    ffn_x = [Held(shift(tile_set(dx), 0, dx)) for dx in range(1, across)]
-    dm = meet_one(right_product(dy_full, w_down), *gathered_y[2])
-    da = dm * c * slope
+    def ffn_piece(dz, dx):
+        place_of = (z - dz) % deep * across + (x - dx) % across
+        return lax.dynamic_slice_in_dim(ffn_part, place_of * slab, slab, 1)
+
+    ffn_x = [
+        [Held(shift(ffn_piece(dz, dx), 0, dx)) for dx in range(1, across)] for dz in range(deep)
+    ]
+    dm = right_product(dy_full, w_down)
+    da = meet_one(dm * c * slope, *ffn_x[1 % deep])
     dc = dm * act
-    da_y, dc_y = Along(da, 1), Along(dc, 1)
-    dhnorm = right_product(da, w_gate) + right_product(dc, w_up)
-    dhnorm = meet_one(dhnorm, *gathered_y[3], *ffn_x)
-    ffn_sum = tile_set(0)
-    for item in ffn_x:
-        ffn_sum = ffn_sum + item.value
+    da_y, dc_y = Along(da, 2), Along(dc, 2)
+    dhnorm = meet_one(right_product(da, w_gate), *ffn_x[2 % deep], *hnorm_y[0])
+    dhnorm = dhnorm + right_product(dc, w_up)
+    dhnorm = meet_one(dhnorm, *hnorm_y[1], *ffn_x[3 % deep])
 
     def ffn_tile(dz):
-        return lax.dynamic_slice_in_dim(ffn_sum, (z - dz) % deep * slab, slab, 1)
+        out = ffn_piece(dz, 0)
+        for item in ffn_x[dz]:
+            out = out + item.value
+        return out
+
+    ffn_steps = []
+
+    def ffn_step(dz):
+        ffn_steps.append(Held(shift(ffn_steps[-1].value + ffn_tile(dz) if ffn_steps else ffn_tile(dz), 1, 0)))
+        return ffn_steps[-1]
 
     d_gain_two = jnp.sum(dhnorm * whole * r2, 0, keepdims=True)
     weighted = dhnorm * gain_two
@@ -817,29 +819,55 @@
     own_gate = Held(left_product(da_pair, hnorm_y.own))
     own_up = Held(left_product(dc_pair, hnorm_y.own))
     own_down = Held(left_product(both_cores(m), tokens_half(dy_full, core)))
-    ffn_step = Held(shift(ffn_tile(1), 1, 0))
     d_part = scatter_columns(
         d_whole,
         jnp.concatenate([d_gain_two, pad], 0),
-        [[ffn_step], [*hnorm_y[0], *hnorm_y[1]], [*hnorm_y[2], own_gate], [own_up]],
+        [
+            [*ffn_x[0], *hnorm_y[2], *hnorm_y[3]],
+            [*hnorm_y[4], *hnorm_y[5], own_down],
+            lambda: [*hnorm_y[6], own_gate, ffn_step(1)],
+            [*hnorm_y[7], *da_y[0], own_up],
+        ],
     )
     d_hidden = grad_output + d_part[:length]
     d_gain_two = d_part[length]
-    d_hidden_y = Along(d_hidden, 1)
-    own_out = Held(left_product(gathered_y.own, both_cores(d_hidden)))
-    ffn_step = Held(shift(ffn_step.value + ffn_tile(2 % deep), 1, 0) if deep > 2 else ffn_step.value)
+    own_out = Held(left_product(gathered_pair, both_cores(d_hidden)))
+    down_y = Along(own_down.value, 4, 1)
+    late = {}
+
+    def cores(values):
+        return [both_cores(value) for value in values]
+
+    def total(name, own, lefts, rights):
+        for left, right in zip(lefts[1:], rights[1:]):
+            own = own + left_product(left, right)
+        late[name] = Held(own)
+        return late[name]
+
+    def placed(name, value, axis, widths=None):
+        late[name] = [Held(item) for item in finish(value, core, axis, widths)]
+        return late[name]
 
     d_gated = scatter_columns(
         right_product(d_hidden, w_out),
         None,
-        [[*hnorm_y[3], own_down], [*da_y[0], ffn_step], [*dc_y[0], own_out], [*d_hidden_y[0]]],
-    )
-    d_gated = meet_one(d_gated, own_down)
-    down_y = [Held(item) for item in other_chips(own_down.value)]
-    ffn = ffn_step.value
+        [
+            lambda: [*da_y[1], *down_y[0], *([ffn_step(2)] if deep > 2 else [])],
+            [*dc_y[0], *down_y[1], own_out],
+            lambda: [
+                *dc_y[1], *down_y[2],
+                total("gate", own_gate.value, cores(da_y.all()), hnorm_y.all()),
+            ],
+            lambda: [
+                *down_y[3],
+                total("up", own_up.value, cores(dc_y.all()), hnorm_y.all()),
+            ],
+        ],
+    )
+    out_y = Along(own_out.value, 1)
     for dz in range(3, deep):
-        ffn = shift(ffn + ffn_tile(dz), 1, 0)
-    ffn = Held(ffn + ffn_tile(0))
+        ffn_step(dz)
+    ffn = Held(ffn_steps[-1].value + ffn_tile(0))
     d_shaped = d_gated * gate_act
     d_gate_pre = d_gated * shaped * gate_slope
     d_post_gain = jnp.sum(d_shaped * centered, 0)
@@ -859,7 +887,7 @@
     dq, dk, dv, d_rate, dw, db, dg, dsh = ttt_backward(
         joined, rate_t, seg, seg_t, w0, b0, gain_col, shift_col, saved, d_mixed, hd, heads
     )
-    dq = meet_one(dq, *down_y, *d_gate_y[0], own_attn, ffn)
+    dq = meet_one(dq, *out_y[0], *d_gate_y[0], own_attn, ffn)
     output = hidden + ffn.value
     ffn = ffn.value
     d_inner_weight, d_inner_bias = state_back(dw, db, heads, hd)
@@ -877,19 +905,7 @@
         tokens * weighted, -1, keepdims=True
     )
 
-    def cores(values):
-        return [both_cores(value) for value in values]
-
-    def total(own, lefts, rights):
-        for left, right in zip(lefts[1:], rights[1:]):
-            own = own + left_product(left, right)
-        return Held(own)
-
     own_three = Held(left_product(normed_pairs[0], both_cores(d_three)))
-    all_attn = total(own_attn.value, normed_pairs, cores(d_gate_y.all()))
-    all_gate = total(own_gate.value, cores(da_y.all()), hnorm_y.all())
-    all_up = total(own_up.value, cores(dc_y.all()), hnorm_y.all())
-    all_out = total(own_out.value, gathered_y.all(), cores(d_hidden_y.all()))
     weights = valid_mask.reshape(-1).astype(f32)[:, None]
     stats = jnp.stack(
         [
@@ -898,32 +914,47 @@
         ]
         + [jnp.sum(weights) / lax.axis_size("heads")]
     )
-    late = []
-
-    def last_hook():
-        late.append(total(own_three.value, normed_pairs, cores(d_three_y.all())))
-        return [late[0], *d_rate_y[0]]
-
+    def rate_total():
+        out = None
+        for pair, d in zip(normed_pairs, d_rate_y.all()):
+            part = product(jnp.concatenate([d, swap(d, "rows", 1)], 1), pair)
+            out = part if out is None else out + part
+        late["rate"] = Held(out)
+        return late["rate"]
+
+    hooks = [
+        lambda: [own_three, *placed("g_gate", late["gate"].value, 1)],
+        lambda: [
+            total("attn", own_attn.value, normed_pairs, cores(d_gate_y.all())),
+            *placed("g_up", late["up"].value, 1),
+        ],
+        lambda: [
+            *d_three_y[0], *d_rate_y[0],
+            *placed("g_down", sum(down_y.all()), 1),
+            *placed("g_out", sum(out_y.all()), 0),
+        ],
+        lambda: [
+            total("three", own_three.value, normed_pairs, cores(d_three_y.all())),
+            *placed("g_attn", late["attn"].value, 0),
+            rate_total(),
+        ],
+    ]
     across_slabs = jnp.tile(jnp.pad(stats, (0, slab - stats.size)), width // slab)[None]
     d_part = scatter_columns(
         d_tokens,
         jnp.concatenate([d_gain_one, across_slabs, pad[1:]], 0),
-        [[own_three], [all_gate, all_attn], [all_up, all_out, *d_three_y[0]], last_hook],
+        hooks,
     )
     d_stream = d_hidden + d_part[:length]
     d_gain_one = d_part[length]
     stats = d_part[length + 1, : stats.size]
 
-    (g_gate,) = finish(all_gate.value, core, 1)
-    (g_up,) = finish(all_up.value, core, 1)
-    (g_out,) = finish(all_out.value, core, 0)
-    (g_down,) = finish(sum((item.value for item in down_y), own_down.value), core, 1)
-    (g_gate_attn,) = finish(all_attn.value, core, 0)
-    g_query, g_key, g_value = finish(late[0].value, core, 0, (span,) * 3)
-    g_rate = None
-    for pair, d in zip(normed_pairs, d_rate_y.all()):
-        part = product(jnp.concatenate([d, swap(d, "rows", 1)], 1), pair)
-        g_rate = part if g_rate is None else g_rate + part
+    ((g_gate,), (g_up,), (g_down,), (g_out,), (g_gate_attn,)) = (
+        [item.value for item in late[name]]
+        for name in ("g_gate", "g_up", "g_down", "g_out", "g_attn")
+    )
+    g_query, g_key, g_value = finish(late["three"].value, core, 0, (span,) * 3)
+    g_rate = late["rate"].value
     ends = (g_rate, swap(g_rate, "rows", 1))
     g_rate = jnp.where(core == 0, jnp.concatenate(ends, 1), jnp.concatenate(ends[::-1], 1))
 

time: 740 us -> 715 us (0.966)
  matrix products: 154 us -> 139 us
  local copies, waits for them, and re-layouts: 115 us -> 105 us
  starting transfers between devices: 76.1 us -> 85.6 us
    ppermute x46 -> x49, waiting for transfers between devices: 118 us -> 140 us  [shift(): return lax.ppermute(value, 'heads', pairs)]
    ppermute x19 -> x24, waiting for transfers between devices: 122 us -> 105 us  [row_shift(): lax.ppermute(value, 'rows', [(r, (r + 2 * step) % size) for r in range(si...]
    slice x7 -> x1, local copies, waits for them, and re-layouts: 13.3 us -> 0.07 us  [the longest x6 13.2 us: __init__(): value[i * size:(i + 1) * size]]
    dot_general x11 -> x10, matrix products: 74.4 us -> 61.1 us  [left_product(): lax.dot_general(left, right, (((0,), (0,)), ((), ())), precision=lax.Prec...]
    ppermute x19 -> x24, starting transfers between devices: 14.8 us -> 25.9 us  [row_shift(): lax.ppermute(value, 'rows', [(r, (r + 2 * step) % size) for r in range(si...]
    split x0 -> x7, local copies, waits for them, and re-layouts: none -> 9.77 us  [__init__(): pieces = jnp.split(value, parts, axis)]
    ppermute x35 -> x34, waiting for transfers between devices: 20.8 us -> 14.4 us  [swap(): lax.ppermute(value, axis, [(i, i ^ bit) for i in range(lax.axis_size(axis...]
    ppermute x35 -> x34, starting transfers between devices: 20.5 us -> 17.9 us  [swap(): lax.ppermute(value, axis, [(i, i ^ bit) for i in range(lax.axis_size(axis...]
  transfers between devices with their start and end apart: 100 -> 107, of which waited for: 48 -> 45; matrix products, arithmetic and copies ran while one was open for 38% -> 38% of each run, Pallas kernels for 8% -> 7%
where the time goes in v6:
time: 715 us; the launch traced here: 707 us
  waiting for transfers between devices  259 us (36%)
  matrix products  139 us (19%)
  local copies, waits for them, and re-layouts  105 us (15%)
  starting transfers between devices  85.6 us (12%)
  Pallas kernels  58.2 us (8%)
  other arithmetic  55.8 us (8%)
    ppermute x49, waiting for transfers between devices, shift(): return lax.ppermute(value, 'heads', pairs)  140 us
    ppermute x24, waiting for transfers between devices, row_shift(): lax.ppermute(value, 'rows', [(r, (r + 2 * step) % size) for r in range(si...  105 us
    dot_general x10, matrix products, left_product(): lax.dot_general(left, right, (((0,), (0,)), ((), ())), precision=lax.Prec...  61.1 us
    ppermute x49, starting transfers between devices, shift(): return lax.ppermute(value, 'heads', pairs)  41.8 us
    dot_general x7, matrix products, product(): jnp.dot(left, right, precision=lax.Precision.HIGH, preferred_element_type...  40.4 us
    dot_general x5, matrix products, right_product(): lax.dot_general(left, right, (((1,), (1,)), ((), ())), precision=lax.Prec...  33 us
    dynamic_update_slice x22, local copies, waits for them, and re-layouts, gather_columns(): out = lax.dynamic_update_slice(out, item, (0, column))  30.8 us
    unnamed x221, local copies, waits for them, and re-layouts  26.8 us
  transfers between devices with their start and end apart: 107, of which 45 were waited for; matrix products, arithmetic and copies ran while one was open for 38% of the time, Pallas kernels for 7%

profile of v6, /device:TPU:0, one launch (start us, length us, event | category | flops | bytes accessed | tf_op | source)
XLA Modules:
  0.0 707.2 jit_solution(5789017644896488411)
XLA Ops:
  45.1 12.5 %fusion.16.joined = f32[512,1024]{1,0:T(8,128)} fusion(f32[2048,1024]{1,0:T(8,128)} %constant_dynamic-update-slice_fusion, f32[512,2048]{1,0:T(8,128)} %bitcast_multiply_fusion.3, f32[2048]{0:T(1024)S(1)} %bitcast.139), kind=kOutput, calls=%fused_computation.29 | convolution fusion | flops 6443499520 | bytes 14688256 | tf_op jit(solution)/shard_map/dot_general | solution.py:458
  76.4 13.0 %inner_forward.1 = (f32[512,256]{1,0:T(8,128)S(1)}, f32[256,512]{1,0:T(8,128)S(1)}, f32[256,512]{1,0:T(8,128)S(1)}, f32[4,256,128]{2,1,0:T(8,128)S(1)}, f32[4,256,1]{2,1,0:T(8,128)S(1)}) custom-call(f32[512,1024]{1,0:T(8,128)S(1)} %copy-done.2, f32[512,4]{1,0:T(8,128)S(1)} %copy-done.5, f32[4,512]{1,0:T(4,128)S(1)} %get-tuple-element.386.rate_t, ...), custom_call_target="tpu_custom_call" | custom-call | tf_op jit(solution)/shard_map/inner_forward/pallas_call | solution.py:182
  127.3 7.2 %collective-permute-done.17 = f32[512,256]{1,0:T(8,128)S(1)} collective-permute-done((f32[512,256]{1,0:T(8,128)S(1)}, f32[512,256]{1,0:T(8,128)S(1)}, u32[]{:S(2)}, u32[]{:S(2)}) %collective-permute-start.17) | collective-permute-done | bytes 524320 | tf_op jit(solution)/shard_map/ppermute | solution.py:493
  152.9 10.6 %collective-permute-done.22 = f32[512,256]{1,0:T(8,128)S(1)} collective-permute-done((f32[512,256]{1,0:T(8,128)S(1)}, f32[512,256]{1,0:T(8,128)S(1)}, u32[]{:S(2)}, u32[]{:S(2)}) %collective-permute-start.22) | collective-permute-done | bytes 524320 | tf_op jit(solution)/shard_map/ppermute | solution.py:493
  184.0 12.0 %collective-permute-done.25 = f32[512,256]{1,0:T(8,128)S(1)} collective-permute-done((f32[512,256]{1,0:T(8,128)S(1)}, f32[512,256]{1,0:T(8,128)S(1)}, u32[]{:S(2)}, u32[]{:S(2)}) %collective-permute-start.25) | collective-permute-done | bytes 524320 | tf_op jit(solution)/shard_map/ppermute | solution.py:493
  205.0 10.9 %collective-permute-done.27 = f32[512,256]{1,0:T(8,128)S(1)} collective-permute-done((f32[512,256]{1,0:T(8,128)S(1)}, f32[512,256]{1,0:T(8,128)S(1)}, u32[]{:S(2)}, u32[]{:S(2)}) %collective-permute-start.27) | collective-permute-done | bytes 524320 | tf_op jit(solution)/shard_map/ppermute | solution.py:493
  221.9 10.8 %collective-permute-done.29 = f32[512,256]{1,0:T(8,128)} collective-permute-done((f32[512,256]{1,0:T(8,128)S(1)}, f32[512,256]{1,0:T(8,128)}, u32[]{:S(2)}, u32[]{:S(2)}) %collective-permute-start.29) | collective-permute-done | bytes 524320 | tf_op jit(solution)/shard_map/ppermute | solution.py:493
  261.5 9.2 %fusion.110 = (f32[512,688]{0,1:T(8,128)S(1)}, f32[512,688]{0,1:T(8,128)}, f32[512,688]{0,1:T(8,128)}) fusion(f32[512,688]{0,1:T(8,128)S(1)} %fusion.156, f32[512,688]{0,1:T(8,128)S(1)} %fusion.155, f32[512,2048]{1,0:T(8,128)} %constant_dynamic-update-slice_fusion.31, f32[688,2048]{1,0:T(8,128)S(1)} %bitcast.127), kind=kOutput, calls=%fused_computation.161 | convolution fusion | flops 4332748800 | bytes 16875520 | tf_op jit(solution)/shard_map/dot_general | solution.py:469
  270.7 7.3 %fusion.157 = f32[512,2048]{1,0:T(8,128)S(1)} fusion(f32[512,688]{0,1:T(8,128)} %get-tuple-element.341, f32[688,2048]{1,0:T(8,128)S(1)} %bitcast.127), kind=kOutput, calls=%fused_computation.347 | convolution fusion | flops 4328521728 | bytes 11239424 | tf_op jit(solution)/shard_map/dot_general | solution.py:458
  301.5 6.8 collective-permute-done.33
  336.8 14.6 %collective-permute-done.41 = f32[512,256]{1,0:T(8,128)S(1)} collective-permute-done((f32[512,256]{1,0:T(8,128)S(1)}, f32[512,256]{1,0:T(8,128)S(1)}, u32[]{:S(2)}, u32[]{:S(2)}) %collective-permute-start.41) | collective-permute-done | bytes 524320 | tf_op jit(solution)/shard_map/ppermute | solution.py:493
  356.4 9.6 %collective-permute-done.39 = f32[520,256]{1,0:T(8,128)S(1)} collective-permute-done((f32[520,256]{1,0:T(8,128)S(1)}, f32[520,256]{1,0:T(8,128)S(1)}, u32[]{:S(2)}, u32[]{:S(2)}) %collective-permute-start.39) | collective-permute-done | bytes 532512 | tf_op jit(solution)/shard_map/ppermute | solution.py:493
  368.6 6.8 fusion
  402.6 9.3 %collective-permute-done.56 = f32[256,688]{0,1:T(8,128)S(1)} collective-permute-done((f32[256,688]{0,1:T(8,128)S(1)}, f32[256,688]{0,1:T(8,128)S(1)}, u32[]{:S(2)}, u32[]{:S(2)}) %collective-permute-start.56) | collective-permute-done | bytes 704544 | tf_op jit(solution)/shard_map/ppermute | solution.py:502
  414.0 9.2 %collective-permute-done.55 = f32[128,1024]{1,0:T(8,128)S(1)} collective-permute-done((f32[128,1024]{1,0:T(8,128)}, f32[128,1024]{1,0:T(8,128)S(1)}, u32[]{:S(2)}, u32[]{:S(2)}) %collective-permute-start.55) | collective-permute-done | bytes 524320 | tf_op jit(solution)/shard_map/ppermute | solution.py:502
  426.9 11.4 %collective-permute-done.62 = f32[256,688]{0,1:T(8,128)S(1)} collective-permute-done((f32[256,688]{0,1:T(8,128)}, f32[256,688]{0,1:T(8,128)S(1)}, u32[]{:S(2)}, u32[]{:S(2)}) %collective-permute-start.62) | collective-permute-done | bytes 704544 | tf_op jit(solution)/shard_map/ppermute | solution.py:502
  438.6 14.7 %collective-permute-done.63 = f32[688,256]{1,0:T(8,128)S(1)} collective-permute-done((f32[688,256]{1,0:T(8,128)S(1)}, f32[688,256]{1,0:T(8,128)S(1)}, u32[]{:S(2)}, u32[]{:S(2)}) %collective-permute-start.63) | collective-permute-done | bytes 704544 | tf_op jit(solution)/shard_map/ppermute | solution.py:502
  468.8 14.7 %collective-permute-done.67 = f32[688,256]{1,0:T(8,128)S(1)} collective-permute-done((f32[688,256]{1,0:T(8,128)S(1)}, f32[688,256]{1,0:T(8,128)S(1)}, u32[]{:S(2)}, u32[]{:S(2)}) %collective-permute-start.67) | collective-permute-done | bytes 704544 | tf_op jit(solution)/shard_map/ppermute | solution.py:502
  498.6 14.6 %collective-permute-done.72 = f32[688,256]{1,0:T(8,128)S(1)} collective-permute-done((f32[688,256]{1,0:T(8,128)S(1)}, f32[688,256]{1,0:T(8,128)S(1)}, u32[]{:S(2)}, u32[]{:S(2)}) %collective-permute-start.72) | collective-permute-done | bytes 704544 | tf_op jit(solution)/shard_map/ppermute | solution.py:502
  552.6 22.2 %inner_backward.1 = (f32[512,256]{1,0:T(8,128)S(1)}, f32[512,256]{1,0:T(8,128)S(1)}, f32[512,256]{1,0:T(8,128)S(1)}, f32[4,512]{1,0:T(4,128)S(1)}, f32[256,128]{...) custom-call(f32[512,1024]{1,0:T(8,128)} %fusion.16.joined, ...), custom_call_target="tpu_custom_call" | custom-call | tf_op jit(solution)/shard_map/inner_backward/pallas_call | solution.py:407
  575.4 6.4 fusion.50
  590.3 9.9 %fusion.51 = f32[512,2048]{1,0:T(8,128)S(1)} fusion(f32[2048,1024]{1,0:T(8,128)} %constant_dynamic-update-slice_fusion, f32[512,256]{1,0:T(8,128)S(1)} %copy-done.82, f32[512,256]{1,0:T(8,128)S(1)} %get-tuple-element.231, f32[512,256]{1,0:T(8,128)} %copy-done.14, f32[512,256]{1,0:T(8,128)} %copy-done.16), kind=kOutput, calls=%fused_computation.66 | convolution fusion | flops 6444023808 | bytes 14680064 | tf_op jit(solution)/shard_map/dot_general | solution.py:469
  616.0 8.9 %fusion.20 = f32[1024,768]{1,0:T(8,128)S(1)} fusion(f32[512,768]{1,0:T(8,128)} %copy-done.93, f32[512,768]{1,0:T(8,128)} %constant_dynamic-update-slice_fusion.12, f32[512,1024]{1,0:T(8,128)} %collective-permute-done.8, f32[512,1024]{1,0:T(8,128)S(1)} %copy-done.30, f32[1024]{0:T(1024)S(1)} %dynamic_slice.216), kind=kOutput, calls=%fused_computation.34 | convolution fusion | flops 4834721792 | bytes 10489856 | tf_op jit(solution)/shard_map/dot_general | solution.py:462
  672.4 8.3 %fusion.24 = f32[1024,768]{1,0:T(8,128)S(1)} fusion(f32[512,768]{1,0:T(8,128)S(1)} %collective-permute-done.99, f32[512,768]{1,0:T(8,128)} %collective-permute-done.94, f32[256,1024]{1,0:T(8,128)S(1)} %copy-done.96, f32[256,1024]{1,0:T(8,128)} %collective-permute-done.9, f32[256,1024]{1,0:T(8,128)} %collective-permute-done.4, ...), kind=kOutput, calls=%fused_computation.38 | convolution fusion | flops 4836818944 | bytes 10489856 | tf_op jit(solution)/shard_map/dot_general | solution.py:462
  (620 shorter events, 442.0 us)
Async XLA Ops:
  0.7 57.0 %collective-permute-start.10 = (f32[512,256]{1,0:T(8,128)}, f32[512,256]{1,0:T(8,128)}, u32[]{:S(2)}, u32[]{:S(2)}) collective-permute-start(f32[512,256]{1,0:T(8,128)} %bitcast.135), channel_id=1, source_target_pairs={{0,1},{1,0},{2,3},{3,2},{4,5},{5,4},{6,7},{7,6},{8,9},{9,8},{10,11... | collective-permute-start | bytes 1572872 | tf_op jit(solution)/shard_map/ppermute | solution.py:493
  3.7 54.0 %collective-permute-start.11 = (f32[512,256]{1,0:T(8,128)}, f32[512,256]{1,0:T(8,128)}, u32[]{:S(2)}, u32[]{:S(2)}) collective-permute-start(f32[512,256]{1,0:T(8,128)} %bitcast.136), channel_id=1, source_target_pairs={{0,2},{1,3},{2,4},{3,5},{4,6},{5,7},{6,0},{7,1},{8,10},{9,11},{10,... | collective-permute-start | bytes 1572872 | tf_op jit(solution)/shard_map/ppermute | solution.py:493
  6.1 29.8 %collective-permute-start = (f32[8,2,256]{2,1,0:T(2,128)S(1)}, f32[8,2,256]{2,1,0:T(2,128)S(1)}, u32[]{:S(2)}, u32[]{:S(2)}) collective-permute-start(f32[8,2,256]{2,1,0:T(2,128)S(1)} %broadcast_select_fusion), channel_id=1, source_target_pairs={{0,1},{1,0},{2,3},{3,2},{4,5},{5,4},{6,7},{7,6},{8,9},{9,8},{10,11... | collective-permute-start | bytes 49160 | tf_op jit(solution)/shard_map/ppermute | solution.py:497
  15.6 58.3 %collective-permute-start.3 = (f32[256,1024]{1,0:T(8,128)}, f32[256,1024]{1,0:T(8,128)}, u32[]{:S(2)}, u32[]{:S(2)}) collective-permute-start(f32[256,1024]{1,0:T(8,128)} %get-tuple-element.334), channel_id=1, source_target_pairs={{0,16},{8,24},{16,0},{24,8},{1,17},{9,25},{17,1},{25,9},{2,18},{10... | collective-permute-start | bytes 3145736 | tf_op jit(solution)/shard_map/ppermute | solution.py:502
  21.9 72.6 %collective-permute-start.8 = (f32[512,1024]{1,0:T(8,128)}, f32[512,1024]{1,0:T(8,128)}, u32[]{:S(2)}, u32[]{:S(2)}) collective-permute-start(f32[512,1024]{1,0:T(8,128)} %get-tuple-element.304), channel_id=1, source_target_pairs={{0,8},{8,0},{16,24},{24,16},{1,9},{9,1},{17,25},{25,17},{2,10},{10... | collective-permute-start | bytes 6291464 | tf_op jit(solution)/shard_map/ppermute | solution.py:497
  44.5 48.1 %collective-permute-start.4 = (f32[256,1024]{1,0:T(8,128)}, f32[256,1024]{1,0:T(8,128)}, u32[]{:S(2)}, u32[]{:S(2)}) collective-permute-start(f32[256,1024]{1,0:T(8,128)} %get-tuple-element.333), channel_id=1, source_target_pairs={{0,16},{8,24},{16,0},{24,8},{1,17},{9,25},{17,1},{25,9},{2,18},{10... | collective-permute-start | bytes 3145736 | tf_op jit(solution)/shard_map/ppermute | solution.py:502
  238.2 116.4 %collective-permute-start.49 = (f32[512,1024]{1,0:T(8,128)}, f32[512,1024]{1,0:T(8,128)}, u32[]{:S(2)}, u32[]{:S(2)}) collective-permute-start(f32[512,1024]{1,0:T(8,128)} %get-tuple-element.328), channel_id=1, source_target_pairs={{0,8},{8,0},{16,24},{24,16},{1,9},{9,1},{17,25},{25,17},{2,10},{10... | collective-permute-start | bytes 6291464 | tf_op jit(solution)/shard_map/ppermute | solution.py:497
  282.1 29.7 %collective-permute-start.35 = (f32[128,1024]{1,0:T(8,128)S(1)}, f32[128,1024]{1,0:T(8,128)S(1)}, u32[]{:S(2)}, u32[]{:S(2)}) collective-permute-start(f32[128,1024]{1,0:T(8,128)S(1)} %get-tuple-element.331), channel_id=1, source_target_pairs={{0,16},{8,24},{16,0},{24,8},{1,17},{9,25},{17,1},{25,9},{2,18},{10... | collective-permute-start | bytes 1572872 | tf_op jit(solution)/shard_map/ppermute | solution.py:502
  301.4 53.2 %collective-permute-start.48 = (f32[512,688]{0,1:T(8,128)S(1)}, f32[512,688]{0,1:T(8,128)}, u32[]{:S(2)}, u32[]{:S(2)}) collective-permute-start(f32[512,688]{0,1:T(8,128)S(1)} %copy-done.33), channel_id=1, source_target_pairs={{0,8},{8,0},{16,24},{24,16},{1,9},{9,1},{17,25},{25,17},{2,10},{10... | collective-permute-start | bytes 4227080 | tf_op jit(solution)/shard_map/ppermute | solution.py:497
  317.9 35.3 %collective-permute-start.45 = (f32[512,1024]{1,0:T(8,128)S(1)}, f32[512,1024]{1,0:T(8,128)S(1)}, u32[]{:S(2)}, u32[]{:S(2)}) collective-permute-start(f32[512,1024]{1,0:T(8,128)S(1)} %copy-done.38), channel_id=1, source_target_pairs={{0,8},{8,0},{16,24},{24,16},{1,9},{9,1},{17,25},{25,17},{2,10},{10... | collective-permute-start | bytes 6291464 | tf_op jit(solution)/shard_map/ppermute | solution.py:497
  351.4 30.5 %collective-permute-start.52 = (f32[512,688]{0,1:T(8,128)S(1)}, f32[512,688]{0,1:T(8,128)S(1)}, u32[]{:S(2)}, u32[]{:S(2)}) collective-permute-start(f32[512,688]{0,1:T(8,128)S(1)} %copy-done.27), channel_id=1, source_target_pairs={{0,8},{8,0},{16,24},{24,16},{1,9},{9,1},{17,25},{25,17},{2,10},{10... | collective-permute-start | bytes 4227080 | tf_op jit(solution)/shard_map/ppermute | solution.py:497
  353.2 33.8 %collective-permute-start.57 = (f32[512,688]{0,1:T(8,128)S(1)}, f32[512,688]{0,1:T(8,128)}, u32[]{:S(2)}, u32[]{:S(2)}) collective-permute-start(f32[512,688]{0,1:T(8,128)S(1)} %get-tuple-element.339), channel_id=1, source_target_pairs={{0,8},{8,0},{16,24},{24,16},{1,9},{9,1},{17,25},{25,17},{2,10},{10... | collective-permute-start | bytes 4227080 | tf_op jit(solution)/shard_map/ppermute | solution.py:497
  387.0 69.2 %collective-permute-start.68 = (f32[512,1024]{1,0:T(8,128)S(1)}, f32[512,1024]{1,0:T(8,128)S(1)}, u32[]{:S(2)}, u32[]{:S(2)}) collective-permute-start(f32[512,1024]{1,0:T(8,128)S(1)} %get-tuple-element.310), channel_id=1, source_target_pairs={{0,8},{8,0},{16,24},{24,16},{1,9},{9,1},{17,25},{25,17},{2,10},{10... | collective-permute-start | bytes 6291464 | tf_op jit(solution)/shard_map/ppermute | solution.py:497
  412.3 41.1 %collective-permute-start.63 = (f32[688,256]{1,0:T(8,128)S(1)}, f32[688,256]{1,0:T(8,128)S(1)}, u32[]{:S(2)}, u32[]{:S(2)}) collective-permute-start(f32[688,256]{1,0:T(8,128)S(1)} %get-tuple-element.338), channel_id=1, source_target_pairs={{0,16},{8,24},{16,0},{24,8},{1,17},{9,25},{17,1},{25,9},{2,18},{10... | collective-permute-start | bytes 2113544 | tf_op jit(solution)/shard_map/ppermute | solution.py:502
  423.2 30.2 %collective-permute-start.64 = (f32[512,256]{1,0:T(8,128)S(1)}, f32[512,256]{1,0:T(8,128)S(1)}, u32[]{:S(2)}, u32[]{:S(2)}) collective-permute-start(f32[512,256]{1,0:T(8,128)S(1)} %add_add_fusion.5), channel_id=1, source_target_pairs={{0,2},{1,3},{2,4},{3,5},{4,6},{5,7},{6,0},{7,1},{8,10},{9,11},{10,... | collective-permute-start | bytes 1572872 | tf_op jit(solution)/shard_map/ppermute | solution.py:493
  438.3 30.2 %collective-permute-start.66 = (f32[256,688]{0,1:T(8,128)S(1)}, f32[256,688]{0,1:T(8,128)S(1)}, u32[]{:S(2)}, u32[]{:S(2)}) collective-permute-start(f32[256,688]{0,1:T(8,128)S(1)} %get-tuple-element.349), channel_id=1, source_target_pairs={{0,16},{8,24},{16,0},{24,8},{1,17},{9,25},{17,1},{25,9},{2,18},{10... | collective-permute-start | bytes 2113544 | tf_op jit(solution)/shard_map/ppermute | solution.py:502
  454.4 31.0 %collective-permute-start.73 = (f32[512,688]{0,1:T(8,128)S(1)}, f32[512,688]{0,1:T(8,128)S(1)}, u32[]{:S(2)}, u32[]{:S(2)}) collective-permute-start(f32[512,688]{0,1:T(8,128)S(1)} %pad_maximum_fusion.3), channel_id=1, source_target_pairs={{0,8},{8,0},{16,24},{24,16},{1,9},{9,1},{17,25},{25,17},{2,10},{10... | collective-permute-start | bytes 4227080 | tf_op jit(solution)/shard_map/ppermute | solution.py:497
  468.4 30.2 %collective-permute-start.71 = (f32[256,688]{0,1:T(8,128)S(1)}, f32[256,688]{0,1:T(8,128)S(1)}, u32[]{:S(2)}, u32[]{:S(2)}) collective-permute-start(f32[256,688]{0,1:T(8,128)S(1)} %get-tuple-element.348), channel_id=1, source_target_pairs={{0,16},{8,24},{16,0},{24,8},{1,17},{9,25},{17,1},{25,9},{2,18},{10... | collective-permute-start | bytes 2113544 | tf_op jit(solution)/shard_map/ppermute | solution.py:502
  536.8 45.1 %collective-permute-start.80 = (f32[1024,256]{1,0:T(8,128)}, f32[1024,256]{1,0:T(8,128)S(1)}, u32[]{:S(2)}, u32[]{:S(2)}) collective-permute-start(f32[1024,256]{1,0:T(8,128)} %fusion.4), channel_id=1, source_target_pairs={{0,16},{8,24},{16,0},{24,8},{1,17},{9,25},{17,1},{25,9},{2,18},{10... | collective-permute-start | bytes 3145736 | tf_op jit(solution)/shard_map/ppermute | solution.py:502
  543.8 66.2 %collective-permute-start.89 = (f32[688,1024]{1,0:T(8,128)}, f32[688,1024]{1,0:T(8,128)}, u32[]{:S(2)}, u32[]{:S(2)}) collective-permute-start(f32[688,1024]{1,0:T(8,128)} %add.622.own), channel_id=1, source_target_pairs={{0,8},{8,0},{16,24},{24,16},{1,9},{9,1},{17,25},{25,17},{2,10},{10... | collective-permute-start | bytes 8454152 | tf_op jit(solution)/shard_map/ppermute | solution.py:497
  543.8 38.0 %collective-permute-start.81 = (f32[512,256]{1,0:T(8,128)}, f32[512,256]{1,0:T(8,128)}, u32[]{:S(2)}, u32[]{:S(2)}) collective-permute-start(f32[512,256]{1,0:T(8,128)} %get-tuple-element.288), channel_id=1, source_target_pairs={{0,16},{8,24},{16,0},{24,8},{1,17},{9,25},{17,1},{25,9},{2,18},{10... | collective-permute-start | bytes 1572872 | tf_op jit(solution)/shard_map/ppermute | solution.py:502
  552.1 76.2 %collective-permute-start.92 = (f32[688,1024]{1,0:T(8,128)}, f32[688,1024]{1,0:T(8,128)}, u32[]{:S(2)}, u32[]{:S(2)}) collective-permute-start(f32[688,1024]{1,0:T(8,128)} %add.625.own), channel_id=1, source_target_pairs={{0,8},{8,0},{16,24},{24,16},{1,9},{9,1},{17,25},{25,17},{2,10},{10... | collective-permute-start | bytes 8454152 | tf_op jit(solution)/shard_map/ppermute | solution.py:497
  575.1 72.6 %collective-permute-start.96 = (f32[688,1024]{1,0:T(8,128)}, f32[688,1024]{1,0:T(8,128)}, u32[]{:S(2)}, u32[]{:S(2)}) collective-permute-start(f32[688,1024]{1,0:T(8,128)} %maximum_add_fusion.own), channel_id=1, source_target_pairs={{0,8},{8,0},{16,24},{24,16},{1,9},{9,1},{17,25},{25,17},{2,10},{10... | collective-permute-start | bytes 8454152 | tf_op jit(solution)/shard_map/ppermute | solution.py:497
  610.0 43.3 %collective-permute-start.94 = (f32[512,768]{1,0:T(8,128)}, f32[512,768]{1,0:T(8,128)}, u32[]{:S(2)}, u32[]{:S(2)}) collective-permute-start(f32[512,768]{1,0:T(8,128)} %constant_dynamic-update-slice_fusion.12), channel_id=1, source_target_pairs={{0,16},{8,24},{16,0},{24,8},{1,17},{9,25},{17,1},{25,9},{2,18},{10... | collective-permute-start | bytes 4718600 | tf_op jit(solution)/shard_map/ppermute | solution.py:502
  (187 other events, 2667.5 us)

commit v7 on v6

--- a/solution.py
+++ b/solution.py
@@ -502,19 +502,20 @@
     return lax.ppermute(value, "rows", [(r, (r + 2 * step) % size) for r in range(size)])
 
 
-def butterfly(value, axis):
-    bit = 1
-    while bit < lax.axis_size(axis):
-        value = value + swap(value, axis, bit)
-        bit *= 2
+def butterfly(value, axis, hooks=()):
+    size = lax.axis_size(axis)
+    bits = [1 << i for i in range(size.bit_length() - 1)][::-1]
+    for index, bit in enumerate(bits):
+        (other,) = meet([swap(value, axis, bit)], turn(hooks, index))
+        value = value + other
     return value
 
 
-def small_gather(value):
+def small_gather(value, hooks=()):
     size = lax.axis_size("heads")
     place = jnp.arange(size) == lax.axis_index("heads")
     place = place.reshape((size,) + (1,) * value.ndim)
-    return butterfly(jnp.where(place, value[None], 0.0), "heads")
+    return butterfly(jnp.where(place, value[None], 0.0), "heads", hooks)
 
 
 class Held:
@@ -727,24 +728,49 @@
     heads, hd = inner_bias.shape
     span = heads * hd
     total_span = span * lax.axis_size("heads")
-    gains = small_gather(jnp.stack([first_gain, second_gain]))
+    grad_output = cotangent.reshape(length, slab)
+    early = {}
+
+    def first():
+        early["r1"] = Held(lax.rsqrt(jnp.mean(tokens * tokens, -1, keepdims=True) + epsilon))
+        return [early["r1"]]
+
+    def second():
+        early["unit"] = Held(tokens * early["r1"].value)
+        return [early["unit"]]
+
+    def third():
+        early["pair"] = Held(half_of(early["unit"].value, core, 1))
+        return [early["pair"]]
+
+    gains = small_gather(jnp.stack([first_gain, second_gain]), [first, second, third])
     gain_one = gains[:, 0].reshape(width)
     gain_two = gains[:, 1].reshape(width)
-    grad_output = cotangent.reshape(length, slab)
-    dy_held = Held(gather_columns(grad_output))
-
+    r1, unit = early["r1"].value, early["unit"].value
+    dy_in, gain_one = lax.optimization_barrier((grad_output, gain_one))
+    unit_y = Along(
+        jnp.concatenate(
+            [early["pair"].value, swap(half_of(unit, 1 - core, 1), "rows", 1)], 0
+        )
+    )
     w_joined = jnp.concatenate([w_query, w_key, w_value, w_gate_attn], axis=1)
-    r1 = lax.rsqrt(jnp.mean(tokens * tokens, -1, keepdims=True) + epsilon)
-    unit = tokens * r1
-    unit_y = Along(tokens_half(unit, core))
     normed = unit * gain_one
     joined = product(normed, w_joined)
     rate_pre = lax.dot_general(
         w_rate, normed, (((0,), (1,)), ((), ())), precision=lax.Precision.HIGH,
         preferred_element_type=f32,
     )
-    joined = meet_one(joined, *unit_y[0])
-    gate_pre = joined[:, 3 * span :]
+    joined = Held(joined)
+    after = {}
+
+    def run_inner():
+        after["mixed"] = [
+            Held(item) for item in ttt_forward(
+                joined.value, rate, rate_t, seg, seg_t, w0, b0, gain_col, shift_col, hd, heads
+            )
+        ]
+        return [*after["mixed"], *unit_y[1]]
+
     sig = jax.nn.sigmoid(rate_pre + b_rate[:, None])
     rate_t = sig / hd
     rate = rate_t.T
@@ -752,10 +778,10 @@
     seg, seg_t = seg[:, None], seg[None]
     w0, b0 = state_in(inner_weight, inner_bias)
     gain_col, shift_col = inner_gain.reshape(span, 1), inner_shift.reshape(span, 1)
-    mixed, *saved = ttt_forward(
-        joined, rate, rate_t, seg, seg_t, w0, b0, gain_col, shift_col, hd, heads
-    )
-    mixed = meet_one(mixed, *unit_y[1])
+    dy_held = Held(gather_columns(dy_in, [[], [joined, *unit_y[0]], run_inner]))
+    joined = joined.value
+    gate_pre = joined[:, 3 * span :]
+    mixed, *saved = [item.value for item in after["mixed"]]
     row_sums = butterfly(jnp.stack([jnp.sum(mixed, 1), jnp.sum(mixed * mixed, 1)]), "heads")
     row_sums = meet_one(row_sums, *unit_y[2], dy_held)
     row_mean = row_sums[0] / total_span
@@ -782,6 +808,8 @@
     deep, across = heads_grid()
     z, x = heads_place()
 
+    dy_full, ffn_part = lax.optimization_barrier((dy_full, ffn_part))
+
     def ffn_piece(dz, dx):
         place_of = (z - dz) % deep * across + (x - dx) % across
         return lax.dynamic_slice_in_dim(ffn_part, place_of * slab, slab, 1)
@@ -793,9 +821,9 @@
     da = meet_one(dm * c * slope, *ffn_x[1 % deep])
     dc = dm * act
     da_y, dc_y = Along(da, 2), Along(dc, 2)
-    dhnorm = meet_one(right_product(da, w_gate), *ffn_x[2 % deep], *hnorm_y[0])
+    dhnorm = meet_one(right_product(da, w_gate), *ffn_x[2 % deep], *ffn_x[3 % deep], *hnorm_y[0])
     dhnorm = dhnorm + right_product(dc, w_up)
-    dhnorm = meet_one(dhnorm, *hnorm_y[1], *ffn_x[3 % deep])
+    dhnorm = meet_one(dhnorm, *hnorm_y[1])
 
     def ffn_tile(dz):
         out = ffn_piece(dz, 0)
@@ -852,22 +880,19 @@
         right_product(d_hidden, w_out),
         None,
         [
-            lambda: [*da_y[1], *down_y[0], *([ffn_step(2)] if deep > 2 else [])],
-            [*dc_y[0], *down_y[1], own_out],
+            lambda: [*da_y[1], *([ffn_step(2)] if deep > 2 else [])],
+            [*dc_y[0], own_out],
             lambda: [
-                *dc_y[1], *down_y[2],
+                *dc_y[1],
                 total("gate", own_gate.value, cores(da_y.all()), hnorm_y.all()),
             ],
             lambda: [
-                *down_y[3],
+                *down_y[0],
                 total("up", own_up.value, cores(dc_y.all()), hnorm_y.all()),
             ],
         ],
     )
     out_y = Along(own_out.value, 1)
-    for dz in range(3, deep):
-        ffn_step(dz)
-    ffn = Held(ffn_steps[-1].value + ffn_tile(0))
     d_shaped = d_gated * gate_act
     d_gate_pre = d_gated * shaped * gate_slope
     d_post_gain = jnp.sum(d_shaped * centered, 0)
@@ -880,6 +905,10 @@
     back_sums = butterfly(
         jnp.stack([jnp.sum(d_center, 1), jnp.sum(d_center * centered, 1)]), "heads"
     )
+    back_sums = meet_one(back_sums, ffn_steps[-1])
+    for dz in range(3, deep):
+        ffn_step(dz)
+    ffn = Held(ffn_steps[-1].value + ffn_tile(0))
     d_mixed = inv_std * (
         d_center - back_sums[0][:, None] / total_span
         - centered * back_sums[1][:, None] / total_span
@@ -887,7 +916,7 @@
     dq, dk, dv, d_rate, dw, db, dg, dsh = ttt_backward(
         joined, rate_t, seg, seg_t, w0, b0, gain_col, shift_col, saved, d_mixed, hd, heads
     )
-    dq = meet_one(dq, *out_y[0], *d_gate_y[0], own_attn, ffn)
+    dq = meet_one(dq, *down_y[1], *down_y[2], *down_y[3], own_attn, ffn)
     output = hidden + ffn.value
     ffn = ffn.value
     d_inner_weight, d_inner_bias = state_back(dw, db, heads, hd)
@@ -899,6 +928,7 @@
         d_rate_pre, w_rate, (((0,), (1,)), ((), ())), precision=lax.Precision.HIGH,
         preferred_element_type=f32,
     )
+    d_normed = meet_one(d_normed, *d_gate_y[0], *out_y[0])
     d_gain_one = jnp.sum(d_normed * tokens * r1, 0, keepdims=True)
     weighted = d_normed * gain_one
     d_tokens = r1 * weighted - tokens * (r1 * r1 * r1) * jnp.mean(
@@ -931,7 +961,6 @@
         lambda: [
             *d_three_y[0], *d_rate_y[0],
             *placed("g_down", sum(down_y.all()), 1),
-            *placed("g_out", sum(out_y.all()), 0),
         ],
         lambda: [
             total("three", own_three.value, normed_pairs, cores(d_three_y.all())),
@@ -949,11 +978,12 @@
     d_gain_one = d_part[length]
     stats = d_part[length + 1, : stats.size]
 
+    placed("g_out", sum(out_y.all()), 0)
+    g_query, g_key, g_value = finish(late["three"].value, core, 0, (span,) * 3)
     ((g_gate,), (g_up,), (g_down,), (g_out,), (g_gate_attn,)) = (
         [item.value for item in late[name]]
         for name in ("g_gate", "g_up", "g_down", "g_out", "g_attn")
     )
-    g_query, g_key, g_value = finish(late["three"].value, core, 0, (span,) * 3)
     g_rate = late["rate"].value
     ends = (g_rate, swap(g_rate, "rows", 1))
     g_rate = jnp.where(core == 0, jnp.concatenate(ends, 1), jnp.concatenate(ends[::-1], 1))

time: 715 us -> 700 us (0.979)
  waiting for transfers between devices: 259 us -> 250 us
  local copies, waits for them, and re-layouts: 105 us -> 97.7 us
    ppermute x24, waiting for transfers between devices: 105 us -> 64.2 us  [row_shift(): lax.ppermute(value, 'rows', [(r, (r + 2 * step) % size) for r in range(si...]
    ppermute x49, waiting for transfers between devices: 140 us -> 162 us  [shift(): return lax.ppermute(value, 'heads', pairs)]
    ppermute x34, waiting for transfers between devices: 14.4 us -> 23 us  [swap(): lax.ppermute(value, axis, [(i, i ^ bit) for i in range(lax.axis_size(axis...]
    unnamed x221 -> x281, local copies, waits for them, and re-layouts: 26.8 us -> 21.6 us
    dynamic_update_slice x22 -> x21, local copies, waits for them, and re-layouts: 30.8 us -> 28.2 us  [gather_columns(): out = lax.dynamic_update_slice(out, item, (0, column))]
  transfers between devices with their start and end apart: 107 -> 107, of which waited for: 45 -> 54; matrix products, arithmetic and copies ran while one was open for 38% -> 35% of each run, Pallas kernels for 7% -> 7%
where the time goes in v7:
time: 700 us; the launch traced here: 691 us
  waiting for transfers between devices  250 us (36%)
  matrix products  137 us (20%)
  local copies, waits for them, and re-layouts  97.7 us (14%)
  starting transfers between devices  86.2 us (12%)
  other arithmetic  60.2 us (9%)
  Pallas kernels  55.7 us (8%)
    ppermute x49, waiting for transfers between devices, shift(): return lax.ppermute(value, 'heads', pairs)  162 us
    ppermute x24, waiting for transfers between devices, row_shift(): lax.ppermute(value, 'rows', [(r, (r + 2 * step) % size) for r in range(si...  64.2 us
    dot_general x10, matrix products, left_product(): lax.dot_general(left, right, (((0,), (0,)), ((), ())), precision=lax.Prec...  60.6 us
    ppermute x49, starting transfers between devices, shift(): return lax.ppermute(value, 'heads', pairs)  40.4 us
    dot_general x7, matrix products, product(): jnp.dot(left, right, precision=lax.Precision.HIGH, preferred_element_type...  38.9 us
    dot_general x5, matrix products, right_product(): lax.dot_general(left, right, (((1,), (1,)), ((), ())), precision=lax.Prec...  33.6 us
    dynamic_update_slice x21, local copies, waits for them, and re-layouts, gather_columns(): out = lax.dynamic_update_slice(out, item, (0, column))  28.2 us
    ppermute x24, starting transfers between devices, row_shift(): lax.ppermute(value, 'rows', [(r, (r + 2 * step) % size) for r in range(si...  27.2 us
  transfers between devices with their start and end apart: 107, of which 54 were waited for; matrix products, arithmetic and copies ran while one was open for 35% of the time, Pallas kernels for 7%

profile of v7, /device:TPU:0, one launch (start us, length us, event | category | flops | bytes accessed | tf_op | source)
XLA Modules:
  0.0 690.8 jit_solution(15645155389260905847)
XLA Ops:
  42.5 8.7 %fusion.16.joined = f32[512,1024]{1,0:T(8,128)} fusion(f32[2048,1024]{1,0:T(8,128)S(1)} %bitcast.143, f32[512,2048]{1,0:T(8,128)S(1)} %bitcast_multiply_fusion.3, f32[2048]{0:T(1024)S(1)} %bitcast.144), kind=kOutput, calls=%fused_computation.29 | convolution fusion | flops 6443499520 | bytes 14688256 | tf_op jit(solution)/shard_map/dot_general | solution.py:458
  63.0 12.8 %inner_forward.1 = (f32[512,256]{1,0:T(8,128)S(1)}, f32[256,512]{1,0:T(8,128)S(1)}, f32[256,512]{1,0:T(8,128)S(1)}, f32[4,256,128]{2,1,0:T(8,128)S(1)}, f32[4,256,1]{2,1,0:T(8,128)S(1)}) custom-call(f32[512,1024]{1,0:T(8,128)S(1)} %copy-done.2, f32[512,4]{1,0:T(8,128)S(1)} %copy-done.5, f32[4,512]{1,0:T(4,128)S(1)} %get-tuple-element.417.rate_t, ...), custom_call_target="tpu_custom_call" | custom-call | tf_op jit(solution)/shard_map/inner_forward/pallas_call | solution.py:182
  116.0 8.9 %collective-permute-done.17 = f32[512,256]{1,0:T(8,128)S(1)} collective-permute-done((f32[512,256]{1,0:T(8,128)S(1)}, f32[512,256]{1,0:T(8,128)S(1)}, u32[]{:S(2)}, u32[]{:S(2)}) %collective-permute-start.17) | collective-permute-done | bytes 524320 | tf_op jit(solution)/shard_map/ppermute | solution.py:493
  142.5 8.1 %collective-permute-done.22 = f32[512,256]{1,0:T(8,128)S(1)} collective-permute-done((f32[512,256]{1,0:T(8,128)S(1)}, f32[512,256]{1,0:T(8,128)S(1)}, u32[]{:S(2)}, u32[]{:S(2)}) %collective-permute-start.22) | collective-permute-done | bytes 524320 | tf_op jit(solution)/shard_map/ppermute | solution.py:493
  172.5 9.8 %collective-permute-done.25 = f32[512,256]{1,0:T(8,128)S(1)} collective-permute-done((f32[512,256]{1,0:T(8,128)S(1)}, f32[512,256]{1,0:T(8,128)S(1)}, u32[]{:S(2)}, u32[]{:S(2)}) %collective-permute-start.25) | collective-permute-done | bytes 524320 | tf_op jit(solution)/shard_map/ppermute | solution.py:493
  188.7 11.2 %collective-permute-done.27 = f32[512,256]{1,0:T(8,128)S(1)} collective-permute-done((f32[512,256]{1,0:T(8,128)S(1)}, f32[512,256]{1,0:T(8,128)S(1)}, u32[]{:S(2)}, u32[]{:S(2)}) %collective-permute-start.27) | collective-permute-done | bytes 524320 | tf_op jit(solution)/shard_map/ppermute | solution.py:493
  205.7 10.4 %collective-permute-done.29 = f32[512,256]{1,0:T(8,128)S(1)} collective-permute-done((f32[512,256]{1,0:T(8,128)S(1)}, f32[512,256]{1,0:T(8,128)S(1)}, u32[]{:S(2)}, u32[]{:S(2)}) %collective-permute-start.29) | collective-permute-done | bytes 524320 | tf_op jit(solution)/shard_map/ppermute | solution.py:493
  247.6 7.5 %fusion.156 = f32[512,2048]{1,0:T(8,128)S(1)} fusion(f32[512,688]{0,1:T(8,128)} %get-tuple-element.426, f32[688,2048]{1,0:T(8,128)S(1)} %bitcast.133), kind=kOutput, calls=%fused_computation.345 | convolution fusion | flops 4328521728 | bytes 11239424 | tf_op jit(solution)/shard_map/dot_general | solution.py:458
  261.5 9.5 %fusion.110 = (f32[512,688]{0,1:T(8,128)S(1)}, f32[512,688]{0,1:T(8,128)}) fusion(f32[512,688]{0,1:T(8,128)} %copy-done.36, f32[512,688]{0,1:T(8,128)} %get-tuple-element.427, f32[512,2048]{1,0:T(8,128)} %constant_dynamic-update-slice_fusion.31, f32[688,2048]{1,0:T(8,128)S(1)} %bitcast.133), kind=kOutput, calls=%fused_computation.161 | convolution fusion | flops 4332396544 | bytes 15466496 | tf_op jit(solution)/shard_map/dot_general | solution.py:469
  303.4 8.7 %collective-permute-done.34 = f32[512,256]{1,0:T(8,128)S(1)} collective-permute-done((f32[512,256]{1,0:T(8,128)S(1)}, f32[512,256]{1,0:T(8,128)S(1)}, u32[]{:S(2)}, u32[]{:S(2)}) %collective-permute-start.34) | collective-permute-done | bytes 524320 | tf_op jit(solution)/shard_map/ppermute | solution.py:493
  324.3 12.6 %collective-permute-done.41 = f32[512,256]{1,0:T(8,128)S(1)} collective-permute-done((f32[512,256]{1,0:T(8,128)S(1)}, f32[512,256]{1,0:T(8,128)S(1)}, u32[]{:S(2)}, u32[]{:S(2)}) %collective-permute-start.41) | collective-permute-done | bytes 524320 | tf_op jit(solution)/shard_map/ppermute | solution.py:493
  337.8 10.1 %collective-permute-done.40 = f32[520,256]{1,0:T(8,128)S(1)} collective-permute-done((f32[520,256]{1,0:T(8,128)S(1)}, f32[520,256]{1,0:T(8,128)S(1)}, u32[]{:S(2)}, u32[]{:S(2)}) %collective-permute-start.40) | collective-permute-done | bytes 532512 | tf_op jit(solution)/shard_map/ppermute | solution.py:493
  352.5 9.1 %collective-permute-done.39 = f32[520,256]{1,0:T(8,128)S(1)} collective-permute-done((f32[520,256]{1,0:T(8,128)S(1)}, f32[520,256]{1,0:T(8,128)S(1)}, u32[]{:S(2)}, u32[]{:S(2)}) %collective-permute-start.39) | collective-permute-done | bytes 532512 | tf_op jit(solution)/shard_map/ppermute | solution.py:493
  363.3 7.1 %fusion = f32[688,1024]{1,0:T(8,128)S(1)} fusion(f32[512,1024]{1,0:T(8,128)S(1)} %collective-permute-done.49, f32[512,1024]{1,0:T(8,128)S(1)} %copy-done.43, f32[512,688]{0,1:T(8,128)} %collective-permute-done.48, f32[512,688]{0,1:T(8,128)} %get-tuple-element.426), kind=kOutput, calls=%fused_computation | convolution fusion | flops 4330274816 | bytes 9830400 | tf_op jit(solution)/shard_map/dot_general | solution.py:462
  390.6 7.4 %collective-permute-done.50 = f32[520,256]{1,0:T(8,128)S(1)} collective-permute-done((f32[520,256]{1,0:T(8,128)S(1)}, f32[520,256]{1,0:T(8,128)S(1)}, u32[]{:S(2)}, u32[]{:S(2)}) %collective-permute-start.50) | collective-permute-done | bytes 532512 | tf_op jit(solution)/shard_map/ppermute | solution.py:493
  408.4 8.7 %collective-permute-done.55 = f32[128,1024]{1,0:T(8,128)} collective-permute-done((f32[128,1024]{1,0:T(8,128)}, f32[128,1024]{1,0:T(8,128)}, u32[]{:S(2)}, u32[]{:S(2)}) %collective-permute-start.55) | collective-permute-done | bytes 524320 | tf_op jit(solution)/shard_map/ppermute | solution.py:502
  421.7 10.4 %collective-permute-done.62 = f32[256,688]{0,1:T(8,128)S(1)} collective-permute-done((f32[256,688]{0,1:T(8,128)S(1)}, f32[256,688]{0,1:T(8,128)S(1)}, u32[]{:S(2)}, u32[]{:S(2)}) %collective-permute-start.62) | collective-permute-done | bytes 704544 | tf_op jit(solution)/shard_map/ppermute | solution.py:502
  477.5 8.7 %collective-permute-done.72 = f32[688,256]{1,0:T(8,128)S(1)} collective-permute-done((f32[688,256]{1,0:T(8,128)S(1)}, f32[688,256]{1,0:T(8,128)S(1)}, u32[]{:S(2)}, u32[]{:S(2)}) %collective-permute-start.72) | collective-permute-done | bytes 704544 | tf_op jit(solution)/shard_map/ppermute | solution.py:502
  510.6 21.8 %inner_backward.1 = (f32[512,256]{1,0:T(8,128)S(1)}, f32[512,256]{1,0:T(8,128)S(1)}, f32[512,256]{1,0:T(8,128)S(1)}, f32[4,512]{1,0:T(4,128)S(1)}, f32[256,128]{...) custom-call(f32[512,1024]{1,0:T(8,128)} %fusion.16.joined, ...), custom_call_target="tpu_custom_call" | custom-call | tf_op jit(solution)/shard_map/inner_backward/pallas_call | solution.py:407
  555.1 10.4 %fusion.51 = f32[512,2048]{1,0:T(8,128)S(1)} fusion(f32[2048,1024]{1,0:T(8,128)} %constant_dynamic-update-slice_fusion, f32[512,256]{1,0:T(8,128)} %get-tuple-element.320, f32[512,256]{1,0:T(8,128)} %copy-done.14, f32[512,256]{1,0:T(8,128)} %copy-done.16, f32[512,256]{1,0:T(8,128)} %copy-done.18), kind=kOutput, calls=%fused_computation.66 | convolution fusion | flops 6444023808 | bytes 14680064 | tf_op jit(solution)/shard_map/dot_general | solution.py:469
  571.3 7.3 %collective-permute-done.82 = f32[512,256]{1,0:T(8,128)} collective-permute-done((f32[512,256]{1,0:T(8,128)}, f32[512,256]{1,0:T(8,128)}, u32[]{:S(2)}, u32[]{:S(2)}) %collective-permute-start.82) | collective-permute-done | bytes 524320 | tf_op jit(solution)/shard_map/ppermute | solution.py:502
  594.2 9.0 %fusion.20 = f32[1024,768]{1,0:T(8,128)S(1)} fusion(f32[512,768]{1,0:T(8,128)} %collective-permute-done.88, f32[512,768]{1,0:T(8,128)} %constant_dynamic-update-slice_fusion.12, f32[512,1024]{1,0:T(8,128)} %collective-permute-done.14, f32[512,1024]{1,0:T(8,128)S(1)} %copy-done.29, f32[1024]{0:T(1024)S(1)} %copy-done.106), kind=kOutput, calls=%fused_computation.34 | convolution fusion | flops 4834721792 | bytes 10489856 | tf_op jit(solution)/shard_map/dot_general | solution.py:462
  629.4 8.5 %collective-permute-done.93 = f32[520,256]{1,0:T(8,128)S(1)} collective-permute-done((f32[520,256]{1,0:T(8,128)S(1)}, f32[520,256]{1,0:T(8,128)S(1)}, u32[]{:S(2)}, u32[]{:S(2)}) %collective-permute-start.93) | collective-permute-done | bytes 532512 | tf_op jit(solution)/shard_map/ppermute | solution.py:493
  651.5 8.5 %fusion.24 = f32[1024,768]{1,0:T(8,128)S(1)} fusion(f32[512,768]{1,0:T(8,128)S(1)} %collective-permute-done.98, f32[512,768]{1,0:T(8,128)} %collective-permute-done.94, f32[256,1024]{1,0:T(8,128)S(1)} %copy-done.124, f32[256,1024]{1,0:T(8,128)} %collective-permute-done.15, f32[256,1024]{1,0:T(8,128)} %collective-permute-done.10, ...), kind=kOutput, calls=%fused_computation.38 | convolution fusion | flops 4836818944 | bytes 10489856 | tf_op jit(solution)/shard_map/dot_general | solution.py:462
  (682 shorter events, 450.9 us)
Async XLA Ops:
  29.5 52.0 %collective-permute-start.14 = (f32[512,1024]{1,0:T(8,128)}, f32[512,1024]{1,0:T(8,128)}, u32[]{:S(2)}, u32[]{:S(2)}) collective-permute-start(f32[512,1024]{1,0:T(8,128)} %get-tuple-element.363), channel_id=1, source_target_pairs={{0,8},{8,0},{16,24},{24,16},{1,9},{9,1},{17,25},{25,17},{2,10},{10... | collective-permute-start | bytes 6291464 | tf_op jit(solution)/shard_map/ppermute | solution.py:497
  30.7 26.0 %collective-permute-start.7 = (f32[256,1024]{1,0:T(8,128)S(1)}, f32[256,1024]{1,0:T(8,128)S(1)}, u32[]{:S(2)}, u32[]{:S(2)}) collective-permute-start(f32[256,1024]{1,0:T(8,128)S(1)} %get-tuple-element.378), channel_id=1, source_target_pairs={{0,16},{8,24},{16,0},{24,8},{1,17},{9,25},{17,1},{25,9},{2,18},{10... | collective-permute-start | bytes 3145736 | tf_op jit(solution)/shard_map/ppermute | solution.py:502
  32.2 47.7 %collective-permute-start.10 = (f32[256,1024]{1,0:T(8,128)}, f32[256,1024]{1,0:T(8,128)}, u32[]{:S(2)}, u32[]{:S(2)}) collective-permute-start(f32[256,1024]{1,0:T(8,128)} %get-tuple-element.377), channel_id=1, source_target_pairs={{0,16},{8,24},{16,0},{24,8},{1,17},{9,25},{17,1},{25,9},{2,18},{10... | collective-permute-start | bytes 3145736 | tf_op jit(solution)/shard_map/ppermute | solution.py:502
  247.6 103.3 %collective-permute-start.48 = (f32[512,688]{0,1:T(8,128)}, f32[512,688]{0,1:T(8,128)}, u32[]{:S(2)}, u32[]{:S(2)}) collective-permute-start(f32[512,688]{0,1:T(8,128)} %get-tuple-element.426), channel_id=1, source_target_pairs={{0,8},{8,0},{16,24},{24,16},{1,9},{9,1},{17,25},{25,17},{2,10},{10... | collective-permute-start | bytes 4227080 | tf_op jit(solution)/shard_map/ppermute | solution.py:497
  275.9 37.9 %collective-permute-start.36 = (f32[128,1024]{1,0:T(8,128)}, f32[128,1024]{1,0:T(8,128)S(1)}, u32[]{:S(2)}, u32[]{:S(2)}) collective-permute-start(f32[128,1024]{1,0:T(8,128)} %get-tuple-element.361), channel_id=1, source_target_pairs={{0,16},{8,24},{16,0},{24,8},{1,17},{9,25},{17,1},{25,9},{2,18},{10... | collective-permute-start | bytes 1572872 | tf_op jit(solution)/shard_map/ppermute | solution.py:502
  295.0 26.7 %collective-permute-start.42 = (f32[128,1024]{1,0:T(8,128)}, f32[128,1024]{1,0:T(8,128)S(1)}, u32[]{:S(2)}, u32[]{:S(2)}) collective-permute-start(f32[128,1024]{1,0:T(8,128)} %get-tuple-element.360), channel_id=1, source_target_pairs={{0,16},{8,24},{16,0},{24,8},{1,17},{9,25},{17,1},{25,9},{2,18},{10... | collective-permute-start | bytes 1572872 | tf_op jit(solution)/shard_map/ppermute | solution.py:502
  312.9 36.6 %collective-permute-start.45 = (f32[512,1024]{1,0:T(8,128)}, f32[512,1024]{1,0:T(8,128)S(1)}, u32[]{:S(2)}, u32[]{:S(2)}) collective-permute-start(f32[512,1024]{1,0:T(8,128)} %get-tuple-element.356), channel_id=1, source_target_pairs={{0,8},{8,0},{16,24},{24,16},{1,9},{9,1},{17,25},{25,17},{2,10},{10... | collective-permute-start | bytes 6291464 | tf_op jit(solution)/shard_map/ppermute | solution.py:497
  314.5 48.7 %collective-permute-start.49 = (f32[512,1024]{1,0:T(8,128)S(1)}, f32[512,1024]{1,0:T(8,128)S(1)}, u32[]{:S(2)}, u32[]{:S(2)}) collective-permute-start(f32[512,1024]{1,0:T(8,128)S(1)} %copy-done.44), channel_id=1, source_target_pairs={{0,8},{8,0},{16,24},{24,16},{1,9},{9,1},{17,25},{25,17},{2,10},{10... | collective-permute-start | bytes 6291464 | tf_op jit(solution)/shard_map/ppermute | solution.py:497
  337.0 40.1 %collective-permute-start.52 = (f32[512,688]{0,1:T(8,128)S(1)}, f32[512,688]{0,1:T(8,128)S(1)}, u32[]{:S(2)}, u32[]{:S(2)}) collective-permute-start(f32[512,688]{0,1:T(8,128)S(1)} %copy-done.35), channel_id=1, source_target_pairs={{0,8},{8,0},{16,24},{24,16},{1,9},{9,1},{17,25},{25,17},{2,10},{10... | collective-permute-start | bytes 4227080 | tf_op jit(solution)/shard_map/ppermute | solution.py:497
  363.2 38.0 %collective-permute-start.57 = (f32[512,688]{0,1:T(8,128)S(1)}, f32[512,688]{0,1:T(8,128)}, u32[]{:S(2)}, u32[]{:S(2)}) collective-permute-start(f32[512,688]{0,1:T(8,128)S(1)} %copy-done.33), channel_id=1, source_target_pairs={{0,8},{8,0},{16,24},{24,16},{1,9},{9,1},{17,25},{25,17},{2,10},{10... | collective-permute-start | bytes 4227080 | tf_op jit(solution)/shard_map/ppermute | solution.py:497
  389.1 28.0 %collective-permute-start.55 = (f32[128,1024]{1,0:T(8,128)}, f32[128,1024]{1,0:T(8,128)}, u32[]{:S(2)}, u32[]{:S(2)}) collective-permute-start(f32[128,1024]{1,0:T(8,128)} %get-tuple-element.371), channel_id=1, source_target_pairs={{0,16},{8,24},{16,0},{24,8},{1,17},{9,25},{17,1},{25,9},{2,18},{10... | collective-permute-start | bytes 1572872 | tf_op jit(solution)/shard_map/ppermute | solution.py:502
  401.2 34.2 %collective-permute-start.66 = (f32[512,1024]{1,0:T(8,128)S(1)}, f32[512,1024]{1,0:T(8,128)S(1)}, u32[]{:S(2)}, u32[]{:S(2)}) collective-permute-start(f32[512,1024]{1,0:T(8,128)S(1)} %get-tuple-element.340), channel_id=1, source_target_pairs={{0,8},{8,0},{16,24},{24,16},{1,9},{9,1},{17,25},{25,17},{2,10},{10... | collective-permute-start | bytes 6291464 | tf_op jit(solution)/shard_map/ppermute | solution.py:497
  421.0 26.2 %collective-permute-start.65 = (f32[256,688]{0,1:T(8,128)S(1)}, f32[256,688]{0,1:T(8,128)S(1)}, u32[]{:S(2)}, u32[]{:S(2)}) collective-permute-start(f32[256,688]{0,1:T(8,128)S(1)} %get-tuple-element.380), channel_id=1, source_target_pairs={{0,16},{8,24},{16,0},{24,8},{1,17},{9,25},{17,1},{25,9},{2,18},{10... | collective-permute-start | bytes 2113544 | tf_op jit(solution)/shard_map/ppermute | solution.py:502
  499.7 42.5 %collective-permute-start.77 = (f32[688,256]{1,0:T(8,128)}, f32[688,256]{1,0:T(8,128)S(1)}, u32[]{:S(2)}, u32[]{:S(2)}) collective-permute-start(f32[688,256]{1,0:T(8,128)} %get-tuple-element.367), channel_id=1, source_target_pairs={{0,16},{8,24},{16,0},{24,8},{1,17},{9,25},{17,1},{25,9},{2,18},{10... | collective-permute-start | bytes 2113544 | tf_op jit(solution)/shard_map/ppermute | solution.py:502
  500.2 43.3 %collective-permute-start.78 = (f32[688,256]{1,0:T(8,128)}, f32[688,256]{1,0:T(8,128)S(1)}, u32[]{:S(2)}, u32[]{:S(2)}) collective-permute-start(f32[688,256]{1,0:T(8,128)} %get-tuple-element.366), channel_id=1, source_target_pairs={{0,16},{8,24},{16,0},{24,8},{1,17},{9,25},{17,1},{25,9},{2,18},{10... | collective-permute-start | bytes 2113544 | tf_op jit(solution)/shard_map/ppermute | solution.py:502
  501.7 47.0 %collective-permute-start.79 = (f32[688,256]{1,0:T(8,128)}, f32[688,256]{1,0:T(8,128)S(1)}, u32[]{:S(2)}, u32[]{:S(2)}) collective-permute-start(f32[688,256]{1,0:T(8,128)} %get-tuple-element.365), channel_id=1, source_target_pairs={{0,16},{8,24},{16,0},{24,8},{1,17},{9,25},{17,1},{25,9},{2,18},{10... | collective-permute-start | bytes 2113544 | tf_op jit(solution)/shard_map/ppermute | solution.py:502
  502.2 31.0 %collective-permute-start.80 = (f32[512,256]{1,0:T(8,128)}, f32[512,256]{1,0:T(8,128)S(1)}, u32[]{:S(2)}, u32[]{:S(2)}) collective-permute-start(f32[512,256]{1,0:T(8,128)} %get-tuple-element.320), channel_id=1, source_target_pairs={{0,8},{8,0},{16,24},{24,16},{1,9},{9,1},{17,25},{25,17},{2,10},{10... | collective-permute-start | bytes 1572872 | tf_op jit(solution)/shard_map/ppermute | solution.py:497
  503.9 37.0 %collective-permute-start.81 = (f32[512,256]{1,0:T(8,128)S(1)}, f32[512,256]{1,0:T(8,128)S(1)}, u32[]{:S(2)}, u32[]{:S(2)}) collective-permute-start(f32[512,256]{1,0:T(8,128)S(1)} %add_add_fusion.1), channel_id=1, source_target_pairs={{0,2},{1,3},{2,4},{3,5},{4,6},{5,7},{6,0},{7,1},{8,10},{9,11},{10,... | collective-permute-start | bytes 1572872 | tf_op jit(solution)/shard_map/ppermute | solution.py:493
  533.2 38.1 %collective-permute-start.83 = (f32[1024,256]{1,0:T(8,128)}, f32[1024,256]{1,0:T(8,128)}, u32[]{:S(2)}, u32[]{:S(2)}) collective-permute-start(f32[1024,256]{1,0:T(8,128)} %fusion.4), channel_id=1, source_target_pairs={{0,16},{8,24},{16,0},{24,8},{1,17},{9,25},{17,1},{25,9},{2,18},{10... | collective-permute-start | bytes 3145736 | tf_op jit(solution)/shard_map/ppermute | solution.py:502
  540.9 48.1 %collective-permute-start.89 = (f32[688,1024]{1,0:T(8,128)S(1)}, f32[688,1024]{1,0:T(8,128)}, u32[]{:S(2)}, u32[]{:S(2)}) collective-permute-start(f32[688,1024]{1,0:T(8,128)S(1)} %copy-done.4), channel_id=1, source_target_pairs={{0,8},{8,0},{16,24},{24,16},{1,9},{9,1},{17,25},{25,17},{2,10},{10... | collective-permute-start | bytes 8454152 | tf_op jit(solution)/shard_map/ppermute | solution.py:497
  542.2 36.5 %collective-permute-start.82 = (f32[512,256]{1,0:T(8,128)}, f32[512,256]{1,0:T(8,128)}, u32[]{:S(2)}, u32[]{:S(2)}) collective-permute-start(f32[512,256]{1,0:T(8,128)} %get-tuple-element.320), channel_id=1, source_target_pairs={{0,16},{8,24},{16,0},{24,8},{1,17},{9,25},{17,1},{25,9},{2,18},{10... | collective-permute-start | bytes 1572872 | tf_op jit(solution)/shard_map/ppermute | solution.py:502
  543.5 69.8 %collective-permute-start.92 = (f32[688,1024]{1,0:T(8,128)}, f32[688,1024]{1,0:T(8,128)}, u32[]{:S(2)}, u32[]{:S(2)}) collective-permute-start(f32[688,1024]{1,0:T(8,128)} %add.626.own), channel_id=1, source_target_pairs={{0,8},{8,0},{16,24},{24,16},{1,9},{9,1},{17,25},{25,17},{2,10},{10... | collective-permute-start | bytes 8454152 | tf_op jit(solution)/shard_map/ppermute | solution.py:497
  581.0 43.5 %collective-permute-start.96 = (f32[688,1024]{1,0:T(8,128)S(1)}, f32[688,1024]{1,0:T(8,128)S(1)}, u32[]{:S(2)}, u32[]{:S(2)}) collective-permute-start(f32[688,1024]{1,0:T(8,128)S(1)} %maximum_add_fusion.own), channel_id=1, source_target_pairs={{0,8},{8,0},{16,24},{24,16},{1,9},{9,1},{17,25},{25,17},{2,10},{10... | collective-permute-start | bytes 8454152 | tf_op jit(solution)/shard_map/ppermute | solution.py:497
  589.0 40.4 %collective-permute-start.94 = (f32[512,768]{1,0:T(8,128)}, f32[512,768]{1,0:T(8,128)}, u32[]{:S(2)}, u32[]{:S(2)}) collective-permute-start(f32[512,768]{1,0:T(8,128)} %constant_dynamic-update-slice_fusion.12), channel_id=1, source_target_pairs={{0,16},{8,24},{16,0},{24,8},{1,17},{9,25},{17,1},{25,9},{2,18},{10... | collective-permute-start | bytes 4718600 | tf_op jit(solution)/shard_map/ppermute | solution.py:502
  (217 other events, 3445.4 us)

commit v8 on v7

--- a/solution.py
+++ b/solution.py
@@ -808,22 +808,25 @@
     deep, across = heads_grid()
     z, x = heads_place()
 
-    dy_full, ffn_part = lax.optimization_barrier((dy_full, ffn_part))
+    dy_full, ffn_part = meet([dy_full, ffn_part], hnorm_y[0])
 
     def ffn_piece(dz, dx):
         place_of = (z - dz) % deep * across + (x - dx) % across
         return lax.dynamic_slice_in_dim(ffn_part, place_of * slab, slab, 1)
 
-    ffn_x = [
-        [Held(shift(ffn_piece(dz, dx), 0, dx)) for dx in range(1, across)] for dz in range(deep)
-    ]
+    def ffn_across(dz):
+        return [Held(shift(ffn_piece(dz, dx), 0, dx)) for dx in range(1, across)]
+
+    soon = [dz for dz in (1, 2) if dz < deep]
+    ffn_x = {dz: ffn_across(dz) for dz in soon}
+    soon_x = [item for dz in soon for item in ffn_x[dz]]
     dm = right_product(dy_full, w_down)
-    da = meet_one(dm * c * slope, *ffn_x[1 % deep])
+    da = meet_one(dm * c * slope, *hnorm_y[1])
     dc = dm * act
     da_y, dc_y = Along(da, 2), Along(dc, 2)
-    dhnorm = meet_one(right_product(da, w_gate), *ffn_x[2 % deep], *ffn_x[3 % deep], *hnorm_y[0])
+    dhnorm = meet_one(right_product(da, w_gate), *soon_x, *hnorm_y[2], *hnorm_y[3])
     dhnorm = dhnorm + right_product(dc, w_up)
-    dhnorm = meet_one(dhnorm, *hnorm_y[1])
+    dhnorm = meet_one(dhnorm, *hnorm_y[4])
 
     def ffn_tile(dz):
         out = ffn_piece(dz, 0)
@@ -851,10 +854,10 @@
         d_whole,
         jnp.concatenate([d_gain_two, pad], 0),
         [
-            [*ffn_x[0], *hnorm_y[2], *hnorm_y[3]],
-            [*hnorm_y[4], *hnorm_y[5], own_down],
-            lambda: [*hnorm_y[6], own_gate, ffn_step(1)],
-            [*hnorm_y[7], *da_y[0], own_up],
+            [*hnorm_y[5], *hnorm_y[6]],
+            [*hnorm_y[7], *da_y[0], own_down],
+            lambda: [*da_y[1], own_gate, *([ffn_step(1)] if deep > 1 else [])],
+            [*dc_y[0], own_up],
         ],
     )
     d_hidden = grad_output + d_part[:length]
@@ -880,14 +883,14 @@
         right_product(d_hidden, w_out),
         None,
         [
-            lambda: [*da_y[1], *([ffn_step(2)] if deep > 2 else [])],
-            [*dc_y[0], own_out],
+            lambda: [*dc_y[1], *([ffn_step(2)] if deep > 2 else [])],
+            [*down_y[0], own_out],
             lambda: [
-                *dc_y[1],
+                *down_y[1],
                 total("gate", own_gate.value, cores(da_y.all()), hnorm_y.all()),
             ],
             lambda: [
-                *down_y[0],
+                *down_y[2],
                 total("up", own_up.value, cores(dc_y.all()), hnorm_y.all()),
             ],
         ],
@@ -905,10 +908,13 @@
     back_sums = butterfly(
         jnp.stack([jnp.sum(d_center, 1), jnp.sum(d_center * centered, 1)]), "heads"
     )
-    back_sums = meet_one(back_sums, ffn_steps[-1])
+    back_sums, ffn_part = meet([back_sums, ffn_part], ffn_steps[-1:])
+    for dz in range(deep):
+        if dz not in ffn_x:
+            ffn_x[dz] = ffn_across(dz)
     for dz in range(3, deep):
         ffn_step(dz)
-    ffn = Held(ffn_steps[-1].value + ffn_tile(0))
+    ffn = Held((ffn_steps[-1].value if ffn_steps else 0.0) + ffn_tile(0))
     d_mixed = inv_std * (
         d_center - back_sums[0][:, None] / total_span
         - centered * back_sums[1][:, None] / total_span
@@ -916,9 +922,7 @@
     dq, dk, dv, d_rate, dw, db, dg, dsh = ttt_backward(
         joined, rate_t, seg, seg_t, w0, b0, gain_col, shift_col, saved, d_mixed, hd, heads
     )
-    dq = meet_one(dq, *down_y[1], *down_y[2], *down_y[3], own_attn, ffn)
-    output = hidden + ffn.value
-    ffn = ffn.value
+    dq = meet_one(dq, *down_y[3], own_attn)
     d_inner_weight, d_inner_bias = state_back(dw, db, heads, hd)
     d_rate_pre = d_rate * rate_t * (1.0 - sig)
     d_three = jnp.concatenate([dq, dk, dv], 1)
@@ -928,7 +932,9 @@
         d_rate_pre, w_rate, (((0,), (1,)), ((), ())), precision=lax.Precision.HIGH,
         preferred_element_type=f32,
     )
-    d_normed = meet_one(d_normed, *d_gate_y[0], *out_y[0])
+    d_normed = meet_one(d_normed, *d_gate_y[0], *out_y[0], ffn)
+    ffn = ffn.value
+    output = hidden + ffn
     d_gain_one = jnp.sum(d_normed * tokens * r1, 0, keepdims=True)
     weighted = d_normed * gain_one
     d_tokens = r1 * weighted - tokens * (r1 * r1 * r1) * jnp.mean(
@@ -959,13 +965,13 @@
             *placed("g_up", late["up"].value, 1),
         ],
         lambda: [
-            *d_three_y[0], *d_rate_y[0],
+            *d_three_y[0],
             *placed("g_down", sum(down_y.all()), 1),
         ],
         lambda: [
             total("three", own_three.value, normed_pairs, cores(d_three_y.all())),
             *placed("g_attn", late["attn"].value, 0),
-            rate_total(),
+            *d_rate_y[0],
         ],
     ]
     across_slabs = jnp.tile(jnp.pad(stats, (0, slab - stats.size)), width // slab)[None]
@@ -984,7 +990,7 @@
         [item.value for item in late[name]]
         for name in ("g_gate", "g_up", "g_down", "g_out", "g_attn")
     )
-    g_rate = late["rate"].value
+    g_rate = rate_total().value
     ends = (g_rate, swap(g_rate, "rows", 1))
     g_rate = jnp.where(core == 0, jnp.concatenate(ends, 1), jnp.concatenate(ends[::-1], 1))
 

time: 700 us -> 653 us (0.933)
  waiting for transfers between devices: 250 us -> 200 us
    ppermute x49, waiting for transfers between devices: 162 us -> 109 us  [shift(): return lax.ppermute(value, 'heads', pairs)]
    unnamed x281 -> x263, local copies, waits for them, and re-layouts: 21.6 us -> 17.5 us
  transfers between devices with their start and end apart: 107 -> 107, of which waited for: 54 -> 49; matrix products, arithmetic and copies ran while one was open for 35% -> 40% of each run, Pallas kernels for 7% -> 8%
where the time goes in v8:
time: 653 us; the launch traced here: 644 us
  waiting for transfers between devices  200 us (31%)
  matrix products  143 us (22%)
  local copies, waits for them, and re-layouts  94.6 us (14%)
  starting transfers between devices  81.5 us (12%)
  other arithmetic  62 us (9%)
  Pallas kernels  57.8 us (9%)
    ppermute x49, waiting for transfers between devices, shift(): return lax.ppermute(value, 'heads', pairs)  109 us
    ppermute x24, waiting for transfers between devices, row_shift(): lax.ppermute(value, 'rows', [(r, (r + 2 * step) % size) for r in range(si...  68.5 us
    dot_general x10, matrix products, left_product(): lax.dot_general(left, right, (((0,), (0,)), ((), ())), precision=lax.Prec...  65.1 us
    dot_general x7, matrix products, product(): jnp.dot(left, right, precision=lax.Precision.HIGH, preferred_element_type...  39.1 us
    ppermute x49, starting transfers between devices, shift(): return lax.ppermute(value, 'heads', pairs)  38 us
    dot_general x5, matrix products, right_product(): lax.dot_general(left, right, (((1,), (1,)), ((), ())), precision=lax.Prec...  33.1 us
    dynamic_update_slice x21, local copies, waits for them, and re-layouts, gather_columns(): out = lax.dynamic_update_slice(out, item, (0, column))  28.2 us
    ppermute x24, starting transfers between devices, row_shift(): lax.ppermute(value, 'rows', [(r, (r + 2 * step) % size) for r in range(si...  24.6 us
  transfers between devices with their start and end apart: 107, of which 49 were waited for; matrix products, arithmetic and copies ran while one was open for 40% of the time, Pallas kernels for 8%

profile of v8, /device:TPU:0, one launch (start us, length us, event | category | flops | bytes accessed | tf_op | source)
XLA Modules:
  0.0 643.5 jit_solution(6308625207239738875)
XLA Ops:
  42.5 8.7 %fusion.16.joined = f32[512,1024]{1,0:T(8,128)} fusion(f32[2048,1024]{1,0:T(8,128)S(1)} %bitcast.143, f32[512,2048]{1,0:T(8,128)S(1)} %bitcast_multiply_fusion.3, f32[2048]{0:T(1024)S(1)} %bitcast.144), kind=kOutput, calls=%fused_computation.29 | convolution fusion | flops 6443499520 | bytes 14688256 | tf_op jit(solution)/shard_map/dot_general | solution.py:458
  62.7 12.8 %inner_forward.1 = (f32[512,256]{1,0:T(8,128)S(1)}, f32[256,512]{1,0:T(8,128)S(1)}, f32[256,512]{1,0:T(8,128)S(1)}, f32[4,256,128]{2,1,0:T(8,128)S(1)}, f32[4,256,1]{2,1,0:T(8,128)S(1)}) custom-call(f32[512,1024]{1,0:T(8,128)S(1)} %copy-done.2, f32[512,4]{1,0:T(8,128)S(1)} %copy-done.5, f32[4,512]{1,0:T(4,128)S(1)} %get-tuple-element.414.rate_t, ...), custom_call_target="tpu_custom_call" | custom-call | tf_op jit(solution)/shard_map/inner_forward/pallas_call | solution.py:182
  115.7 8.9 %collective-permute-done.17 = f32[512,256]{1,0:T(8,128)S(1)} collective-permute-done((f32[512,256]{1,0:T(8,128)S(1)}, f32[512,256]{1,0:T(8,128)S(1)}, u32[]{:S(2)}, u32[]{:S(2)}) %collective-permute-start.17) | collective-permute-done | bytes 524320 | tf_op jit(solution)/shard_map/ppermute | solution.py:493
  129.8 6.3 collective-permute-done.21
  142.3 7.9 %collective-permute-done.22 = f32[512,256]{1,0:T(8,128)S(1)} collective-permute-done((f32[512,256]{1,0:T(8,128)S(1)}, f32[512,256]{1,0:T(8,128)S(1)}, u32[]{:S(2)}, u32[]{:S(2)}) %collective-permute-start.22) | collective-permute-done | bytes 524320 | tf_op jit(solution)/shard_map/ppermute | solution.py:493
  172.2 10.0 %collective-permute-done.25 = f32[512,256]{1,0:T(8,128)S(1)} collective-permute-done((f32[512,256]{1,0:T(8,128)S(1)}, f32[512,256]{1,0:T(8,128)S(1)}, u32[]{:S(2)}, u32[]{:S(2)}) %collective-permute-start.25) | collective-permute-done | bytes 524320 | tf_op jit(solution)/shard_map/ppermute | solution.py:493
  188.4 11.2 %collective-permute-done.27 = f32[512,256]{1,0:T(8,128)S(1)} collective-permute-done((f32[512,256]{1,0:T(8,128)S(1)}, f32[512,256]{1,0:T(8,128)S(1)}, u32[]{:S(2)}, u32[]{:S(2)}) %collective-permute-start.27) | collective-permute-done | bytes 524320 | tf_op jit(solution)/shard_map/ppermute | solution.py:493
  205.5 10.1 %collective-permute-done.29 = f32[512,256]{1,0:T(8,128)} collective-permute-done((f32[512,256]{1,0:T(8,128)S(1)}, f32[512,256]{1,0:T(8,128)}, u32[]{:S(2)}, u32[]{:S(2)}) %collective-permute-start.29) | collective-permute-done | bytes 524320 | tf_op jit(solution)/shard_map/ppermute | solution.py:493
  246.3 6.4 fusion.111
  252.7 7.4 %fusion.156 = f32[512,2048]{1,0:T(8,128)S(1)} fusion(f32[512,688]{0,1:T(8,128)} %get-tuple-element.423, f32[688,2048]{1,0:T(8,128)S(1)} %bitcast.133), kind=kOutput, calls=%fused_computation.345 | convolution fusion | flops 4328521728 | bytes 11239424 | tf_op jit(solution)/shard_map/dot_general | solution.py:458
  260.1 9.6 %fusion.110 = (f32[512,688]{0,1:T(8,128)S(1)}, f32[512,688]{0,1:T(8,128)S(1)}) fusion(f32[512,688]{0,1:T(8,128)S(1)} %copy-done.31, f32[512,688]{0,1:T(8,128)} %get-tuple-element.424, f32[512,2048]{1,0:T(8,128)} %constant_dynamic-update-slice_fusion.31, f32[688,2048]{1,0:T(8,128)S(1)} %bitcast.133), kind=kOutput, calls=%fused_computation.161 | convolution fusion | flops 4332396544 | bytes 15466496 | tf_op jit(solution)/shard_map/dot_general | solution.py:469
  311.4 10.4 %collective-permute-done.45 = f32[128,1024]{1,0:T(8,128)S(1)} collective-permute-done((f32[128,1024]{1,0:T(8,128)}, f32[128,1024]{1,0:T(8,128)S(1)}, u32[]{:S(2)}, u32[]{:S(2)}) %collective-permute-start.45) | collective-permute-done | bytes 524320 | tf_op jit(solution)/shard_map/ppermute | solution.py:502
  324.3 16.2 %collective-permute-done.48 = f32[256,688]{0,1:T(8,128)S(1)} collective-permute-done((f32[256,688]{0,1:T(8,128)S(1)}, f32[256,688]{0,1:T(8,128)S(1)}, u32[]{:S(2)}, u32[]{:S(2)}) %collective-permute-start.48) | collective-permute-done | bytes 704544 | tf_op jit(solution)/shard_map/ppermute | solution.py:502
  342.4 7.6 %fusion = f32[688,1024]{1,0:T(8,128)S(1)} fusion(f32[512,1024]{1,0:T(8,128)} %collective-permute-done.50, f32[512,1024]{1,0:T(8,128)S(1)} %copy-done.42, f32[512,688]{0,1:T(8,128)} %collective-permute-done.49, f32[512,688]{0,1:T(8,128)} %get-tuple-element.423), kind=kOutput, calls=%fused_computation | convolution fusion | flops 4330274816 | bytes 9830400 | tf_op jit(solution)/shard_map/dot_general | solution.py:462
  356.6 6.9 %fusion.19 = f32[688,1024]{1,0:T(8,128)S(1)} fusion(f32[512,1024]{1,0:T(8,128)} %collective-permute-done.38, f32[512,1024]{1,0:T(8,128)S(1)} %copy-done.41, f32[512,688]{0,1:T(8,128)} %copy-done.108, f32[512,688]{0,1:T(8,128)S(1)} %copy-done.29), kind=kOutput, calls=%fused_computation.32 | convolution fusion | flops 4330274816 | bytes 9830400 | tf_op jit(solution)/shard_map/dot_general | solution.py:462
  371.0 8.4 %collective-permute-done.51 = f32[520,256]{1,0:T(8,128)S(1)} collective-permute-done((f32[520,256]{1,0:T(8,128)S(1)}, f32[520,256]{1,0:T(8,128)S(1)}, u32[]{:S(2)}, u32[]{:S(2)}) %collective-permute-start.51) | collective-permute-done | bytes 532512 | tf_op jit(solution)/shard_map/ppermute | solution.py:493
  381.4 6.8 %fusion.18 = f32[688,1024]{1,0:T(8,128)S(1)} fusion(f32[512,1024]{1,0:T(8,128)} %collective-permute-done.38, f32[512,1024]{1,0:T(8,128)S(1)} %copy-done.41, f32[512,688]{0,1:T(8,128)} %collective-permute-done.57, f32[512,688]{0,1:T(8,128)S(1)} %copy-done.27), kind=kOutput, calls=%fused_computation.31 | convolution fusion | flops 4330274816 | bytes 9830400 | tf_op jit(solution)/shard_map/dot_general | solution.py:462
  390.1 6.4 %collective-permute-done.55 = f32[520,256]{1,0:T(8,128)S(1)} collective-permute-done((f32[520,256]{1,0:T(8,128)S(1)}, f32[520,256]{1,0:T(8,128)S(1)}, u32[]{:S(2)}, u32[]{:S(2)}) %collective-permute-start.55) | collective-permute-done | bytes 532512 | tf_op jit(solution)/shard_map/ppermute | solution.py:493
  474.1 22.2 %inner_backward.1 = (f32[512,256]{1,0:T(8,128)S(1)}, f32[512,256]{1,0:T(8,128)S(1)}, f32[512,256]{1,0:T(8,128)S(1)}, f32[4,512]{1,0:T(4,128)S(1)}, f32[256,128]{...) custom-call(f32[512,1024]{1,0:T(8,128)} %fusion.16.joined, ...), custom_call_target="tpu_custom_call" | custom-call | tf_op jit(solution)/shard_map/inner_backward/pallas_call | solution.py:407
  497.3 6.2 fusion.50
  507.3 9.6 %fusion.51 = f32[512,2048]{1,0:T(8,128)S(1)} fusion(f32[2048,1024]{1,0:T(8,128)} %constant_dynamic-update-slice_fusion, f32[512,256]{1,0:T(8,128)} %get-tuple-element.380, f32[512,256]{1,0:T(8,128)S(1)} %get-tuple-element.256, f32[512,256]{1,0:T(8,128)S(1)} %get-tuple-element.255, f32[512,256]{1,0:T(8,128)S(1)} %get-tuple-element.254), kind=kOutput, calls=%fused_computation.66 | convolution fusion | flops 6444023808 | bytes 14680064 | tf_op jit(solution)/shard_map/dot_general | solution.py:469
  544.6 9.1 %fusion.20 = f32[1024,768]{1,0:T(8,128)S(1)} fusion(f32[512,768]{1,0:T(8,128)} %collective-permute-done.88, f32[512,768]{1,0:T(8,128)} %constant_dynamic-update-slice_fusion.12, f32[512,1024]{1,0:T(8,128)} %collective-permute-done.14, f32[512,1024]{1,0:T(8,128)S(1)} %copy-done.24, f32[1024]{0:T(1024)S(1)} %copy-done.93), kind=kOutput, calls=%fused_computation.34 | convolution fusion | flops 4834721792 | bytes 10489856 | tf_op jit(solution)/shard_map/dot_general | solution.py:462
  584.2 6.4 %collective-permute-done.94 = f32[512,768]{1,0:T(8,128)} collective-permute-done((f32[512,768]{1,0:T(8,128)}, f32[512,768]{1,0:T(8,128)}, u32[]{:S(2)}, u32[]{:S(2)}) %collective-permute-start.94) | collective-permute-done | bytes 1572896 | tf_op jit(solution)/shard_map/ppermute | solution.py:502
  598.6 8.5 %fusion.24 = f32[1024,768]{1,0:T(8,128)S(1)} fusion(f32[512,768]{1,0:T(8,128)S(1)} %collective-permute-done.97, f32[512,768]{1,0:T(8,128)} %collective-permute-done.94, f32[256,1024]{1,0:T(8,128)S(1)} %copy-done.112, f32[256,1024]{1,0:T(8,128)} %collective-permute-done.15, f32[256,1024]{1,0:T(8,128)} %collective-permute-done.10, ...), kind=kOutput, calls=%fused_computation.38 | convolution fusion | flops 4836818944 | bytes 10489856 | tf_op jit(solution)/shard_map/dot_general | solution.py:462
  (664 shorter events, 415.1 us)
Async XLA Ops:
  29.5 51.8 %collective-permute-start.14 = (f32[512,1024]{1,0:T(8,128)}, f32[512,1024]{1,0:T(8,128)}, u32[]{:S(2)}, u32[]{:S(2)}) collective-permute-start(f32[512,1024]{1,0:T(8,128)} %get-tuple-element.358), channel_id=1, source_target_pairs={{0,8},{8,0},{16,24},{24,16},{1,9},{9,1},{17,25},{25,17},{2,10},{10... | collective-permute-start | bytes 6291464 | tf_op jit(solution)/shard_map/ppermute | solution.py:497
  30.7 26.0 %collective-permute-start.7 = (f32[256,1024]{1,0:T(8,128)S(1)}, f32[256,1024]{1,0:T(8,128)S(1)}, u32[]{:S(2)}, u32[]{:S(2)}) collective-permute-start(f32[256,1024]{1,0:T(8,128)S(1)} %get-tuple-element.373), channel_id=1, source_target_pairs={{0,16},{8,24},{16,0},{24,8},{1,17},{9,25},{17,1},{25,9},{2,18},{10... | collective-permute-start | bytes 3145736 | tf_op jit(solution)/shard_map/ppermute | solution.py:502
  32.2 47.5 %collective-permute-start.10 = (f32[256,1024]{1,0:T(8,128)}, f32[256,1024]{1,0:T(8,128)}, u32[]{:S(2)}, u32[]{:S(2)}) collective-permute-start(f32[256,1024]{1,0:T(8,128)} %get-tuple-element.372), channel_id=1, source_target_pairs={{0,16},{8,24},{16,0},{24,8},{1,17},{9,25},{17,1},{25,9},{2,18},{10... | collective-permute-start | bytes 3145736 | tf_op jit(solution)/shard_map/ppermute | solution.py:502
  244.3 48.8 %collective-permute-start.36 = (f32[128,1024]{1,0:T(8,128)}, f32[128,1024]{1,0:T(8,128)}, u32[]{:S(2)}, u32[]{:S(2)}) collective-permute-start(f32[128,1024]{1,0:T(8,128)} %get-tuple-element.353), channel_id=1, source_target_pairs={{0,16},{8,24},{16,0},{24,8},{1,17},{9,25},{17,1},{25,9},{2,18},{10... | collective-permute-start | bytes 1572872 | tf_op jit(solution)/shard_map/ppermute | solution.py:502
  245.8 47.3 %collective-permute-start.37 = (f32[128,1024]{1,0:T(8,128)}, f32[128,1024]{1,0:T(8,128)}, u32[]{:S(2)}, u32[]{:S(2)}) collective-permute-start(f32[128,1024]{1,0:T(8,128)} %get-tuple-element.352), channel_id=1, source_target_pairs={{0,16},{8,24},{16,0},{24,8},{1,17},{9,25},{17,1},{25,9},{2,18},{10... | collective-permute-start | bytes 1572872 | tf_op jit(solution)/shard_map/ppermute | solution.py:502
  246.3 36.6 %collective-permute-start.38 = (f32[512,1024]{1,0:T(8,128)}, f32[512,1024]{1,0:T(8,128)}, u32[]{:S(2)}, u32[]{:S(2)}) collective-permute-start(f32[512,1024]{1,0:T(8,128)} %get-tuple-element.349), channel_id=1, source_target_pairs={{0,8},{8,0},{16,24},{24,16},{1,9},{9,1},{17,25},{25,17},{2,10},{10... | collective-permute-start | bytes 6291464 | tf_op jit(solution)/shard_map/ppermute | solution.py:497
  293.0 48.4 %collective-permute-start.49 = (f32[512,688]{0,1:T(8,128)}, f32[512,688]{0,1:T(8,128)}, u32[]{:S(2)}, u32[]{:S(2)}) collective-permute-start(f32[512,688]{0,1:T(8,128)} %get-tuple-element.423), channel_id=1, source_target_pairs={{0,8},{8,0},{16,24},{24,16},{1,9},{9,1},{17,25},{25,17},{2,10},{10... | collective-permute-start | bytes 4227080 | tf_op jit(solution)/shard_map/ppermute | solution.py:497
  293.1 49.2 %collective-permute-start.50 = (f32[512,1024]{1,0:T(8,128)}, f32[512,1024]{1,0:T(8,128)}, u32[]{:S(2)}, u32[]{:S(2)}) collective-permute-start(f32[512,1024]{1,0:T(8,128)} %get-tuple-element.351), channel_id=1, source_target_pairs={{0,8},{8,0},{16,24},{24,16},{1,9},{9,1},{17,25},{25,17},{2,10},{10... | collective-permute-start | bytes 6291464 | tf_op jit(solution)/shard_map/ppermute | solution.py:497
  311.4 43.5 %collective-permute-start.53 = (f32[512,688]{0,1:T(8,128)S(1)}, f32[512,688]{0,1:T(8,128)S(1)}, u32[]{:S(2)}, u32[]{:S(2)}) collective-permute-start(f32[512,688]{0,1:T(8,128)S(1)} %copy-done.29), channel_id=1, source_target_pairs={{0,8},{8,0},{16,24},{24,16},{1,9},{9,1},{17,25},{25,17},{2,10},{10... | collective-permute-start | bytes 4227080 | tf_op jit(solution)/shard_map/ppermute | solution.py:497
  323.6 26.5 %collective-permute-start.47 = (f32[128,1024]{1,0:T(8,128)S(1)}, f32[128,1024]{1,0:T(8,128)S(1)}, u32[]{:S(2)}, u32[]{:S(2)}) collective-permute-start(f32[128,1024]{1,0:T(8,128)S(1)} %copy-done.83), channel_id=1, source_target_pairs={{0,16},{8,24},{16,0},{24,8},{1,17},{9,25},{17,1},{25,9},{2,18},{10... | collective-permute-start | bytes 1572872 | tf_op jit(solution)/shard_map/ppermute | solution.py:502
  342.4 38.5 %collective-permute-start.57 = (f32[512,688]{0,1:T(8,128)S(1)}, f32[512,688]{0,1:T(8,128)}, u32[]{:S(2)}, u32[]{:S(2)}) collective-permute-start(f32[512,688]{0,1:T(8,128)S(1)} %copy-done.27), channel_id=1, source_target_pairs={{0,8},{8,0},{16,24},{24,16},{1,9},{9,1},{17,25},{25,17},{2,10},{10... | collective-permute-start | bytes 4227080 | tf_op jit(solution)/shard_map/ppermute | solution.py:497
  368.3 43.5 %collective-permute-start.66 = (f32[512,1024]{1,0:T(8,128)S(1)}, f32[512,1024]{1,0:T(8,128)S(1)}, u32[]{:S(2)}, u32[]{:S(2)}) collective-permute-start(f32[512,1024]{1,0:T(8,128)S(1)} %copy-done.40), channel_id=1, source_target_pairs={{0,8},{8,0},{16,24},{24,16},{1,9},{9,1},{17,25},{25,17},{2,10},{10... | collective-permute-start | bytes 6291464 | tf_op jit(solution)/shard_map/ppermute | solution.py:497
  412.1 27.3 %collective-permute-start.73 = (f32[512,688]{0,1:T(8,128)S(1)}, f32[512,688]{0,1:T(8,128)S(1)}, u32[]{:S(2)}, u32[]{:S(2)}) collective-permute-start(f32[512,688]{0,1:T(8,128)S(1)} %pad_maximum_fusion.4), channel_id=1, source_target_pairs={{0,8},{8,0},{16,24},{24,16},{1,9},{9,1},{17,25},{25,17},{2,10},{10... | collective-permute-start | bytes 4227080 | tf_op jit(solution)/shard_map/ppermute | solution.py:497
  425.1 26.6 %collective-permute-start.72 = (f32[688,256]{1,0:T(8,128)S(1)}, f32[688,256]{1,0:T(8,128)S(1)}, u32[]{:S(2)}, u32[]{:S(2)}) collective-permute-start(f32[688,256]{1,0:T(8,128)S(1)} %get-tuple-element.361), channel_id=1, source_target_pairs={{0,16},{8,24},{16,0},{24,8},{1,17},{9,25},{17,1},{25,9},{2,18},{10... | collective-permute-start | bytes 2113544 | tf_op jit(solution)/shard_map/ppermute | solution.py:502
  465.6 37.9 %collective-permute-start.77 = (f32[688,256]{1,0:T(8,128)}, f32[688,256]{1,0:T(8,128)S(1)}, u32[]{:S(2)}, u32[]{:S(2)}) collective-permute-start(f32[688,256]{1,0:T(8,128)} %get-tuple-element.360), channel_id=1, source_target_pairs={{0,16},{8,24},{16,0},{24,8},{1,17},{9,25},{17,1},{25,9},{2,18},{10... | collective-permute-start | bytes 2113544 | tf_op jit(solution)/shard_map/ppermute | solution.py:502
  468.4 28.6 %collective-permute-start.78 = (f32[512,256]{1,0:T(8,128)}, f32[512,256]{1,0:T(8,128)S(1)}, u32[]{:S(2)}, u32[]{:S(2)}) collective-permute-start(f32[512,256]{1,0:T(8,128)} %get-tuple-element.380), channel_id=1, source_target_pairs={{0,8},{8,0},{16,24},{24,16},{1,9},{9,1},{17,25},{25,17},{2,10},{10... | collective-permute-start | bytes 1572872 | tf_op jit(solution)/shard_map/ppermute | solution.py:497
  470.7 34.0 %collective-permute-start.81 = (f32[512,256]{1,0:T(8,128)S(1)}, f32[512,256]{1,0:T(8,128)S(1)}, u32[]{:S(2)}, u32[]{:S(2)}) collective-permute-start(f32[512,256]{1,0:T(8,128)S(1)} %get-tuple-element.331), channel_id=1, source_target_pairs={{0,1},{1,0},{2,3},{3,2},{4,5},{5,4},{6,7},{7,6},{8,9},{9,8},{10,11... | collective-permute-start | bytes 1572872 | tf_op jit(solution)/shard_map/ppermute | solution.py:493
  472.2 55.7 %collective-permute-start.80 = (f32[1024,256]{1,0:T(8,128)S(1)}, f32[1024,256]{1,0:T(8,128)}, u32[]{:S(2)}, u32[]{:S(2)}) collective-permute-start(f32[1024,256]{1,0:T(8,128)S(1)} %copy-done.37), channel_id=1, source_target_pairs={{0,16},{8,24},{16,0},{24,8},{1,17},{9,25},{17,1},{25,9},{2,18},{10... | collective-permute-start | bytes 3145736 | tf_op jit(solution)/shard_map/ppermute | solution.py:502
  474.0 79.6 %collective-permute-start.89 = (f32[688,1024]{1,0:T(8,128)}, f32[688,1024]{1,0:T(8,128)}, u32[]{:S(2)}, u32[]{:S(2)}) collective-permute-start(f32[688,1024]{1,0:T(8,128)} %add.623.own), channel_id=1, source_target_pairs={{0,8},{8,0},{16,24},{24,16},{1,9},{9,1},{17,25},{25,17},{2,10},{10... | collective-permute-start | bytes 8454152 | tf_op jit(solution)/shard_map/ppermute | solution.py:497
  497.0 30.9 %collective-permute-start.79 = (f32[512,256]{1,0:T(8,128)}, f32[512,256]{1,0:T(8,128)S(1)}, u32[]{:S(2)}, u32[]{:S(2)}) collective-permute-start(f32[512,256]{1,0:T(8,128)} %get-tuple-element.380), channel_id=1, source_target_pairs={{0,16},{8,24},{16,0},{24,8},{1,17},{9,25},{17,1},{25,9},{2,18},{10... | collective-permute-start | bytes 1572872 | tf_op jit(solution)/shard_map/ppermute | solution.py:502
  526.2 42.5 %collective-permute-start.92 = (f32[688,1024]{1,0:T(8,128)S(1)}, f32[688,1024]{1,0:T(8,128)}, u32[]{:S(2)}, u32[]{:S(2)}) collective-permute-start(f32[688,1024]{1,0:T(8,128)S(1)} %copy-done.4), channel_id=1, source_target_pairs={{0,8},{8,0},{16,24},{24,16},{1,9},{9,1},{17,25},{25,17},{2,10},{10... | collective-permute-start | bytes 8454152 | tf_op jit(solution)/shard_map/ppermute | solution.py:497
  527.9 49.0 %collective-permute-start.95 = (f32[688,1024]{1,0:T(8,128)}, f32[688,1024]{1,0:T(8,128)}, u32[]{:S(2)}, u32[]{:S(2)}) collective-permute-start(f32[688,1024]{1,0:T(8,128)} %maximum_add_fusion.own), channel_id=1, source_target_pairs={{0,8},{8,0},{16,24},{24,16},{1,9},{9,1},{17,25},{25,17},{2,10},{10... | collective-permute-start | bytes 8454152 | tf_op jit(solution)/shard_map/ppermute | solution.py:497
  553.7 37.0 %collective-permute-start.94 = (f32[512,768]{1,0:T(8,128)}, f32[512,768]{1,0:T(8,128)}, u32[]{:S(2)}, u32[]{:S(2)}) collective-permute-start(f32[512,768]{1,0:T(8,128)} %constant_dynamic-update-slice_fusion.12), channel_id=1, source_target_pairs={{0,16},{8,24},{16,0},{24,8},{1,17},{9,25},{17,1},{25,9},{2,18},{10... | collective-permute-start | bytes 4718600 | tf_op jit(solution)/shard_map/ppermute | solution.py:502
  610.1 27.1 %collective-permute-start.102 = (f32[1024,768]{1,0:T(8,128)}, f32[1024,768]{1,0:T(8,128)}, u32[]{:S(2)}, u32[]{:S(2)}) collective-permute-start(f32[1024,768]{1,0:T(8,128)} %add.647.own), channel_id=1, source_target_pairs={{0,8},{8,0},{16,24},{24,16},{1,9},{9,1},{17,25},{25,17},{2,10},{10... | collective-permute-start | bytes 9437192 | tf_op jit(solution)/shard_map/ppermute | solution.py:497
  (208 other events, 3087.7 us)

commit v9 on v8

--- a/solution.py
+++ b/solution.py
@@ -821,12 +821,12 @@
     ffn_x = {dz: ffn_across(dz) for dz in soon}
     soon_x = [item for dz in soon for item in ffn_x[dz]]
     dm = right_product(dy_full, w_down)
-    da = meet_one(dm * c * slope, *hnorm_y[1])
+    da = meet_one(dm * c * slope, *hnorm_y[1], *soon_x[: across - 1])
     dc = dm * act
     da_y, dc_y = Along(da, 2), Along(dc, 2)
-    dhnorm = meet_one(right_product(da, w_gate), *soon_x, *hnorm_y[2], *hnorm_y[3])
+    dhnorm = meet_one(right_product(da, w_gate), *soon_x[across - 1 :], *hnorm_y[2], *hnorm_y[3])
     dhnorm = dhnorm + right_product(dc, w_up)
-    dhnorm = meet_one(dhnorm, *hnorm_y[4])
+    dhnorm = meet_one(dhnorm, *hnorm_y[4], *hnorm_y[5])
 
     def ffn_tile(dz):
         out = ffn_piece(dz, 0)
@@ -854,8 +854,8 @@
         d_whole,
         jnp.concatenate([d_gain_two, pad], 0),
         [
-            [*hnorm_y[5], *hnorm_y[6]],
-            [*hnorm_y[7], *da_y[0], own_down],
+            [*hnorm_y[6], *hnorm_y[7]],
+            [*da_y[0], own_down],
             lambda: [*da_y[1], own_gate, *([ffn_step(1)] if deep > 1 else [])],
             [*dc_y[0], own_up],
         ],

time: 653 us -> 653 us (level)
    unnamed x263 -> x259, local copies, waits for them, and re-layouts: 17.5 us -> 21.5 us
  transfers between devices with their start and end apart: 107 -> 107, of which waited for: 49 -> 48; matrix products, arithmetic and copies ran while one was open for 40% -> 40% of each run, Pallas kernels for 8% -> 8%
where the time goes in v9:
time: 653 us; the launch traced here: 644 us
  waiting for transfers between devices  202 us (31%)
  matrix products  142 us (22%)
  local copies, waits for them, and re-layouts  98.2 us (15%)
  starting transfers between devices  76.8 us (12%)
  other arithmetic  62.8 us (10%)
  Pallas kernels  57.8 us (9%)
    ppermute x49, waiting for transfers between devices, shift(): return lax.ppermute(value, 'heads', pairs)  108 us
    ppermute x24, waiting for transfers between devices, row_shift(): lax.ppermute(value, 'rows', [(r, (r + 2 * step) % size) for r in range(si...  72.1 us
    dot_general x10, matrix products, left_product(): lax.dot_general(left, right, (((0,), (0,)), ((), ())), precision=lax.Prec...  65 us
    dot_general x7, matrix products, product(): jnp.dot(left, right, precision=lax.Precision.HIGH, preferred_element_type...  39.3 us
    ppermute x49, starting transfers between devices, shift(): return lax.ppermute(value, 'heads', pairs)  33.5 us
    dot_general x5, matrix products, right_product(): lax.dot_general(left, right, (((1,), (1,)), ((), ())), precision=lax.Prec...  31.4 us
    dynamic_update_slice x21, local copies, waits for them, and re-layouts, gather_columns(): out = lax.dynamic_update_slice(out, item, (0, column))  28.2 us
    ppermute x24, starting transfers between devices, row_shift(): lax.ppermute(value, 'rows', [(r, (r + 2 * step) % size) for r in range(si...  25.7 us
  transfers between devices with their start and end apart: 107, of which 48 were waited for; matrix products, arithmetic and copies ran while one was open for 40% of the time, Pallas kernels for 8%

profile of v9, /device:TPU:0, one launch (start us, length us, event | category | flops | bytes accessed | tf_op | source)
XLA Modules:
  0.0 644.0 jit_solution(2019679174106809609)
XLA Ops:
  42.5 8.7 %fusion.16.joined = f32[512,1024]{1,0:T(8,128)} fusion(f32[2048,1024]{1,0:T(8,128)S(1)} %bitcast.143, f32[512,2048]{1,0:T(8,128)S(1)} %bitcast_multiply_fusion.3, f32[2048]{0:T(1024)S(1)} %bitcast.144), kind=kOutput, calls=%fused_computation.29 | convolution fusion | flops 6443499520 | bytes 14688256 | tf_op jit(solution)/shard_map/dot_general | solution.py:458
  62.7 12.8 %inner_forward.1 = (f32[512,256]{1,0:T(8,128)S(1)}, f32[256,512]{1,0:T(8,128)S(1)}, f32[256,512]{1,0:T(8,128)S(1)}, f32[4,256,128]{2,1,0:T(8,128)S(1)}, f32[4,256,1]{2,1,0:T(8,128)S(1)}) custom-call(f32[512,1024]{1,0:T(8,128)S(1)} %copy-done.2, f32[512,4]{1,0:T(8,128)S(1)} %copy-done.5, f32[4,512]{1,0:T(4,128)S(1)} %get-tuple-element.414.rate_t, ...), custom_call_target="tpu_custom_call" | custom-call | tf_op jit(solution)/shard_map/inner_forward/pallas_call | solution.py:182
  115.7 8.9 %collective-permute-done.17 = f32[512,256]{1,0:T(8,128)S(1)} collective-permute-done((f32[512,256]{1,0:T(8,128)S(1)}, f32[512,256]{1,0:T(8,128)S(1)}, u32[]{:S(2)}, u32[]{:S(2)}) %collective-permute-start.17) | collective-permute-done | bytes 524320 | tf_op jit(solution)/shard_map/ppermute | solution.py:493
  142.3 7.9 %collective-permute-done.22 = f32[512,256]{1,0:T(8,128)S(1)} collective-permute-done((f32[512,256]{1,0:T(8,128)S(1)}, f32[512,256]{1,0:T(8,128)S(1)}, u32[]{:S(2)}, u32[]{:S(2)}) %collective-permute-start.22) | collective-permute-done | bytes 524320 | tf_op jit(solution)/shard_map/ppermute | solution.py:493
  172.3 9.9 %collective-permute-done.25 = f32[512,256]{1,0:T(8,128)S(1)} collective-permute-done((f32[512,256]{1,0:T(8,128)S(1)}, f32[512,256]{1,0:T(8,128)S(1)}, u32[]{:S(2)}, u32[]{:S(2)}) %collective-permute-start.25) | collective-permute-done | bytes 524320 | tf_op jit(solution)/shard_map/ppermute | solution.py:493
  188.5 11.2 %collective-permute-done.27 = f32[512,256]{1,0:T(8,128)S(1)} collective-permute-done((f32[512,256]{1,0:T(8,128)S(1)}, f32[512,256]{1,0:T(8,128)S(1)}, u32[]{:S(2)}, u32[]{:S(2)}) %collective-permute-start.27) | collective-permute-done | bytes 524320 | tf_op jit(solution)/shard_map/ppermute | solution.py:493
  205.5 10.0 %collective-permute-done.29 = f32[512,256]{1,0:T(8,128)S(1)} collective-permute-done((f32[512,256]{1,0:T(8,128)S(1)}, f32[512,256]{1,0:T(8,128)S(1)}, u32[]{:S(2)}, u32[]{:S(2)}) %collective-permute-start.29) | collective-permute-done | bytes 524320 | tf_op jit(solution)/shard_map/ppermute | solution.py:493
  245.8 6.5 %fusion.111 = (f32[512,688]{0,1:T(8,128)}, f32[512,688]{0,1:T(8,128)}) fusion(f32[512,688]{0,1:T(8,128)S(1)} %fusion.155, f32[512,2048]{1,0:T(8,128)S(1)} %multiply_multiply_fusion, f32[2048,688]{0,1:T(8,128)S(1)} %bitcast.129), kind=kOutput, calls=%fused_computation.162 | convolution fusion | flops 4330283008 | bytes 14057472 | tf_op jit(solution)/shard_map/dot_general | solution.py:458
  252.4 7.4 %fusion.156 = f32[512,2048]{1,0:T(8,128)S(1)} fusion(f32[512,688]{0,1:T(8,128)} %get-tuple-element.423, f32[688,2048]{1,0:T(8,128)S(1)} %bitcast.133), kind=kOutput, calls=%fused_computation.345 | convolution fusion | flops 4328521728 | bytes 11239424 | tf_op jit(solution)/shard_map/dot_general | solution.py:458
  267.6 7.9 %fusion.110 = (f32[512,688]{0,1:T(8,128)S(1)}, f32[512,688]{0,1:T(8,128)S(1)}) fusion(f32[512,688]{0,1:T(8,128)S(1)} %copy-done.31, f32[512,688]{0,1:T(8,128)} %get-tuple-element.424, f32[512,2048]{1,0:T(8,128)} %constant_dynamic-update-slice_fusion.31, f32[688,2048]{1,0:T(8,128)S(1)} %bitcast.133), kind=kOutput, calls=%fused_computation.161 | convolution fusion | flops 4332396544 | bytes 15466496 | tf_op jit(solution)/shard_map/dot_general | solution.py:469
  302.5 9.7 %collective-permute-done.40 = f32[128,1024]{1,0:T(8,128)S(1)} collective-permute-done((f32[128,1024]{1,0:T(8,128)S(1)}, f32[128,1024]{1,0:T(8,128)S(1)}, u32[]{:S(2)}, u32[]{:S(2)}) %collective-permute-start.40) | collective-permute-done | bytes 524320 | tf_op jit(solution)/shard_map/ppermute | solution.py:502
  325.7 8.2 %collective-permute-done.46 = f32[128,1024]{1,0:T(8,128)S(1)} collective-permute-done((f32[128,1024]{1,0:T(8,128)}, f32[128,1024]{1,0:T(8,128)S(1)}, u32[]{:S(2)}, u32[]{:S(2)}) %collective-permute-start.46) | collective-permute-done | bytes 524320 | tf_op jit(solution)/shard_map/ppermute | solution.py:502
  338.7 7.6 %fusion = f32[688,1024]{1,0:T(8,128)S(1)} fusion(f32[512,1024]{1,0:T(8,128)} %collective-permute-done.50, f32[512,1024]{1,0:T(8,128)S(1)} %copy-done.40, f32[512,688]{0,1:T(8,128)} %collective-permute-done.49, f32[512,688]{0,1:T(8,128)} %get-tuple-element.423), kind=kOutput, calls=%fused_computation | convolution fusion | flops 4330274816 | bytes 9830400 | tf_op jit(solution)/shard_map/dot_general | solution.py:462
  355.8 6.8 %fusion.19 = f32[688,1024]{1,0:T(8,128)S(1)} fusion(f32[512,1024]{1,0:T(8,128)} %collective-permute-done.38, f32[512,1024]{1,0:T(8,128)S(1)} %copy-done.39, f32[512,688]{0,1:T(8,128)} %copy-done.106, f32[512,688]{0,1:T(8,128)S(1)} %copy-done.29), kind=kOutput, calls=%fused_computation.32 | convolution fusion | flops 4330274816 | bytes 9830400 | tf_op jit(solution)/shard_map/dot_general | solution.py:462
  362.6 7.5 %collective-permute-done.54 = f32[512,256]{1,0:T(8,128)S(1)} collective-permute-done((f32[512,256]{1,0:T(8,128)}, f32[512,256]{1,0:T(8,128)S(1)}, u32[]{:S(2)}, u32[]{:S(2)}) %collective-permute-start.54) | collective-permute-done | bytes 524320 | tf_op jit(solution)/shard_map/ppermute | solution.py:493
  372.1 6.7 %collective-permute-done.51 = f32[520,256]{1,0:T(8,128)S(1)} collective-permute-done((f32[520,256]{1,0:T(8,128)S(1)}, f32[520,256]{1,0:T(8,128)S(1)}, u32[]{:S(2)}, u32[]{:S(2)}) %collective-permute-start.51) | collective-permute-done | bytes 532512 | tf_op jit(solution)/shard_map/ppermute | solution.py:493
  381.5 6.8 %fusion.18 = f32[688,1024]{1,0:T(8,128)S(1)} fusion(f32[512,1024]{1,0:T(8,128)} %collective-permute-done.38, f32[512,1024]{1,0:T(8,128)S(1)} %copy-done.39, f32[512,688]{0,1:T(8,128)} %collective-permute-done.57, f32[512,688]{0,1:T(8,128)S(1)} %copy-done.27), kind=kOutput, calls=%fused_computation.31 | convolution fusion | flops 4330274816 | bytes 9830400 | tf_op jit(solution)/shard_map/dot_general | solution.py:462
  397.9 6.5 %collective-permute-done.62 = f32[256,688]{0,1:T(8,128)S(1)} collective-permute-done((f32[256,688]{0,1:T(8,128)}, f32[256,688]{0,1:T(8,128)S(1)}, u32[]{:S(2)}, u32[]{:S(2)}) %collective-permute-start.62) | collective-permute-done | bytes 704544 | tf_op jit(solution)/shard_map/ppermute | solution.py:502
  412.2 9.6 %collective-permute-done.65 = f32[688,256]{1,0:T(8,128)S(1)} collective-permute-done((f32[688,256]{1,0:T(8,128)S(1)}, f32[688,256]{1,0:T(8,128)S(1)}, u32[]{:S(2)}, u32[]{:S(2)}) %collective-permute-start.65) | collective-permute-done | bytes 704544 | tf_op jit(solution)/shard_map/ppermute | solution.py:502
  432.2 8.2 %collective-permute-done.69 = f32[688,256]{1,0:T(8,128)S(1)} collective-permute-done((f32[688,256]{1,0:T(8,128)S(1)}, f32[688,256]{1,0:T(8,128)S(1)}, u32[]{:S(2)}, u32[]{:S(2)}) %collective-permute-start.69) | collective-permute-done | bytes 704544 | tf_op jit(solution)/shard_map/ppermute | solution.py:502
  475.7 22.2 %inner_backward.1 = (f32[512,256]{1,0:T(8,128)S(1)}, f32[512,256]{1,0:T(8,128)S(1)}, f32[512,256]{1,0:T(8,128)S(1)}, f32[4,512]{1,0:T(4,128)S(1)}, f32[256,128]{...) custom-call(f32[512,1024]{1,0:T(8,128)} %fusion.16.joined, ...), custom_call_target="tpu_custom_call" | custom-call | tf_op jit(solution)/shard_map/inner_backward/pallas_call | solution.py:407
  507.3 9.6 %fusion.51 = f32[512,2048]{1,0:T(8,128)S(1)} fusion(f32[2048,1024]{1,0:T(8,128)} %constant_dynamic-update-slice_fusion, f32[512,256]{1,0:T(8,128)} %get-tuple-element.380, f32[512,256]{1,0:T(8,128)S(1)} %get-tuple-element.256, f32[512,256]{1,0:T(8,128)S(1)} %get-tuple-element.255, f32[512,256]{1,0:T(8,128)S(1)} %get-tuple-element.254), kind=kOutput, calls=%fused_computation.66 | convolution fusion | flops 6444023808 | bytes 14680064 | tf_op jit(solution)/shard_map/dot_general | solution.py:469
  545.0 9.1 %fusion.20 = f32[1024,768]{1,0:T(8,128)S(1)} fusion(f32[512,768]{1,0:T(8,128)} %collective-permute-done.88, f32[512,768]{1,0:T(8,128)} %constant_dynamic-update-slice_fusion.12, f32[512,1024]{1,0:T(8,128)} %collective-permute-done.14, f32[512,1024]{1,0:T(8,128)S(1)} %copy-done.24, f32[1024]{0:T(1024)S(1)} %copy-done.91), kind=kOutput, calls=%fused_computation.34 | convolution fusion | flops 4834721792 | bytes 10489856 | tf_op jit(solution)/shard_map/dot_general | solution.py:462
  600.0 8.5 %fusion.24 = f32[1024,768]{1,0:T(8,128)S(1)} fusion(f32[512,768]{1,0:T(8,128)S(1)} %collective-permute-done.97, f32[512,768]{1,0:T(8,128)} %collective-permute-done.94, f32[256,1024]{1,0:T(8,128)S(1)} %copy-done.110, f32[256,1024]{1,0:T(8,128)} %collective-permute-done.15, f32[256,1024]{1,0:T(8,128)} %collective-permute-done.10, ...), kind=kOutput, calls=%fused_computation.38 | convolution fusion | flops 4836818944 | bytes 10489856 | tf_op jit(solution)/shard_map/dot_general | solution.py:462
  (660 shorter events, 421.2 us)
Async XLA Ops:
  29.5 51.7 %collective-permute-start.14 = (f32[512,1024]{1,0:T(8,128)}, f32[512,1024]{1,0:T(8,128)}, u32[]{:S(2)}, u32[]{:S(2)}) collective-permute-start(f32[512,1024]{1,0:T(8,128)} %get-tuple-element.358), channel_id=1, source_target_pairs={{0,8},{8,0},{16,24},{24,16},{1,9},{9,1},{17,25},{25,17},{2,10},{10... | collective-permute-start | bytes 6291464 | tf_op jit(solution)/shard_map/ppermute | solution.py:497
  32.3 47.5 %collective-permute-start.10 = (f32[256,1024]{1,0:T(8,128)}, f32[256,1024]{1,0:T(8,128)}, u32[]{:S(2)}, u32[]{:S(2)}) collective-permute-start(f32[256,1024]{1,0:T(8,128)} %get-tuple-element.372), channel_id=1, source_target_pairs={{0,16},{8,24},{16,0},{24,8},{1,17},{9,25},{17,1},{25,9},{2,18},{10... | collective-permute-start | bytes 3145736 | tf_op jit(solution)/shard_map/ppermute | solution.py:502
  243.3 38.3 %collective-permute-start.33 = (f32[128,1024]{1,0:T(8,128)}, f32[128,1024]{1,0:T(8,128)S(1)}, u32[]{:S(2)}, u32[]{:S(2)}) collective-permute-start(f32[128,1024]{1,0:T(8,128)} %get-tuple-element.356), channel_id=1, source_target_pairs={{0,16},{8,24},{16,0},{24,8},{1,17},{9,25},{17,1},{25,9},{2,18},{10... | collective-permute-start | bytes 1572872 | tf_op jit(solution)/shard_map/ppermute | solution.py:502
  243.8 50.3 %collective-permute-start.36 = (f32[128,1024]{1,0:T(8,128)}, f32[128,1024]{1,0:T(8,128)}, u32[]{:S(2)}, u32[]{:S(2)}) collective-permute-start(f32[128,1024]{1,0:T(8,128)} %get-tuple-element.355), channel_id=1, source_target_pairs={{0,16},{8,24},{16,0},{24,8},{1,17},{9,25},{17,1},{25,9},{2,18},{10... | collective-permute-start | bytes 1572872 | tf_op jit(solution)/shard_map/ppermute | solution.py:502
  245.3 48.8 %collective-permute-start.37 = (f32[128,1024]{1,0:T(8,128)}, f32[128,1024]{1,0:T(8,128)}, u32[]{:S(2)}, u32[]{:S(2)}) collective-permute-start(f32[128,1024]{1,0:T(8,128)} %get-tuple-element.354), channel_id=1, source_target_pairs={{0,16},{8,24},{16,0},{24,8},{1,17},{9,25},{17,1},{25,9},{2,18},{10... | collective-permute-start | bytes 1572872 | tf_op jit(solution)/shard_map/ppermute | solution.py:502
  245.8 37.6 %collective-permute-start.38 = (f32[512,1024]{1,0:T(8,128)}, f32[512,1024]{1,0:T(8,128)}, u32[]{:S(2)}, u32[]{:S(2)}) collective-permute-start(f32[512,1024]{1,0:T(8,128)} %get-tuple-element.351), channel_id=1, source_target_pairs={{0,8},{8,0},{16,24},{24,16},{1,9},{9,1},{17,25},{25,17},{2,10},{10... | collective-permute-start | bytes 6291464 | tf_op jit(solution)/shard_map/ppermute | solution.py:497
  294.1 43.2 %collective-permute-start.49 = (f32[512,688]{0,1:T(8,128)}, f32[512,688]{0,1:T(8,128)}, u32[]{:S(2)}, u32[]{:S(2)}) collective-permute-start(f32[512,688]{0,1:T(8,128)} %get-tuple-element.423), channel_id=1, source_target_pairs={{0,8},{8,0},{16,24},{24,16},{1,9},{9,1},{17,25},{25,17},{2,10},{10... | collective-permute-start | bytes 4227080 | tf_op jit(solution)/shard_map/ppermute | solution.py:497
  294.2 44.4 %collective-permute-start.50 = (f32[512,1024]{1,0:T(8,128)}, f32[512,1024]{1,0:T(8,128)}, u32[]{:S(2)}, u32[]{:S(2)}) collective-permute-start(f32[512,1024]{1,0:T(8,128)} %get-tuple-element.353), channel_id=1, source_target_pairs={{0,8},{8,0},{16,24},{24,16},{1,9},{9,1},{17,25},{25,17},{2,10},{10... | collective-permute-start | bytes 6291464 | tf_op jit(solution)/shard_map/ppermute | solution.py:497
  297.5 27.3 %collective-permute-start.45 = (f32[128,1024]{1,0:T(8,128)}, f32[128,1024]{1,0:T(8,128)S(1)}, u32[]{:S(2)}, u32[]{:S(2)}) collective-permute-start(f32[128,1024]{1,0:T(8,128)} %get-tuple-element.367), channel_id=1, source_target_pairs={{0,16},{8,24},{16,0},{24,8},{1,17},{9,25},{17,1},{25,9},{2,18},{10... | collective-permute-start | bytes 1572872 | tf_op jit(solution)/shard_map/ppermute | solution.py:502
  301.0 32.9 %collective-permute-start.46 = (f32[128,1024]{1,0:T(8,128)}, f32[128,1024]{1,0:T(8,128)S(1)}, u32[]{:S(2)}, u32[]{:S(2)}) collective-permute-start(f32[128,1024]{1,0:T(8,128)} %get-tuple-element.366), channel_id=1, source_target_pairs={{0,16},{8,24},{16,0},{24,8},{1,17},{9,25},{17,1},{25,9},{2,18},{10... | collective-permute-start | bytes 1572872 | tf_op jit(solution)/shard_map/ppermute | solution.py:502
  324.9 29.3 %collective-permute-start.53 = (f32[512,688]{0,1:T(8,128)S(1)}, f32[512,688]{0,1:T(8,128)S(1)}, u32[]{:S(2)}, u32[]{:S(2)}) collective-permute-start(f32[512,688]{0,1:T(8,128)S(1)} %copy-done.29), channel_id=1, source_target_pairs={{0,8},{8,0},{16,24},{24,16},{1,9},{9,1},{17,25},{25,17},{2,10},{10... | collective-permute-start | bytes 4227080 | tf_op jit(solution)/shard_map/ppermute | solution.py:497
  338.6 42.3 %collective-permute-start.57 = (f32[512,688]{0,1:T(8,128)S(1)}, f32[512,688]{0,1:T(8,128)}, u32[]{:S(2)}, u32[]{:S(2)}) collective-permute-start(f32[512,688]{0,1:T(8,128)S(1)} %copy-done.27), channel_id=1, source_target_pairs={{0,8},{8,0},{16,24},{24,16},{1,9},{9,1},{17,25},{25,17},{2,10},{10... | collective-permute-start | bytes 4227080 | tf_op jit(solution)/shard_map/ppermute | solution.py:497
  370.9 36.3 %collective-permute-start.66 = (f32[512,1024]{1,0:T(8,128)S(1)}, f32[512,1024]{1,0:T(8,128)S(1)}, u32[]{:S(2)}, u32[]{:S(2)}) collective-permute-start(f32[512,1024]{1,0:T(8,128)S(1)} %get-tuple-element.337), channel_id=1, source_target_pairs={{0,8},{8,0},{16,24},{24,16},{1,9},{9,1},{17,25},{25,17},{2,10},{10... | collective-permute-start | bytes 6291464 | tf_op jit(solution)/shard_map/ppermute | solution.py:497
  407.5 33.9 %collective-permute-start.73 = (f32[512,688]{0,1:T(8,128)S(1)}, f32[512,688]{0,1:T(8,128)S(1)}, u32[]{:S(2)}, u32[]{:S(2)}) collective-permute-start(f32[512,688]{0,1:T(8,128)S(1)} %pad_maximum_fusion.4), channel_id=1, source_target_pairs={{0,8},{8,0},{16,24},{24,16},{1,9},{9,1},{17,25},{25,17},{2,10},{10... | collective-permute-start | bytes 4227080 | tf_op jit(solution)/shard_map/ppermute | solution.py:497
  423.6 29.8 %collective-permute-start.72 = (f32[688,256]{1,0:T(8,128)S(1)}, f32[688,256]{1,0:T(8,128)S(1)}, u32[]{:S(2)}, u32[]{:S(2)}) collective-permute-start(f32[688,256]{1,0:T(8,128)S(1)} %get-tuple-element.361), channel_id=1, source_target_pairs={{0,16},{8,24},{16,0},{24,8},{1,17},{9,25},{17,1},{25,9},{2,18},{10... | collective-permute-start | bytes 2113544 | tf_op jit(solution)/shard_map/ppermute | solution.py:502
  466.9 38.4 %collective-permute-start.77 = (f32[688,256]{1,0:T(8,128)}, f32[688,256]{1,0:T(8,128)S(1)}, u32[]{:S(2)}, u32[]{:S(2)}) collective-permute-start(f32[688,256]{1,0:T(8,128)} %get-tuple-element.360), channel_id=1, source_target_pairs={{0,16},{8,24},{16,0},{24,8},{1,17},{9,25},{17,1},{25,9},{2,18},{10... | collective-permute-start | bytes 2113544 | tf_op jit(solution)/shard_map/ppermute | solution.py:502
  469.9 28.7 %collective-permute-start.78 = (f32[512,256]{1,0:T(8,128)}, f32[512,256]{1,0:T(8,128)S(1)}, u32[]{:S(2)}, u32[]{:S(2)}) collective-permute-start(f32[512,256]{1,0:T(8,128)} %get-tuple-element.380), channel_id=1, source_target_pairs={{0,8},{8,0},{16,24},{24,16},{1,9},{9,1},{17,25},{25,17},{2,10},{10... | collective-permute-start | bytes 1572872 | tf_op jit(solution)/shard_map/ppermute | solution.py:497
  472.1 33.9 %collective-permute-start.81 = (f32[512,256]{1,0:T(8,128)S(1)}, f32[512,256]{1,0:T(8,128)S(1)}, u32[]{:S(2)}, u32[]{:S(2)}) collective-permute-start(f32[512,256]{1,0:T(8,128)S(1)} %get-tuple-element.331), channel_id=1, source_target_pairs={{0,1},{1,0},{2,3},{3,2},{4,5},{5,4},{6,7},{7,6},{8,9},{9,8},{10,11... | collective-permute-start | bytes 1572872 | tf_op jit(solution)/shard_map/ppermute | solution.py:493
  474.1 53.8 %collective-permute-start.80 = (f32[1024,256]{1,0:T(8,128)S(1)}, f32[1024,256]{1,0:T(8,128)}, u32[]{:S(2)}, u32[]{:S(2)}) collective-permute-start(f32[1024,256]{1,0:T(8,128)S(1)} %copy-done.36), channel_id=1, source_target_pairs={{0,16},{8,24},{16,0},{24,8},{1,17},{9,25},{17,1},{25,9},{2,18},{10... | collective-permute-start | bytes 3145736 | tf_op jit(solution)/shard_map/ppermute | solution.py:502
  475.7 78.4 %collective-permute-start.89 = (f32[688,1024]{1,0:T(8,128)}, f32[688,1024]{1,0:T(8,128)}, u32[]{:S(2)}, u32[]{:S(2)}) collective-permute-start(f32[688,1024]{1,0:T(8,128)} %add.623.own), channel_id=1, source_target_pairs={{0,8},{8,0},{16,24},{24,16},{1,9},{9,1},{17,25},{25,17},{2,10},{10... | collective-permute-start | bytes 8454152 | tf_op jit(solution)/shard_map/ppermute | solution.py:497
  498.6 29.3 %collective-permute-start.79 = (f32[512,256]{1,0:T(8,128)}, f32[512,256]{1,0:T(8,128)S(1)}, u32[]{:S(2)}, u32[]{:S(2)}) collective-permute-start(f32[512,256]{1,0:T(8,128)} %get-tuple-element.380), channel_id=1, source_target_pairs={{0,16},{8,24},{16,0},{24,8},{1,17},{9,25},{17,1},{25,9},{2,18},{10... | collective-permute-start | bytes 1572872 | tf_op jit(solution)/shard_map/ppermute | solution.py:502
  526.2 42.7 %collective-permute-start.92 = (f32[688,1024]{1,0:T(8,128)S(1)}, f32[688,1024]{1,0:T(8,128)}, u32[]{:S(2)}, u32[]{:S(2)}) collective-permute-start(f32[688,1024]{1,0:T(8,128)S(1)} %copy-done.4), channel_id=1, source_target_pairs={{0,8},{8,0},{16,24},{24,16},{1,9},{9,1},{17,25},{25,17},{2,10},{10... | collective-permute-start | bytes 8454152 | tf_op jit(solution)/shard_map/ppermute | solution.py:497
  527.9 50.2 %collective-permute-start.95 = (f32[688,1024]{1,0:T(8,128)}, f32[688,1024]{1,0:T(8,128)}, u32[]{:S(2)}, u32[]{:S(2)}) collective-permute-start(f32[688,1024]{1,0:T(8,128)} %maximum_add_fusion.own), channel_id=1, source_target_pairs={{0,8},{8,0},{16,24},{24,16},{1,9},{9,1},{17,25},{25,17},{2,10},{10... | collective-permute-start | bytes 8454152 | tf_op jit(solution)/shard_map/ppermute | solution.py:497
  554.1 37.0 %collective-permute-start.94 = (f32[512,768]{1,0:T(8,128)}, f32[512,768]{1,0:T(8,128)}, u32[]{:S(2)}, u32[]{:S(2)}) collective-permute-start(f32[512,768]{1,0:T(8,128)} %constant_dynamic-update-slice_fusion.12), channel_id=1, source_target_pairs={{0,16},{8,24},{16,0},{24,8},{1,17},{9,25},{17,1},{25,9},{2,18},{10... | collective-permute-start | bytes 4718600 | tf_op jit(solution)/shard_map/ppermute | solution.py:502
  (206 other events, 2997.8 us)
